TPU v7x, 32 devices: a whole 2x2x4 slice. The times are simulated.
32 devices in a mesh: dp: 8 (over z, x), tensor: 4 (over y, core).
Axes of the slice: x: 2, y: 2, z: 4, core: 2. Of those that a mesh axis runs over, the one named last changes fastest.
Arguments:
- hidden_in: float32 [4096, 1536], P('dp'), may hold values from -6 to 6
- doc_lengths: int32 [2, 2], replicated, may hold values from 1 to 1792, 2048 in all within a row
- norm_attn: float32 [2, 1536], replicated, may hold values from 0.5 to 1.5
- norm_mlp: float32 [2, 1536], replicated, may hold values from 0.5 to 1.5
- w_query: bfloat16 [2, 1536, 1536], P(None, None, 'tensor'), may hold values from -0.15625 to 0.15625
- w_key: bfloat16 [2, 1536, 768], P(None, None, 'tensor'), may hold values from -0.15625 to 0.15625
- w_value: bfloat16 [2, 1536, 768], P(None, None, 'tensor'), may hold values from -0.15625 to 0.15625
- w_out: bfloat16 [2, 1536, 1536], P(None, 'tensor'), may hold values from -0.625 to 0.625
- w_gate: bfloat16 [2, 1536, 4096], P(None, None, 'tensor'), may hold values from -0.15625 to 0.15625
- w_up: bfloat16 [2, 1536, 4096], P(None, None, 'tensor'), may hold values from -0.15625 to 0.15625
- w_down: bfloat16 [2, 4096, 1536], P(None, 'tensor'), may hold values from -0.09375 to 0.09375
- cotangent: float32 [4096, 1536], P('dp'), may hold values from -6 to 6
Outputs:
- hidden_out: float32 [4096, 1536], P('dp')
- input_grad: float32 [4096, 1536], P('dp')
- norm_attn_grad: float32 [2, 1536], P(None, 'dp')
- norm_mlp_grad: float32 [2, 1536], P(None, 'dp')
- w_query_grad: float32 [2, 1536, 1536], P(None, 'dp', 'tensor')
- w_key_grad: float32 [2, 1536, 768], P(None, 'dp', 'tensor')
- w_value_grad: float32 [2, 1536, 768], P(None, 'dp', 'tensor')
- w_out_grad: float32 [2, 1536, 1536], P(None, 'tensor', 'dp')
- w_gate_grad: float32 [2, 1536, 4096], P(None, 'dp', 'tensor')
- w_up_grad: float32 [2, 1536, 4096], P(None, 'dp', 'tensor')
- w_down_grad: float32 [2, 4096, 1536], P(None, 'tensor', 'dp')
Inputs may be any that keep to these rules, and one draw needn't show every extreme that they name: `doc_lengths`: each row holds 2 document lengths that add up to 2048, each at most 1792.
All inputs are finite; a program needn't handle non-finite values.
Results may differ from a plain program's by a relative error of at most 0.028.
Values may be sent and summed in bfloat16 or wider, within the bound.
No kernel may reach another device: no remote copies, remote signals or barrier semaphores. Data moves between devices by JAX's collectives and lax.ppermute only.
A program may use at most 320 MiB of HBM per device.

v0:
```python
import jax
import jax.numpy as jnp
from jax import lax
from jax.sharding import PartitionSpec as P

HD = 96
LAYERS = 2
STRETCHES = 4


EPS = 1e-05
BASE = 100000.0


def passed_along(block, axis, distance):
    devices = range(lax.axis_size(axis))
    route = [((i - distance) % len(devices), i) for i in devices]
    return lax.ppermute(block, axis, route)


def rope_tables(positions):
    half_dim = HD // 2
    frequency = BASE ** (-(jnp.arange(half_dim, dtype=jnp.float32) * 2.0 / HD))
    angles = positions.astype(jnp.float32)[:, None] * frequency[None, :]
    angles = jnp.concatenate([angles, angles], axis=1)
    return (jnp.cos(angles)[:, None, :], jnp.sin(angles)[:, None, :])


def rotate(values, cosine, sine_table):
    half_dim = values.shape[-1] // 2
    turned = jnp.concatenate([-values[..., half_dim:], values[..., :half_dim]], axis=-1)
    return values * cosine + turned * sine_table


def unrotate(gradient, cosine, sine_table):
    half_dim = gradient.shape[-1] // 2
    scaled_values = gradient * sine_table
    turned = jnp.concatenate(
        [scaled_values[..., half_dim:], -scaled_values[..., :half_dim]], axis=-1
    )
    return gradient * cosine + turned


def doc_place(places, lengths):
    doc_ends = jnp.cumsum(lengths, axis=1)
    passed = (places[:, None] >= doc_ends).astype(jnp.int32)
    doc_ids = jnp.sum(passed, axis=1)
    starts = jnp.sum(passed * lengths, axis=1)
    return (doc_ids, places - starts)


def scores_of(queries, key_rows, allowed):
    scores = jnp.einsum(
        "qkgd,tkd->kgqt", queries, key_rows, preferred_element_type=jnp.float32
    ) * HD ** (-0.5)
    return jnp.where(allowed[None, None], scores, -jnp.inf)


def attention_forward(queries, key_rows, value_rows, allowed):
    scores = scores_of(queries, key_rows, allowed)
    row_top = jnp.max(scores, axis=-1, keepdims=True)
    log_total = row_top + jnp.log(jnp.sum(jnp.exp(scores - row_top), axis=-1, keepdims=True))
    attn_probs = jnp.exp(scores - log_total).astype(jnp.bfloat16)
    mixed_heads = jnp.einsum(
        "kgqt,tkd->qkgd", attn_probs, value_rows, preferred_element_type=jnp.float32
    )
    return (mixed_heads.astype(jnp.bfloat16), log_total)


def attention_backward(queries, key_rows, value_rows, allowed, log_total, mixed_grad):
    scores = scores_of(queries, key_rows, allowed)
    attn_probs = jnp.exp(scores - log_total)
    prob_grad = jnp.einsum(
        "qkgd,tkd->kgqt", mixed_grad, value_rows, preferred_element_type=jnp.float32
    )
    centre = jnp.sum(attn_probs * prob_grad, axis=-1, keepdims=True)
    score_grad = (attn_probs * (prob_grad - centre) * HD ** (-0.5)).astype(jnp.bfloat16)
    probs_bf = attn_probs.astype(jnp.bfloat16)
    value_grad = jnp.einsum(
        "kgqt,qkgd->tkd", probs_bf, mixed_grad, preferred_element_type=jnp.float32
    )
    query_grad = jnp.einsum(
        "kgqt,tkd->qkgd", score_grad, key_rows, preferred_element_type=jnp.float32
    )
    key_grad = jnp.einsum("kgqt,qkgd->tkd", score_grad, queries, preferred_element_type=jnp.float32)
    return (query_grad, key_grad, value_grad)


def norm_back(residual_stream, inverse_norm, gain, normalized_gradient, incoming_gradient):
    normalized_input = residual_stream * inverse_norm
    scaled_values = normalized_gradient * gain
    gain_gradient = jnp.sum(normalized_gradient * normalized_input, axis=0)
    residual_gradient = incoming_gradient + inverse_norm * (
        scaled_values
        - normalized_input * jnp.mean(scaled_values * normalized_input, axis=1, keepdims=True)
    )
    return (residual_gradient, gain_gradient)


def forward_layer(residual_stream, params, tables, allowed):
    gain_attn, gain_mlp, query_w, key_w, value_w, out_w, gate_w, up_w, down_w = params
    cosine, sine_table = tables
    row_count = residual_stream.shape[0]
    query_heads = query_w.shape[1] // HD
    kv_heads = key_w.shape[1] // HD
    inv_attn = lax.rsqrt(jnp.mean(residual_stream * residual_stream, axis=1, keepdims=True) + EPS)
    normed_attn = (residual_stream * inv_attn * gain_attn).astype(jnp.bfloat16)
    queries = jnp.dot(normed_attn, query_w, preferred_element_type=jnp.float32).reshape(
        row_count, query_heads, HD
    )
    queries = rotate(queries, cosine, sine_table).astype(jnp.bfloat16)
    key_rows = jnp.dot(normed_attn, key_w, preferred_element_type=jnp.float32).reshape(
        row_count, kv_heads, HD
    )
    key_rows = (
        rotate(key_rows, cosine, sine_table).astype(jnp.bfloat16).reshape(row_count, kv_heads * HD)
    )
    value_rows = jnp.dot(normed_attn, value_w, preferred_element_type=jnp.float32).astype(
        jnp.bfloat16
    )
    key_list = [key_rows]
    value_list = [value_rows]
    for distance in range(1, STRETCHES):
        moved_keys, moved_values = passed_along((key_rows, value_rows), "dp", distance)
        key_list.append(moved_keys)
        value_list.append(moved_values)
    all_keys = jnp.concatenate(key_list, axis=0).reshape(STRETCHES * row_count, kv_heads, HD)
    all_values = jnp.concatenate(value_list, axis=0).reshape(STRETCHES * row_count, kv_heads, HD)
    grouped = queries.reshape(row_count, kv_heads, query_heads // kv_heads, HD)
    mixed_heads, log_total = attention_forward(grouped, all_keys, all_values, allowed)
    mixed_heads = mixed_heads.reshape(row_count, query_heads * HD)
    head_part = jnp.dot(mixed_heads, out_w, preferred_element_type=jnp.float32)
    middle = residual_stream + lax.psum(head_part, "tensor")
    inv_mlp = lax.rsqrt(jnp.mean(middle * middle, axis=1, keepdims=True) + EPS)
    normed_mlp = (middle * inv_mlp * gain_mlp).astype(jnp.bfloat16)
    gate_pre = jnp.dot(normed_mlp, gate_w, preferred_element_type=jnp.float32)
    up_values = jnp.dot(normed_mlp, up_w, preferred_element_type=jnp.float32)
    activated = (jax.nn.silu(gate_pre) * up_values).astype(jnp.bfloat16)
    unit_part = jnp.dot(activated, down_w, preferred_element_type=jnp.float32)
    result = middle + lax.psum(unit_part, "tensor")
    record = (
        residual_stream,
        inv_attn,
        normed_attn,
        grouped,
        all_keys,
        all_values,
        log_total,
        mixed_heads,
        middle,
        inv_mlp,
        normed_mlp,
        gate_pre,
        up_values,
        activated,
    )
    return (record, result)


def backward_layer(grad_flow, record, params, tables, allowed):
    gain_attn, gain_mlp, query_w, key_w, value_w, out_w, gate_w, up_w, down_w = params
    (
        residual_stream,
        inv_attn,
        normed_attn,
        grouped,
        all_keys,
        all_values,
        log_total,
        mixed_heads,
        middle,
        inv_mlp,
        normed_mlp,
        gate_pre,
        up_values,
        activated,
    ) = record
    cosine, sine_table = tables
    row_count = residual_stream.shape[0]
    query_heads = query_w.shape[1] // HD
    kv_heads = key_w.shape[1] // HD
    down_in = grad_flow.astype(jnp.bfloat16)
    grad_down = jnp.dot(activated.T, down_in, preferred_element_type=jnp.float32)
    hidden_grad = jnp.dot(down_in, down_w.T, preferred_element_type=jnp.float32)
    sigmoid_gate = jax.nn.sigmoid(gate_pre)
    gate_grad = (
        hidden_grad * up_values * sigmoid_gate * (1.0 + gate_pre * (1.0 - sigmoid_gate))
    ).astype(jnp.bfloat16)
    up_grad = (hidden_grad * gate_pre * sigmoid_gate).astype(jnp.bfloat16)
    grad_gate = jnp.dot(normed_mlp.T, gate_grad, preferred_element_type=jnp.float32)
    grad_up = jnp.dot(normed_mlp.T, up_grad, preferred_element_type=jnp.float32)
    unit_back = jnp.dot(gate_grad, gate_w.T, preferred_element_type=jnp.float32) + jnp.dot(
        up_grad, up_w.T, preferred_element_type=jnp.float32
    )
    mlp_norm_grad = lax.psum(unit_back, "tensor")
    middle_grad, grad_gain_mlp = norm_back(middle, inv_mlp, gain_mlp, mlp_norm_grad, grad_flow)
    out_in = middle_grad.astype(jnp.bfloat16)
    grad_out = jnp.dot(mixed_heads.T, out_in, preferred_element_type=jnp.float32)
    mixed_grad = jnp.dot(out_in, out_w.T, preferred_element_type=jnp.float32).astype(jnp.bfloat16)
    mixed_grad = mixed_grad.reshape(row_count, kv_heads, query_heads // kv_heads, HD)
    query_grad, key_grad, value_grad = attention_backward(
        grouped, all_keys, all_values, allowed, log_total, mixed_grad
    )
    key_grad = key_grad.reshape(STRETCHES * row_count, kv_heads * HD)
    value_grad = value_grad.reshape(STRETCHES * row_count, kv_heads * HD)
    key_total = key_grad[:row_count]
    value_total = value_grad[:row_count]
    for distance in range(1, STRETCHES):
        key_piece = key_grad[distance * row_count : (distance + 1) * row_count]
        value_piece = value_grad[distance * row_count : (distance + 1) * row_count]
        moved_keys, moved_values = passed_along((key_piece, value_piece), "dp", -distance)
        key_total = key_total + moved_keys
        value_total = value_total + moved_values
    query_grad = (
        unrotate(query_grad.reshape(row_count, query_heads, HD), cosine, sine_table)
        .astype(jnp.bfloat16)
        .reshape(row_count, query_heads * HD)
    )
    key_total = (
        unrotate(key_total.reshape(row_count, kv_heads, HD), cosine, sine_table)
        .astype(jnp.bfloat16)
        .reshape(row_count, kv_heads * HD)
    )
    value_total = value_total.astype(jnp.bfloat16)
    grad_query = jnp.dot(normed_attn.T, query_grad, preferred_element_type=jnp.float32)
    grad_key = jnp.dot(normed_attn.T, key_total, preferred_element_type=jnp.float32)
    grad_value = jnp.dot(normed_attn.T, value_total, preferred_element_type=jnp.float32)
    head_back = jnp.dot(query_grad, query_w.T, preferred_element_type=jnp.float32)
    head_back = head_back + jnp.dot(key_total, key_w.T, preferred_element_type=jnp.float32)
    head_back = head_back + jnp.dot(value_total, value_w.T, preferred_element_type=jnp.float32)
    attn_norm_grad = lax.psum(head_back, "tensor")
    residual_gradient, grad_gain_attn = norm_back(
        residual_stream, inv_attn, gain_attn, attn_norm_grad, middle_grad
    )
    return (
        residual_gradient,
        (
            grad_gain_attn,
            grad_gain_mlp,
            grad_query,
            grad_key,
            grad_value,
            grad_out,
            grad_gate,
            grad_up,
            grad_down,
        ),
    )


def shards(
    hidden_in,
    doc_lengths,
    norm_attn,
    norm_mlp,
    w_query,
    w_key,
    w_value,
    w_out,
    w_gate,
    w_up,
    w_down,
    cotangent,
):
    row_count = hidden_in.shape[0]
    seq_count = lax.axis_size("dp") // STRETCHES
    shifted_index = lax.axis_index("dp") + STRETCHES // 2
    stretch_index = shifted_index % STRETCHES
    seq_index = shifted_index // STRETCHES % seq_count
    lengths = lax.dynamic_slice_in_dim(doc_lengths, seq_index, 1, 0)
    local_rows = jnp.arange(row_count, dtype=jnp.int32)
    query_place = stretch_index * row_count + local_rows
    query_doc, query_pos = doc_place(query_place, lengths)
    key_parts = []
    for distance in range(STRETCHES):
        key_parts.append((stretch_index - distance) * row_count + local_rows)
    key_place = jnp.concatenate(key_parts)
    key_doc = doc_place(key_place, lengths)[0]
    allowed = (
        (key_place[None, :] >= 0)
        & (key_place[None, :] <= query_place[:, None])
        & (key_doc[None, :] == query_doc[:, None])
    )
    tables = rope_tables(query_pos)
    records = []
    flowing = hidden_in
    for layer_index in range(LAYERS):
        params = (
            norm_attn[layer_index],
            norm_mlp[layer_index],
            w_query[layer_index],
            w_key[layer_index],
            w_value[layer_index],
            w_out[layer_index],
            w_gate[layer_index],
            w_up[layer_index],
            w_down[layer_index],
        )
        record, flowing = forward_layer(flowing, params, tables, allowed)
        records.append(record)
    grad_flow = cotangent
    collected = [None] * LAYERS
    for layer_index in reversed(range(LAYERS)):
        params = (
            norm_attn[layer_index],
            norm_mlp[layer_index],
            w_query[layer_index],
            w_key[layer_index],
            w_value[layer_index],
            w_out[layer_index],
            w_gate[layer_index],
            w_up[layer_index],
            w_down[layer_index],
        )
        grad_flow, layer_grads = backward_layer(
            grad_flow, records[layer_index], params, tables, allowed
        )
        collected[layer_index] = layer_grads
    stacked = tuple(
        (jnp.stack([member[position] for member in collected]) for position in range(9))
    )
    stacked = (
        lax.psum_scatter(
            stacked[0].astype(jnp.bfloat16), "dp", scatter_dimension=1, tiled=True
        ).astype(jnp.float32),
        lax.psum_scatter(
            stacked[1].astype(jnp.bfloat16), "dp", scatter_dimension=1, tiled=True
        ).astype(jnp.float32),
        lax.psum_scatter(
            stacked[2].astype(jnp.bfloat16), "dp", scatter_dimension=1, tiled=True
        ).astype(jnp.float32),
        lax.psum_scatter(
            stacked[3].astype(jnp.bfloat16), "dp", scatter_dimension=1, tiled=True
        ).astype(jnp.float32),
        lax.psum_scatter(
            stacked[4].astype(jnp.bfloat16), "dp", scatter_dimension=1, tiled=True
        ).astype(jnp.float32),
        lax.psum_scatter(
            stacked[5].astype(jnp.bfloat16), "dp", scatter_dimension=2, tiled=True
        ).astype(jnp.float32),
        lax.psum_scatter(
            stacked[6].astype(jnp.bfloat16), "dp", scatter_dimension=1, tiled=True
        ).astype(jnp.float32),
        lax.psum_scatter(
            stacked[7].astype(jnp.bfloat16), "dp", scatter_dimension=1, tiled=True
        ).astype(jnp.float32),
        lax.psum_scatter(
            stacked[8].astype(jnp.bfloat16), "dp", scatter_dimension=2, tiled=True
        ).astype(jnp.float32),
    )
    return (
        flowing,
        grad_flow,
        stacked[0],
        stacked[1],
        stacked[2],
        stacked[3],
        stacked[4],
        stacked[5],
        stacked[6],
        stacked[7],
        stacked[8],
    )


def solution(mesh):
    placed = (
        P("dp", None),
        P(),
        P(),
        P(),
        P(None, None, "tensor"),
        P(None, None, "tensor"),
        P(None, None, "tensor"),
        P(None, "tensor", None),
        P(None, None, "tensor"),
        P(None, None, "tensor"),
        P(None, "tensor", None),
        P("dp", None),
    )
    return jax.shard_map(
        shards,
        mesh=mesh,
        in_specs=placed,
        out_specs=(
            P("dp", None),
            P("dp", None),
            P(None, "dp"),
            P(None, "dp"),
            P(None, "dp", "tensor"),
            P(None, "dp", "tensor"),
            P(None, "dp", "tensor"),
            P(None, "tensor", "dp"),
            P(None, "dp", "tensor"),
            P(None, "dp", "tensor"),
            P(None, "tensor", "dp"),
        ),
        check_vma=False,
    )
```

profile of v0, /device:TPU:0, one launch (start us, length us, event | category | flops | bytes accessed | tf_op | source)
XLA Modules:
  0.0 1885.0 jit_solution(11726850413629536480)
XLA Ops:
  38.5 14.9 collective-permute-done.5
  72.2 64.6 %all-reduce.13.cloned.1.call-done = f32[512,1536]{1,0:T(8,128)} async-done(((f32[512,1536]{1,0:T(8,128)}), f32[512,1536]{1,0:T(8,128)}) %all-reduce.13.cloned.1.call-update) | async-done | bytes 3145744 | tf_op jit(solution)/shard_map/psum | solution.py:133
  155.3 66.3 %all-reduce.15.cloned.1.call-done = f32[512,1536]{1,0:T(8,128)} async-done(((f32[512,1536]{1,0:T(8,128)}), f32[512,1536]{1,0:T(8,128)}) %all-reduce.15.cloned.1.call-update) | async-done | bytes 3145744 | tf_op jit(solution)/shard_map/psum | solution.py:140
  238.2 22.7 %collective-permute-done.11 = bf16[512,192]{0,1:T(8,128)(2,1)S(1)} collective-permute-done((bf16[512,192]{0,1:T(8,128)(2,1)S(1)}, bf16[512,192]{0,1:T(8,128)(2,1)S(1)}, u32[]{:S(2)}, u32[]{:S(2)}) %collective-permute-start.11) | collective-permute-done | bytes 196640 | tf_op jit(solution)/shard_map/ppermute | solution.py:18
  279.3 64.6 %all-reduce.17.cloned.1.call-done = f32[512,1536]{1,0:T(8,128)} async-done(((f32[512,1536]{1,0:T(8,128)}), f32[512,1536]{1,0:T(8,128)}) %all-reduce.17.cloned.1.call-update) | async-done | bytes 3145744 | tf_op jit(solution)/shard_map/psum | solution.py:133
  365.1 68.7 %all-reduce.19.cloned.1.call-done = f32[512,1536]{1,0:T(8,128)} async-done(((f32[512,1536]{1,0:T(8,128)}), f32[512,1536]{1,0:T(8,128)}) %all-reduce.19.cloned.1.call-update) | async-done | bytes 3145744 | tf_op jit(solution)/shard_map/psum | solution.py:195
  444.3 9.5 convolution_bitcast_fusion.1
  453.8 8.2 fusion.188
  462.0 25.3 %fusion.63 = f32[2048,2,96]{0,2,1:T(8,128)} fusion(bf16[512,2,2,96]{0,3,2,1:T(8,128)(2,1)} %bitcast.491, f32[2,2048,512,2]{2,1,3,0:T(8,128)} %fusion.188, f32[2,2048,512,2]{2,1,3,0:T(8,128)} %copy-done.12, f32[2,2,512]{2,1,0:T(2,128)} %copy-done.94, pred[512,2048]{0,1:T(8,128)(4,1)} %copy-done.25), kind=kOutput, calls=%fused_computation.113 | convolution fusion | flops 851447808 | bytes 36577280 | tf_op jit(solution)/shard_map/kgqt,qkgd->tkd/dot_general | solution.py:85
  487.3 25.1 %fusion.41 = f32[2,96,2,512]{3,1,2,0:T(8,128)} fusion(f32[2,2048,512,2]{2,1,3,0:T(8,128)} %fusion.188, f32[2,2048,512,2]{2,1,3,0:T(8,128)} %copy-done.12, f32[2,2,512]{2,1,0:T(2,128)} %copy-done.94, pred[512,2048]{0,1:T(8,128)(4,1)} %copy-done.25, bf16[512,2,96]{0,2,1:T(8,128)(2,1)} %bitcast.530, bf16[512,2,96]{0,2,1:T(8,128)(2,1)} %bitcast.528, ...), kind=kOutput, calls=%fused_computation.87 | convolution fusion | flops 854593536 | bytes 36184064 | tf_op jit(solution)/shard_map/kgqt,tkd->qkgd/dot_general | solution.py:82
  525.8 19.0 %collective-permute-done.12 = f32[512,192]{0,1:T(8,128)S(1)} collective-permute-done((f32[512,192]{0,1:T(8,128)S(1)}, f32[512,192]{0,1:T(8,128)S(1)}, u32[]{:S(2)}, u32[]{:S(2)}) %collective-permute-start.12) | collective-permute-done | bytes 393248 | tf_op jit(solution)/shard_map/ppermute | solution.py:18
  553.2 8.4 collective-permute-done.14
  562.7 6.1 collective-permute-done.17
  571.9 86.6 %all-reduce.21.cloned.1.call-done = f32[512,1536]{1,0:T(8,128)} async-done(((f32[512,1536]{1,0:T(8,128)}), f32[512,1536]{1,0:T(8,128)}) %all-reduce.21.cloned.1.call-update) | async-done | bytes 3145744 | tf_op jit(solution)/shard_map/psum | solution.py:231
  666.2 6.6 multiply_convert_fusion.4
  684.1 63.0 %all-reduce.23.cloned.1.call-done = f32[512,1536]{1,0:T(8,128)} async-done(((f32[512,1536]{1,0:T(8,128)}), f32[512,1536]{1,0:T(8,128)}) %all-reduce.23.cloned.1.call-update) | async-done | bytes 3145744 | tf_op jit(solution)/shard_map/psum | solution.py:195
  754.7 9.7 convolution_bitcast_fusion
  764.4 8.1 fusion.189
  772.5 24.6 %fusion.62 = f32[2048,2,96]{0,2,1:T(8,128)} fusion(bf16[512,2,2,96]{0,3,2,1:T(8,128)(2,1)S(1)} %bitcast.489, f32[2,2048,512,2]{2,1,3,0:T(8,128)} %fusion.189, f32[2,2048,512,2]{2,1,3,0:T(8,128)} %copy-done.11, f32[2,2,512]{2,1,0:T(2,128)S(1)} %copy-done.93, pred[512,2048]{0,1:T(8,128)(4,1)S(1)} %copy-done.28), kind=kOutput, calls=%fused_computation.112 | convolution fusion | flops 851447808 | bytes 36577280 | tf_op jit(solution)/shard_map/kgqt,qkgd->tkd/dot_general | solution.py:85
  797.2 23.6 %fusion.44 = f32[2,96,2,512]{3,1,2,0:T(8,128)S(1)} fusion(f32[2,2048,512,2]{2,1,3,0:T(8,128)} %fusion.189, f32[2,2048,512,2]{2,1,3,0:T(8,128)} %copy-done.11, f32[2,2,512]{2,1,0:T(2,128)S(1)} %copy-done.93, pred[512,2048]{0,1:T(8,128)(4,1)S(1)} %copy-done.28, bf16[512,2,96]{0,2,1:T(8,128)(2,1)} %bitcast.14, bf16[512,2,96]{0,2,1:T(8,128)(2,1)} %bitcast.13, ...), kind=kOutput, calls=%fused_computation.90 | convolution fusion | flops 854593536 | bytes 36184064 | tf_op jit(solution)/shard_map/kgqt,tkd->qkgd/dot_general | solution.py:82
  834.4 19.0 %collective-permute-done.18 = f32[512,192]{0,1:T(8,128)S(1)} collective-permute-done((f32[512,192]{0,1:T(8,128)S(1)}, f32[512,192]{0,1:T(8,128)S(1)}, u32[]{:S(2)}, u32[]{:S(2)}) %collective-permute-start.18) | collective-permute-done | bytes 393248 | tf_op jit(solution)/shard_map/ppermute | solution.py:18
  861.8 8.4 collective-permute-done.20
  913.4 105.2 %all-reduce.25.cloned.1.call-done = (f32[512,1536]{1,0:T(8,128)}, f32[512,1536]{1,0:T(8,128)}) async-done(((f32[512,1536]{1,0:T(8,128)}, f32[512,1536]{1,0:T(8,128)}), (f32[512,1536]{1,0:T(8,128)}, f32[512,1536]{1,0:T(8,128)})) %all-reduce.25.cloned.1.call-update) | async-done | bytes 6291472 | tf_op jit(solution)/shard_map/psum | solution.py:140
  1037.8 16.4 copy.64
  1058.7 6.8 copy.63
  1086.7 63.9 %reduce-scatter.28.cloned.1.call-done = bf16[192,384]{1,0:T(8,128)(2,1)} async-done(((bf16[1536,384]{1,0:T(8,128)(2,1)}), bf16[192,384]{1,0:T(8,128)(2,1)}) %reduce-scatter.28.cloned.1.call-update) | async-done | bytes 147472
  1152.8 64.8 %reduce-scatter.26.cloned.1.call-done = bf16[192,384]{1,0:T(8,128)(2,1)} async-done(((bf16[1536,384]{1,0:T(8,128)(2,1)}), bf16[192,384]{1,0:T(8,128)(2,1)}) %reduce-scatter.26.cloned.1.call-update) | async-done | bytes 147472
  1227.4 54.4 %reduce-scatter.22.cloned.1.call-done = bf16[192,2]{1,0:T(8,128)(2,1)} async-done(((bf16[1536,2]{1,0:T(8,128)(2,1)}), bf16[192,2]{1,0:T(8,128)(2,1)}) %reduce-scatter.22.cloned.1.call-update) | async-done | bytes 784
  1283.3 69.9 %reduce-scatter.16.cloned.1.call-done = bf16[2,192,384]{2,1,0:T(8,128)(2,1)} async-done(((bf16[2,1536,384]{2,1,0:T(8,128)(2,1)}), bf16[2,192,384]{2,1,0:T(8,128)(2,1)}) %reduce-scatter.16.cloned.1.call-update) | async-done | bytes 294928 | tf_op jit(solution)/shard_map/reduce_scatter | solution.py:329
  1355.0 278.8 %all-reduce.27.cloned.1.call-done = (bf16[2,384,1536]{1,0,2:T(2,128)(2,1)}, bf16[2,1024,1536]{1,0,2:T(2,128)(2,1)}) async-done(((bf16[2,384,1536]{1,0,2:T(2,128)(2,1)}, bf16[2,1024,1536]{1,0,2:T(2,128)(2,1)}), (bf16[2,384,1536]{1,0,2:T(2,128)(2,1)}, bf16[2,1024,1536]{1,0,2:T(2,128)(2,1)})) %all-reduce.27.cloned.1.call-update) | async-done | bytes 8650768
  1639.1 115.5 %reduce-scatter.20.cloned.1.call-done = bf16[2,192,1024]{2,1,0:T(8,128)(2,1)} async-done(((bf16[2,1536,1024]{2,1,0:T(8,128)(2,1)}), bf16[2,192,1024]{2,1,0:T(8,128)(2,1)}) %reduce-scatter.20.cloned.1.call-update) | async-done | bytes 786448 | tf_op jit(solution)/shard_map/reduce_scatter | solution.py:344
  1757.1 118.5 %reduce-scatter.18.cloned.1.call-done = bf16[2,192,1024]{2,1,0:T(8,128)(2,1)} async-done(((bf16[2,1536,1024]{2,1,0:T(8,128)(2,1)}), bf16[2,192,1024]{2,1,0:T(8,128)(2,1)}) %reduce-scatter.18.cloned.1.call-update) | async-done | bytes 786448 | tf_op jit(solution)/shard_map/reduce_scatter | solution.py:341
  (495 shorter events, 320.9 us)
Async XLA Ops:
  7.2 129.6 %all-reduce.13.cloned.1.call-start = ((), (), s32[]{:S(2)}) async-start(), calls=%async_computation.7 | async-start | bytes 6291456 | tf_op jit(solution)/shard_map/psum | solution.py:133
  21.3 32.1 %collective-permute-start.5 = (bf16[512,192]{0,1:T(8,128)(2,1)}, bf16[512,192]{0,1:T(8,128)(2,1)}, u32[]{:S(2)}, u32[]{:S(2)}) collective-permute-start(bf16[512,192]{0,1:T(8,128)(2,1)} %bitcast.11), channel_id=1, source_target_pairs={{20,0},{24,4},{28,8},{0,12},{4,16},{8,20},{12,24},{16,28},{21,1},{... | collective-permute-start | bytes 589832 | tf_op jit(solution)/shard_map/ppermute | solution.py:18
  24.6 37.1 %collective-permute-start = (bf16[512,192]{0,1:T(8,128)(2,1)S(1)}, bf16[512,192]{0,1:T(8,128)(2,1)S(1)}, u32[]{:S(2)}, u32[]{:S(2)}) collective-permute-start(bf16[512,192]{0,1:T(8,128)(2,1)S(1)} %convolution_convert_fusion.19), channel_id=1, source_target_pairs={{28,0},{0,4},{4,8},{8,12},{12,16},{16,20},{20,24},{24,28},{29,1},{... | collective-permute-start | bytes 589832 | tf_op jit(solution)/shard_map/ppermute | solution.py:18
  26.1 35.6 %collective-permute-start.1 = (bf16[512,192]{0,1:T(8,128)(2,1)S(1)}, bf16[512,192]{0,1:T(8,128)(2,1)}, u32[]{:S(2)}, u32[]{:S(2)}) collective-permute-start(bf16[512,192]{0,1:T(8,128)(2,1)S(1)} %convolution_convert_fusion.19), channel_id=1, source_target_pairs={{24,0},{28,4},{0,8},{4,12},{8,16},{12,20},{16,24},{20,28},{25,1},{... | collective-permute-start | bytes 589832 | tf_op jit(solution)/shard_map/ppermute | solution.py:18
  35.8 25.9 %collective-permute-start.2 = (bf16[512,192]{0,1:T(8,128)(2,1)S(1)}, bf16[512,192]{0,1:T(8,128)(2,1)S(1)}, u32[]{:S(2)}, u32[]{:S(2)}) collective-permute-start(bf16[512,192]{0,1:T(8,128)(2,1)S(1)} %convolution_convert_fusion.19), channel_id=1, source_target_pairs={{20,0},{24,4},{28,8},{0,12},{4,16},{8,20},{12,24},{16,28},{21,1},{... | collective-permute-start | bytes 589832 | tf_op jit(solution)/shard_map/ppermute | solution.py:18
  70.9 150.6 %all-reduce.15.cloned.1.call-start = ((), (), s32[]{:S(2)}) async-start(), calls=%async_computation.8 | async-start | bytes 6291456 | tf_op jit(solution)/shard_map/psum | solution.py:140
  152.9 191.1 %all-reduce.17.cloned.1.call-start = ((), (), s32[]{:S(2)}) async-start(), calls=%async_computation.9 | async-start | bytes 6291456 | tf_op jit(solution)/shard_map/psum | solution.py:133
  229.2 31.6 %collective-permute-start.11 = (bf16[512,192]{0,1:T(8,128)(2,1)S(1)}, bf16[512,192]{0,1:T(8,128)(2,1)S(1)}, u32[]{:S(2)}, u32[]{:S(2)}) collective-permute-start(bf16[512,192]{0,1:T(8,128)(2,1)S(1)} %bitcast.506), channel_id=1, source_target_pairs={{20,0},{24,4},{28,8},{0,12},{4,16},{8,20},{12,24},{16,28},{21,1},{... | collective-permute-start | bytes 589832 | tf_op jit(solution)/shard_map/ppermute | solution.py:18
  232.3 35.3 %collective-permute-start.6 = (bf16[512,192]{0,1:T(8,128)(2,1)S(1)}, bf16[512,192]{0,1:T(8,128)(2,1)S(1)}, u32[]{:S(2)}, u32[]{:S(2)}) collective-permute-start(bf16[512,192]{0,1:T(8,128)(2,1)S(1)} %convolution_convert_fusion.18), channel_id=1, source_target_pairs={{28,0},{0,4},{4,8},{8,12},{12,16},{16,20},{20,24},{24,28},{29,1},{... | collective-permute-start | bytes 589832 | tf_op jit(solution)/shard_map/ppermute | solution.py:18
  233.8 33.8 %collective-permute-start.7 = (bf16[512,192]{0,1:T(8,128)(2,1)S(1)}, bf16[512,192]{0,1:T(8,128)(2,1)S(1)}, u32[]{:S(2)}, u32[]{:S(2)}) collective-permute-start(bf16[512,192]{0,1:T(8,128)(2,1)S(1)} %convolution_convert_fusion.18), channel_id=1, source_target_pairs={{24,0},{28,4},{0,8},{4,12},{8,16},{12,20},{16,24},{20,28},{25,1},{... | collective-permute-start | bytes 589832 | tf_op jit(solution)/shard_map/ppermute | solution.py:18
  236.9 30.8 %collective-permute-start.8 = (bf16[512,192]{0,1:T(8,128)(2,1)S(1)}, bf16[512,192]{0,1:T(8,128)(2,1)S(1)}, u32[]{:S(2)}, u32[]{:S(2)}) collective-permute-start(bf16[512,192]{0,1:T(8,128)(2,1)S(1)} %convolution_convert_fusion.18), channel_id=1, source_target_pairs={{20,0},{24,4},{28,8},{0,12},{4,16},{8,20},{12,24},{16,28},{21,1},{... | collective-permute-start | bytes 589832 | tf_op jit(solution)/shard_map/ppermute | solution.py:18
  278.8 154.9 %all-reduce.19.cloned.1.call-start = ((), (), s32[]{:S(2)}) async-start(), calls=%async_computation.10 | async-start | bytes 6291456 | tf_op jit(solution)/shard_map/psum | solution.py:195
  365.0 293.5 %all-reduce.21.cloned.1.call-start = ((), (), s32[]{:S(2)}) async-start(), calls=%async_computation.11 | async-start | bytes 6291456 | tf_op jit(solution)/shard_map/psum | solution.py:231
  514.0 48.6 %collective-permute-start.15 = (f32[512,192]{0,1:T(8,128)S(1)}, f32[512,192]{0,1:T(8,128)S(1)}, u32[]{:S(2)}, u32[]{:S(2)}) collective-permute-start(f32[512,192]{0,1:T(8,128)S(1)} %bitcast.497), channel_id=1, source_target_pairs={{4,0},{8,4},{12,8},{16,12},{20,16},{24,20},{28,24},{0,28},{5,1},{9... | collective-permute-start | bytes 1179656 | tf_op jit(solution)/shard_map/ppermute | solution.py:18
  518.3 44.4 %collective-permute-start.16 = (f32[512,192]{0,1:T(8,128)S(1)}, f32[512,192]{0,1:T(8,128)S(1)}, u32[]{:S(2)}, u32[]{:S(2)}) collective-permute-start(f32[512,192]{0,1:T(8,128)S(1)} %bitcast.495), channel_id=1, source_target_pairs={{8,0},{12,4},{16,8},{20,12},{24,16},{28,20},{0,24},{4,28},{9,1},{1... | collective-permute-start | bytes 1179656 | tf_op jit(solution)/shard_map/ppermute | solution.py:18
  519.0 25.7 %collective-permute-start.12 = (f32[512,192]{0,1:T(8,128)S(1)}, f32[512,192]{0,1:T(8,128)S(1)}, u32[]{:S(2)}, u32[]{:S(2)}) collective-permute-start(f32[512,192]{0,1:T(8,128)S(1)} %bitcast.502), channel_id=1, source_target_pairs={{4,0},{8,4},{12,8},{16,12},{20,16},{24,20},{28,24},{0,28},{5,1},{9... | collective-permute-start | bytes 1179656 | tf_op jit(solution)/shard_map/ppermute | solution.py:18
  519.6 33.6 %collective-permute-start.13 = (f32[512,192]{0,1:T(8,128)S(1)}, f32[512,192]{0,1:T(8,128)S(1)}, u32[]{:S(2)}, u32[]{:S(2)}) collective-permute-start(f32[512,192]{0,1:T(8,128)S(1)} %bitcast.500), channel_id=1, source_target_pairs={{8,0},{12,4},{16,8},{20,12},{24,16},{28,20},{0,24},{4,28},{9,1},{1... | collective-permute-start | bytes 1179656 | tf_op jit(solution)/shard_map/ppermute | solution.py:18
  520.2 41.4 %collective-permute-start.14 = (f32[512,192]{0,1:T(8,128)S(1)}, f32[512,192]{0,1:T(8,128)S(1)}, u32[]{:S(2)}, u32[]{:S(2)}) collective-permute-start(f32[512,192]{0,1:T(8,128)S(1)} %bitcast.498), channel_id=1, source_target_pairs={{12,0},{16,4},{20,8},{24,12},{28,16},{0,20},{4,24},{8,28},{13,1},{... | collective-permute-start | bytes 1179656 | tf_op jit(solution)/shard_map/ppermute | solution.py:18
  571.9 175.2 %all-reduce.23.cloned.1.call-start = ((), (), s32[]{:S(2)}) async-start(), calls=%async_computation.12 | async-start | bytes 6291456 | tf_op jit(solution)/shard_map/psum | solution.py:195
  678.4 340.1 %all-reduce.25.cloned.1.call-start = ((), (), s32[]{:S(2)}) async-start(), calls=%async_computation.20 | async-start | bytes 12582912 | tf_op jit(solution)/shard_map/psum | solution.py:140
  822.6 48.6 %collective-permute-start.21 = (f32[512,192]{0,1:T(8,128)S(1)}, f32[512,192]{0,1:T(8,128)S(1)}, u32[]{:S(2)}, u32[]{:S(2)}) collective-permute-start(f32[512,192]{0,1:T(8,128)S(1)} %bitcast.496), channel_id=1, source_target_pairs={{4,0},{8,4},{12,8},{16,12},{20,16},{24,20},{28,24},{0,28},{5,1},{9... | collective-permute-start | bytes 1179656 | tf_op jit(solution)/shard_map/ppermute | solution.py:18
  826.9 44.4 %collective-permute-start.22 = (f32[512,192]{0,1:T(8,128)S(1)}, f32[512,192]{0,1:T(8,128)S(1)}, u32[]{:S(2)}, u32[]{:S(2)}) collective-permute-start(f32[512,192]{0,1:T(8,128)S(1)} %bitcast.494), channel_id=1, source_target_pairs={{8,0},{12,4},{16,8},{20,12},{24,16},{28,20},{0,24},{4,28},{9,1},{1... | collective-permute-start | bytes 1179656 | tf_op jit(solution)/shard_map/ppermute | solution.py:18
  828.2 33.6 %collective-permute-start.19 = (f32[512,192]{0,1:T(8,128)S(1)}, f32[512,192]{0,1:T(8,128)S(1)}, u32[]{:S(2)}, u32[]{:S(2)}) collective-permute-start(f32[512,192]{0,1:T(8,128)S(1)} %bitcast.501), channel_id=1, source_target_pairs={{8,0},{12,4},{16,8},{20,12},{24,16},{28,20},{0,24},{4,28},{9,1},{1... | collective-permute-start | bytes 1179656 | tf_op jit(solution)/shard_map/ppermute | solution.py:18
  828.8 41.4 %collective-permute-start.20 = (f32[512,192]{0,1:T(8,128)S(1)}, f32[512,192]{0,1:T(8,128)S(1)}, u32[]{:S(2)}, u32[]{:S(2)}) collective-permute-start(f32[512,192]{0,1:T(8,128)S(1)} %bitcast.499), channel_id=1, source_target_pairs={{12,0},{16,4},{20,8},{24,12},{28,16},{0,20},{4,24},{8,28},{13,1},{... | collective-permute-start | bytes 1179656 | tf_op jit(solution)/shard_map/ppermute | solution.py:18
  880.5 204.7 %reduce-scatter.24.cloned.1.call-start = ((), (), s32[]{:S(2)}) async-start(), calls=%async_computation.17 | async-start | bytes 442368
  884.2 266.5 %reduce-scatter.28.cloned.1.call-start = ((), (), s32[]{:S(2)}) async-start(), calls=%async_computation.19 | async-start | bytes 1327104
  897.3 320.3 %reduce-scatter.26.cloned.1.call-start = ((), (), s32[]{:S(2)}) async-start(), calls=%async_computation.18 | async-start | bytes 1327104
  905.8 376.0 %reduce-scatter.22.cloned.1.call-start = ((), (), s32[]{:S(2)}) async-start(), calls=%async_computation.16 | async-start | bytes 442368
  1022.2 331.0 %reduce-scatter.16.cloned.1.call-start = ((), (), s32[]{:S(2)}) async-start(), calls=%async_computation.13 | async-start | bytes 2654208 | tf_op jit(solution)/shard_map/reduce_scatter | solution.py:329
  1025.6 608.2 %all-reduce.27.cloned.1.call-start = ((), (), s32[]{:S(2)}) async-start(), calls=%async_computation.21 | async-start | bytes 17301504
  1065.5 689.1 %reduce-scatter.20.cloned.1.call-start = ((), (), s32[]{:S(2)}) async-start(), calls=%async_computation.15 | async-start | bytes 7077888 | tf_op jit(solution)/shard_map/reduce_scatter | solution.py:344
  1074.3 801.3 %reduce-scatter.18.cloned.1.call-start = ((), (), s32[]{:S(2)}) async-start(), calls=%async_computation.14 | async-start | bytes 7077888 | tf_op jit(solution)/shard_map/reduce_scatter | solution.py:341
  (133 other events, 1330.5 us)
Sparse Core Ops, SparseCore 0:
  71.1 65.7 all-reduce.12
  153.0 68.5 all-reduce.14
  278.9 64.9 all-reduce.16
  365.1 68.5 all-reduce.18
  572.0 86.5 all-reduce.20
  678.5 68.5 all-reduce.22
  880.6 137.8 all-reduce.24
  1022.4 61.5 reduce-scatter.23
  1087.4 63.2 reduce-scatter.27
  1154.5 63.0 reduce-scatter.25
  1221.4 60.3 reduce-scatter.21
  1285.1 68.0 reduce-scatter.15
  1357.2 276.5 all-reduce.26
  1637.7 116.9 reduce-scatter.19
  1758.5 117.0 reduce-scatter.17
where the time goes:
time: 1890 us; the launch traced here: 1880 us
  waiting for transfers between devices  1400 us (74%)
  matrix products  249 us (13%)
  other arithmetic  89 us (5%)
  local copies, waits for them, and re-layouts  81.4 us (4%)
  starting transfers between devices  45.7 us (2%)
    unnamed x20, waiting for transfers between devices  462 us
    psum x2, waiting for transfers between devices, forward_layer(): result = middle + lax.psum(unit_part, 'tensor')  171 us
    psum x2, waiting for transfers between devices, backward_layer(): mlp_norm_grad = lax.psum(unit_back, 'tensor')  132 us
    psum x2, waiting for transfers between devices, forward_layer(): middle = residual_stream + lax.psum(head_part, 'tensor')  129 us
    reduce_scatter x1, waiting for transfers between devices, shards(): lax.psum_scatter(stacked[6].astype(jnp.bfloat16), 'dp', scatter_dimension...  119 us
    ppermute x24, waiting for transfers between devices, passed_along(): return lax.ppermute(block, axis, route)  118 us
    reduce_scatter x1, waiting for transfers between devices, shards(): lax.psum_scatter(stacked[7].astype(jnp.bfloat16), 'dp', scatter_dimension...  116 us
    psum x1, waiting for transfers between devices, backward_layer(): attn_norm_grad = lax.psum(head_back, 'tensor')  86.6 us
  transfers between devices with their start and end apart: 39, of which 25 were waited for; matrix products, arithmetic and copies ran while one was open for 9% of the time, Pallas kernels for 0%

commit v1 on v0

v1 whole, which is shorter than its diff:
```python
import functools

import jax
import jax.numpy as jnp
from jax import lax
from jax.experimental import pallas as pl
from jax.experimental.pallas import tpu as pltpu
from jax.sharding import PartitionSpec as P

HD = 96
LAYERS = 2
STRETCHES = 4
EPS = 1e-05
BASE = 100000.0

BF = jnp.bfloat16
F32 = jnp.float32
NEG = -1e30
VMEM_BYTES = 56 * 2**20


def mm(a, b, ca, cb):
    return lax.dot_general(a, b, (((ca,), (cb,)), ((), ())), preferred_element_type=F32)


def swap(block, axis, mask):
    n = lax.axis_size(axis)
    return lax.ppermute(block, axis, [(i, i ^ mask) for i in range(n)])


def bf16_of(x):
    return lax.reduce_precision(x, 8, 7).astype(BF)


def gather_rows(own):
    pair = jnp.concatenate([own, swap(own, "tensor", 2)], axis=0)
    return jnp.concatenate([pair, swap(pair, "tensor", 1)], axis=0)


def reduce_rows(keep, send):
    quarter = keep.shape[0] // 2
    got = swap(send, "tensor", 1)
    far = (keep[quarter:] + got[quarter:].astype(F32)).astype(BF)
    near = keep[:quarter] + got[:quarter].astype(F32)
    return near + swap(far, "tensor", 2).astype(F32)


RELATIVE = (0, 2, 1, 3)


def to_relative(rows, index):
    quarter = rows.shape[0] // 4
    return jnp.concatenate(
        [lax.dynamic_slice_in_dim(rows, (index ^ m) * quarter, quarter, 0) for m in RELATIVE], axis=0
    )


def to_absolute(rows, index):
    quarter = rows.shape[0] // 4
    parts = []
    for j in range(4):
        m = index ^ j
        place = ((m & 1) << 1) | (m >> 1)
        parts.append(lax.dynamic_slice_in_dim(rows, place * quarter, quarter, 0))
    return jnp.concatenate(parts, axis=0)


def in_stretches(pairs_of, n):
    pairs = []
    for i in range(n):
        offset = pairs_of((i + STRETCHES // 2) % STRETCHES)
        if offset is not None:
            pairs.append((i, (i + offset) % n))
    return pairs


def keys_onward(kv):
    n = lax.axis_size("dp")
    beside = swap(kv, "dp", 1)
    behind = lax.ppermute(kv, "dp", in_stretches(lambda s: 2 if s < 2 else None, n))
    across = lax.ppermute(behind, "dp", [(i, i ^ 1) for i in range(n) if (i + 2) % 4 >= 2])
    return beside, behind, across


def keys_back(beside, behind, across):
    n = lax.axis_size("dp")
    late = [i for i in range(n) if (i + 2) % 4 >= 2]
    got = lax.ppermute(across, "dp", [(i, i ^ 1) for i in late])
    from_beside = swap(beside, "dp", 1)
    total = (behind.astype(F32) + got.astype(F32)).astype(BF)
    from_behind = lax.ppermute(total, "dp", in_stretches(lambda s: -2 if s >= 2 else None, n))
    return from_beside, from_behind


def scatter_line(grad):
    n = lax.axis_size("dp")
    outer = n // 8
    r = grad.shape[0] * 2 // n
    z = lax.axis_index("dp") // 2 % 4
    g4 = grad.reshape(outer, 4, r, grad.shape[1])
    out_in, middle, in_out = [], [], []
    for i in range(n):
        zi = i // 2 % 4
        if zi in (0, 3):
            j = i + 2 if zi == 0 else i - 2
            out_in.append((i, j))
            in_out.append((j, i))
        else:
            middle.append((i, i + 2 if zi == 1 else i - 2))
    cross = lax.dynamic_slice_in_dim(g4, 2 * (1 - z // 2), 2, 1)
    beside = lax.dynamic_slice_in_dim(g4, z ^ 1, 1, 1)
    got_cross = lax.ppermute(cross, "dp", out_in)
    got_beside = lax.ppermute(beside, "dp", out_in)
    over = lax.ppermute((cross.astype(F32) + got_cross.astype(F32)).astype(BF), "dp", middle)
    on = beside.astype(F32) + lax.dynamic_slice_in_dim(over, (z ^ 1) & 1, 1, 1).astype(F32)
    last = lax.ppermute(on.astype(BF), "dp", in_out)
    own = lax.dynamic_slice_in_dim(g4, z, 1, 1).astype(F32)
    own = own + got_beside.astype(F32)
    own = own + lax.dynamic_slice_in_dim(over, z & 1, 1, 1).astype(F32) + last.astype(F32)
    own = own[:, 0]
    if outer == 1:
        return own[0]
    place = lax.axis_index("dp") // 8
    total = lax.dynamic_index_in_dim(own, place, 0, keepdims=False)
    for k in range(1, outer):
        piece = lax.dynamic_index_in_dim(own, (place + k) % outer, 0, keepdims=False).astype(BF)
        total = total + lax.ppermute(piece, "dp", [(i, (i + 8 * k) % n) for i in range(n)]).astype(F32)
    return total


def sum_everywhere(x):
    x = x + swap(x, "tensor", 1)
    x = x + swap(x, "tensor", 2)
    n = lax.axis_size("dp")
    mask = 1
    while mask < n:
        x = x + swap(x, "dp", mask)
        mask *= 2
    return x


def turned_pair(top, low, cosine, sine):
    return top * cosine - low * sine, low * cosine + top * sine


def qkv_kernel(heads, x_ref, w_ref, cos_ref, sin_ref, out_ref, t_ref):
    t_ref[...] = mm(x_ref[...], w_ref[...], 1, 0).T
    half = HD // 2
    cosine, sine = cos_ref[...], sin_ref[...]
    for h in range(heads):
        a = h * HD
        top, low = turned_pair(t_ref[a : a + half], t_ref[a + half : a + HD], cosine, sine)
        out_ref[a : a + half] = top.astype(BF)
        out_ref[a + half : a + HD] = low.astype(BF)
    rest = heads * HD
    out_ref[rest:] = t_ref[rest:].astype(BF)


def qkv_call(x, w, cosine, sine, heads):
    rows, cols = x.shape[0], w.shape[1]
    return pl.pallas_call(
        functools.partial(qkv_kernel, heads),
        out_shape=jax.ShapeDtypeStruct((cols, rows), BF),
        scratch_shapes=[pltpu.VMEM((cols, rows), F32)],
        compiler_params=pltpu.CompilerParams(vmem_limit_bytes=VMEM_BYTES),
        name="qkv_rotary",
    )(x, w, cosine, sine)


def both_heads(block):
    return jnp.concatenate([block[:HD], block[HD:]], axis=1)


def flip(block):
    return block.astype(F32).T.astype(BF)


def allowed_of(base, rows_ref, top_ref, start_ref):
    key_place = rows_ref[...] + base
    two = lambda ref: jnp.concatenate([ref[...], ref[...]], axis=1)
    return (key_place >= two(start_ref)) & (key_place <= two(top_ref))


def attn_fwd_kernel(base_ref, rows_ref, top_ref, start_ref, q_ref, *refs):
    keys, values = refs[0:8:2], refs[1:8:2]
    mixed_t_ref, log_ref, s_ref = refs[8:]
    qt = both_heads(q_ref[...])
    top = jnp.full((1, qt.shape[1]), NEG, F32)
    for b in range(4):
        scores = mm(flip(keys[b][...]), qt, 1, 0) * HD ** (-0.5)
        scores = jnp.where(allowed_of(base_ref[b], rows_ref, top_ref, start_ref), scores, NEG)
        s_ref[b] = scores
        top = jnp.maximum(top, jnp.max(scores, axis=0, keepdims=True))
    total = jnp.zeros_like(top)
    acc = jnp.zeros((HD, qt.shape[1]), F32)
    for b in range(4):
        weight = jnp.exp(s_ref[b] - top)
        total = total + jnp.sum(weight, axis=0, keepdims=True)
        acc = acc + mm(values[b][...], weight.astype(BF), 1, 0)
    acc = acc / total
    log_ref[0] = top + jnp.log(total)
    half = qt.shape[1] // 2
    mixed_t_ref[:HD] = acc[:, :half].astype(BF)
    mixed_t_ref[HD:] = acc[:, half:].astype(BF)


def attn_specs(rows, kv):
    q_spec = pl.BlockSpec((2 * HD, rows), lambda g: (g, 0))
    own_k = pl.BlockSpec((HD, rows), lambda g: (2 * kv + g, 0))
    own_v = pl.BlockSpec((HD, rows), lambda g: (3 * kv + g, 0))
    far_k = pl.BlockSpec((HD, rows), lambda g: (g, 0))
    far_v = pl.BlockSpec((HD, rows), lambda g: (kv + g, 0))
    whole = lambda shape: pl.BlockSpec(shape, lambda g: (0,) * len(shape))
    places = [
        pl.BlockSpec(memory_space=pltpu.SMEM),
        whole((rows, 1)),
        whole((1, rows)),
        whole((1, rows)),
    ]
    return places, q_spec, [own_k, own_v] + [far_k, far_v] * 3


def attn_fwd(qkv_t, far, places, kv):
    rows = qkv_t.shape[1]
    place_specs, q_spec, kv_specs = attn_specs(rows, kv)
    operands = [qkv_t, qkv_t]
    for block in far:
        operands += [block, block]
    mixed_t, log_total = pl.pallas_call(
        attn_fwd_kernel,
        grid=(kv,),
        in_specs=place_specs + [q_spec] + kv_specs,
        out_specs=[
            pl.BlockSpec((2 * HD, rows), lambda g: (g, 0)),
            pl.BlockSpec((1, 1, 2 * rows), lambda g: (g, 0, 0)),
        ],
        out_shape=[
            jax.ShapeDtypeStruct((2 * kv * HD, rows), BF),
            jax.ShapeDtypeStruct((kv, 1, 2 * rows), F32),
        ],
        scratch_shapes=[pltpu.VMEM((4, rows, 2 * rows), F32)],
        compiler_params=pltpu.CompilerParams(vmem_limit_bytes=VMEM_BYTES),
        name="attention_forward",
    )(*places, qkv_t, *operands)
    return mixed_t, log_total


def attn_bwd_kernel(base_ref, rows_ref, top_ref, start_ref, cos_ref, sin_ref, q_ref, *refs):
    keys, values = refs[0:8:2], refs[1:8:2]
    log_ref, mixed_ref, grad_ref = refs[8:11]
    dq_ref, own_ref, far_refs = refs[11], refs[12], refs[13:]
    qt = both_heads(q_ref[...])
    grad_t = both_heads(grad_ref[...])
    q_rows, grad_rows = flip(qt), flip(grad_t)
    log_total = log_ref[0]
    centre = jnp.sum(
        grad_t.astype(F32) * both_heads(mixed_ref[...]).astype(F32), axis=0, keepdims=True
    )
    dq = jnp.zeros((HD, qt.shape[1]), F32)
    for b in range(4):
        scores = mm(flip(keys[b][...]), qt, 1, 0) * HD ** (-0.5)
        scores = jnp.where(allowed_of(base_ref[b], rows_ref, top_ref, start_ref), scores, NEG)
        probs = jnp.exp(scores - log_total)
        prob_grad = mm(flip(values[b][...]), grad_t, 1, 0)
        score_grad = (probs * (prob_grad - centre) * HD ** (-0.5)).astype(BF)
        dq = dq + mm(keys[b][...], score_grad, 1, 0)
        dv = mm(probs.astype(BF), grad_rows, 1, 0).T
        dk = mm(score_grad, q_rows, 1, 0).T
        out = own_ref if b == 0 else far_refs[b - 1]
        out[0] = dk.astype(out.dtype)
        out[1] = dv.astype(out.dtype)
    half, rows = HD // 2, qt.shape[1] // 2
    cosine, sine = cos_ref[...], sin_ref[...]
    for h in range(2):
        part = dq[:, h * rows : (h + 1) * rows]
        top, low = turned_pair(part[:half], part[half:], cosine, -sine)
        dq_ref[h * HD : h * HD + half] = top.astype(BF)
        dq_ref[h * HD + half : (h + 1) * HD] = low.astype(BF)


def attn_bwd(qkv_t, far, places, kv, tables, log_total, mixed_t, grad_t):
    rows = qkv_t.shape[1]
    place_specs, q_spec, kv_specs = attn_specs(rows, kv)
    operands = [qkv_t, qkv_t]
    for block in far:
        operands += [block, block]
    table = pl.BlockSpec((HD // 2, rows), lambda g: (0, 0))
    two = pl.BlockSpec((2 * HD, rows), lambda g: (g, 0))
    pair = pl.BlockSpec((2, HD, rows), lambda g: (0, g, 0))
    outs = pl.pallas_call(
        attn_bwd_kernel,
        grid=(kv,),
        in_specs=place_specs
        + [table, table, q_spec]
        + kv_specs
        + [pl.BlockSpec((1, 1, 2 * rows), lambda g: (g, 0, 0)), two, two],
        out_specs=[two, pair, pair, pair, pair],
        out_shape=[jax.ShapeDtypeStruct((2 * kv * HD, rows), BF)]
        + [jax.ShapeDtypeStruct((2, kv * HD, rows), F32)]
        + [jax.ShapeDtypeStruct((2, kv * HD, rows), BF)] * 3,
        compiler_params=pltpu.CompilerParams(vmem_limit_bytes=VMEM_BYTES),
        name="attention_backward",
    )(*places, *tables, qkv_t, *operands, log_total, mixed_t, grad_t)
    return outs


def join_kernel(kv, dq_ref, own_ref, one_ref, two_ref, cos_ref, sin_ref, out_ref, t_ref):
    wide = dq_ref.shape[0]
    half = HD // 2
    cosine, sine = cos_ref[...], sin_ref[...]
    t_ref[:wide] = dq_ref[...].astype(F32)
    dk = own_ref[0] + one_ref[0].astype(F32) + two_ref[0].astype(F32)
    for h in range(kv):
        a = h * HD
        top, low = turned_pair(dk[a : a + half], dk[a + half : a + HD], cosine, -sine)
        t_ref[wide + a : wide + a + half] = top
        t_ref[wide + a + half : wide + a + HD] = low
    t_ref[wide + kv * HD :] = own_ref[1] + one_ref[1].astype(F32) + two_ref[1].astype(F32)
    out_ref[...] = t_ref[...].T.astype(BF)


def join_call(dq, own, one, two, tables, kv):
    rows = dq.shape[1]
    cols = dq.shape[0] + 2 * kv * HD
    return pl.pallas_call(
        functools.partial(join_kernel, kv),
        out_shape=jax.ShapeDtypeStruct((rows, cols), BF),
        scratch_shapes=[pltpu.VMEM((cols, rows), F32)],
        compiler_params=pltpu.CompilerParams(vmem_limit_bytes=VMEM_BYTES),
        name="join_gradients",
    )(dq, own, one, two, *tables)


def halves_of(x, n):
    side = lax.axis_index("dp") % 2
    cols = x.T.reshape(n // 2, 2, x.shape[1] // n, x.shape[0])
    mine = lax.dynamic_index_in_dim(cols, side, 1, keepdims=False)
    other = lax.dynamic_index_in_dim(cols, 1 - side, 1, keepdims=False)
    return mine.reshape(-1, x.shape[0]), other.reshape(-1, x.shape[0])


class Side:
    def __init__(self, mine, theirs):
        self.mine = mine
        self.theirs = theirs


def split_side(x, n):
    mine, other = halves_of(x, n)
    return Side(mine, swap(other, "dp", 1))


def whole_side(x):
    return Side(x, swap(x, "dp", 1))


def weight_grad(left, right):
    total = mm(left.mine, right.mine, 1, 0) + mm(left.theirs, right.theirs, 1, 0)
    return scatter_line(total.astype(BF))


def inverse_rms(x):
    return lax.rsqrt(jnp.mean(x * x, axis=1, keepdims=True) + EPS)


def norm_back(x, inverse, gain, grad, incoming):
    normalized = x * inverse
    scaled = grad * gain
    gain_grad = jnp.sum(grad * normalized, axis=0)
    out = incoming + inverse * (
        scaled - normalized * jnp.mean(scaled * normalized, axis=1, keepdims=True)
    )
    return out, gain_grad


def shards(
    hidden_in,
    doc_lengths,
    norm_attn,
    norm_mlp,
    w_query,
    w_key,
    w_value,
    w_out,
    w_gate,
    w_up,
    w_down,
    cotangent,
):
    rows = hidden_in.shape[0]
    n = lax.axis_size("dp")
    quarter = rows // 4
    pair = rows // 2
    t = lax.axis_index("tensor")
    kv = w_key.shape[2] // HD
    heads = w_query.shape[2] // HD
    seq_count = n // STRETCHES
    shifted = lax.axis_index("dp") + STRETCHES // 2
    stretch = shifted % STRETCHES
    lengths = lax.dynamic_index_in_dim(doc_lengths, shifted // STRETCHES % seq_count, 0, keepdims=False)
    local = jnp.concatenate([(t ^ m) * quarter + jnp.arange(quarter, dtype=jnp.int32) for m in RELATIVE])
    place = stretch * rows + local
    ends = jnp.cumsum(lengths)
    passed = (place[:, None] >= ends[None, :]).astype(jnp.int32)
    start = jnp.sum(passed * lengths[None, :], axis=1)
    frequency = BASE ** (-(jnp.arange(HD // 2, dtype=F32) * 2.0 / HD))
    angles = frequency[:, None] * (place - start).astype(F32)[None, :]
    tables = (jnp.cos(angles), jnp.sin(angles))
    bases = jnp.stack([stretch, stretch ^ 1, stretch - 2, (stretch ^ 1) - 2]) * rows
    places = (bases.astype(jnp.int32), local[:, None], place[None, :], start[None, :])

    w_qkv = jnp.concatenate([w_query, w_key, w_value], axis=2)

    def own_rows(x):
        return lax.dynamic_slice_in_dim(x, t * quarter, quarter, 0)

    flow = own_rows(hidden_in)
    inverse = inverse_rms(flow)
    normed_all = to_relative((hidden_in * inverse_rms(hidden_in) * norm_attn[0]).astype(BF), t)
    records = []
    for l in range(LAYERS):
        qkv_t = qkv_call(normed_all, w_qkv[l], *tables, heads + kv)
        far = keys_onward(qkv_t[heads * HD :])
        mixed_t, log_total = attn_fwd(qkv_t, far, places, kv)
        send = mm(mixed_t[:, pair:], w_out[l], 0, 0).astype(BF)
        keep = mm(mixed_t[:, :pair], w_out[l], 0, 0)
        middle = flow + reduce_rows(keep, send)
        inverse_mlp = inverse_rms(middle)
        normed_mlp = gather_rows((middle * inverse_mlp * norm_mlp[l]).astype(BF))
        gate = mm(normed_mlp, w_gate[l], 1, 0)
        up = mm(normed_mlp, w_up[l], 1, 0)
        activated = (jax.nn.silu(gate) * up).astype(BF)
        send = mm(activated[pair:], w_down[l], 1, 0).astype(BF)
        keep = mm(activated[:pair], w_down[l], 1, 0)
        after = middle + reduce_rows(keep, send)
        records.append(
            (flow, inverse, normed_all, qkv_t, far, mixed_t, log_total, middle, inverse_mlp, normed_mlp, gate, up, activated)
        )
        flow = after
        if l + 1 < LAYERS:
            inverse = inverse_rms(flow)
            normed_all = gather_rows((flow * inverse * norm_attn[l + 1]).astype(BF))
    hidden_out = to_absolute(gather_rows(bf16_of(flow)), t).astype(F32)

    flow = own_rows(cotangent)
    down_in = to_relative(cotangent.astype(BF), t)
    grads = [None] * LAYERS
    gains = [None] * LAYERS
    for l in reversed(range(LAYERS)):
        (before, inverse, normed_all, qkv_t, far, mixed_t, log_total, middle, inverse_mlp, normed_mlp, gate, up, activated) = records[l]
        g_down = weight_grad(split_side(down_in, n), whole_side(activated))
        hidden = mm(down_in, w_down[l], 1, 1)
        sig = jax.nn.sigmoid(gate)
        gate_grad = (hidden * up * sig * (1.0 + gate * (1.0 - sig))).astype(BF)
        up_grad = (hidden * gate * sig).astype(BF)
        send = (mm(gate_grad[pair:], w_gate[l], 1, 1) + mm(up_grad[pair:], w_up[l], 1, 1)).astype(BF)
        keep = mm(gate_grad[:pair], w_gate[l], 1, 1) + mm(up_grad[:pair], w_up[l], 1, 1)
        flow, gain_mlp = norm_back(middle, inverse_mlp, norm_mlp[l], reduce_rows(keep, send), flow)
        normed_side = split_side(normed_mlp, n)
        g_gate = weight_grad(normed_side, whole_side(gate_grad))
        g_up = weight_grad(normed_side, whole_side(up_grad))
        out_in = gather_rows(flow.astype(BF))
        grad_t = mm(w_out[l], out_in, 1, 1).astype(BF)
        dq, own, d_beside, d_behind, d_across = attn_bwd(
            qkv_t, far, places, kv, tables, log_total, mixed_t, grad_t
        )
        g_out = weight_grad(split_side(out_in, n), whole_side(mixed_t.T))
        from_beside, from_behind = keys_back(d_beside, d_behind, d_across)
        d_qkv = join_call(dq, own, from_beside, from_behind, tables, kv)
        send = mm(d_qkv[pair:], w_qkv[l], 1, 1).astype(BF)
        keep = mm(d_qkv[:pair], w_qkv[l], 1, 1)
        flow, gain_attn = norm_back(before, inverse, norm_attn[l], reduce_rows(keep, send), flow)
        g_qkv = weight_grad(split_side(normed_all, n), whole_side(d_qkv))
        if l > 0:
            down_in = gather_rows(flow.astype(BF))
        grads[l] = (g_qkv, g_out, g_gate, g_up, g_down)
        gains[l] = (gain_attn, gain_mlp)
    input_grad = to_absolute(gather_rows(bf16_of(flow)), t).astype(F32)

    early = sum_everywhere(jnp.stack([gains[1][0], gains[1][1], gains[0][1]]))
    late = sum_everywhere(gains[0][0][None])
    width = early.shape[1] // n
    dp = lax.axis_index("dp")
    early = lax.dynamic_slice_in_dim(early, dp * width, width, 1)
    late = lax.dynamic_slice_in_dim(late, dp * width, width, 1)
    norm_attn_grad = jnp.concatenate([late, early[:1]], axis=0)
    norm_mlp_grad = jnp.stack([early[2], early[1]])

    stack = lambda i: jnp.stack([grads[l][i] for l in range(LAYERS)])
    g_qkv = stack(0)
    a, b = heads * HD, (heads + kv) * HD
    turned = lambda i: jnp.stack([grads[l][i].T for l in range(LAYERS)])
    return (
        hidden_out,
        input_grad,
        norm_attn_grad,
        norm_mlp_grad,
        g_qkv[:, :, :a],
        g_qkv[:, :, a:b],
        g_qkv[:, :, b:],
        turned(1),
        stack(2),
        stack(3),
        turned(4),
    )


def solution(mesh):
    placed = (
        P("dp", None),
        P(),
        P(),
        P(),
        P(None, None, "tensor"),
        P(None, None, "tensor"),
        P(None, None, "tensor"),
        P(None, "tensor", None),
        P(None, None, "tensor"),
        P(None, None, "tensor"),
        P(None, "tensor", None),
        P("dp", None),
    )
    return jax.shard_map(
        shards,
        mesh=mesh,
        in_specs=placed,
        out_specs=(
            P("dp", None),
            P("dp", None),
            P(None, "dp"),
            P(None, "dp"),
            P(None, "dp", "tensor"),
            P(None, "dp", "tensor"),
            P(None, "dp", "tensor"),
            P(None, "tensor", "dp"),
            P(None, "dp", "tensor"),
            P(None, "dp", "tensor"),
            P(None, "tensor", "dp"),
        ),
        check_vma=False,
    )
```

time: 1890 us -> 873 us (0.46)
  waiting for transfers between devices: 1400 us -> 327 us
  starting transfers between devices: 45.7 us -> 219 us
  matrix products: 249 us -> 108 us
  Pallas kernels: 0 us -> 69.8 us
  local copies, waits for them, and re-layouts: 81.4 us -> 59.6 us
    psum x7 -> x0, waiting for transfers between devices: 519 us -> none  [the longest x2 171 us: forward_layer(): result = middle + lax.psum(unit_part, 'tensor')]
    unnamed x20 -> x0, waiting for transfers between devices: 462 us -> none
    reduce_scatter x3 -> x0, waiting for transfers between devices: 304 us -> none  [the longest x1 119 us: shards(): lax.psum_scatter(stacked[6].astype(jnp.bfloat16), 'dp', scatter_dimension...]
    ppermute x24 -> x112, waiting for transfers between devices: 118 us -> 327 us  [the longest x64 230 us: swap(): return lax.ppermute(block, axis, [(i, i ^ mask) for i in range(n)])]
    ppermute x24 -> x112, starting transfers between devices: 44 us -> 219 us  [the longest x10 67.7 us: scatter_line(): got_beside = lax.ppermute(beside, 'dp', out_in)]
    dot_general x54 -> x48, matrix products: 249 us -> 108 us  [mm(): lax.dot_general(a, b, (((ca,), (cb,)), ((), ())), preferred_element_type=...]
    pallas_call x0 -> x8, Pallas kernels: none -> 69.8 us  [the longest x2 33.1 us: attn_bwd(): pl.pallas_call(attn_bwd_kernel, grid=(kv,), in_specs=place_specs + [table...]
    unnamed x269 -> x249, local copies, waits for them, and re-layouts: 43.1 us -> 16.3 us
  transfers between devices with their start and end apart: 39 -> 112, of which waited for: 25 -> 42; matrix products, arithmetic and copies ran while one was open for 9% -> 23% of each run, Pallas kernels for 0% -> 4%
where the time goes in v1:
time: 873 us; the launch traced here: 866 us
  waiting for transfers between devices  327 us (37%)
  starting transfers between devices  219 us (25%)
  matrix products  108 us (12%)
  other arithmetic  79.4 us (9%)
  Pallas kernels  69.8 us (8%)
  local copies, waits for them, and re-layouts  59.6 us (7%)
    ppermute x64, waiting for transfers between devices, swap(): return lax.ppermute(block, axis, [(i, i ^ mask) for i in range(n)])  230 us
    dot_general x48, matrix products, mm(): lax.dot_general(a, b, (((ca,), (cb,)), ((), ())), preferred_element_type=...  108 us
    ppermute x10, starting transfers between devices, scatter_line(): got_beside = lax.ppermute(beside, 'dp', out_in)  67.7 us
    ppermute x64, starting transfers between devices, swap(): return lax.ppermute(block, axis, [(i, i ^ mask) for i in range(n)])  64.6 us
    ppermute x10, waiting for transfers between devices, scatter_line(): got_cross = lax.ppermute(cross, 'dp', out_in)  46.6 us
    pallas_call x2, Pallas kernels, attn_bwd(): pl.pallas_call(attn_bwd_kernel, grid=(kv,), in_specs=place_specs + [table...  33.1 us
    ppermute x10, starting transfers between devices, scatter_line(): got_cross = lax.ppermute(cross, 'dp', out_in)  28.8 us
    ppermute x2, waiting for transfers between devices, keys_onward(): lax.ppermute(kv, 'dp', in_stretches(lambda s: 2 if s < 2 else None, n))  22 us
  transfers between devices with their start and end apart: 112, of which 42 were waited for; matrix products, arithmetic and copies ran while one was open for 23% of the time, Pallas kernels for 4%

profile of v1, /device:TPU:0, one launch (start us, length us, event | category | flops | bytes accessed | tf_op | source)
XLA Modules:
  0.0 865.9 jit_solution(16630719141194793995)
XLA Ops:
  30.4 10.5 %collective-permute-done.1.refs_4_.refs_5_ = bf16[384,512]{1,0:T(8,128)(2,1)S(1)} collective-permute-done((bf16[384,512]{1,0:T(8,128)(2,1)}, bf16[384,512]{1,0:T(8,128)(2,1)S(1)}, u32[]{:S(2)}, u32[]{:S(2)}) %collective-permute-start.1) | collective-permute-done | bytes 393248 | tf_op jit(solution)/shard_map/ppermute | solution.py:80
  46.2 6.9 collective-permute-done.2.refs_6_.refs_7_
  53.9 11.1 %attention_forward.2 = (bf16[384,512]{1,0:T(8,128)(2,1)}, f32[2,1,1024]{2,1,0:T(1,128)}) custom-call(s32[4]{0:T(128)} %add_multiply_fusion.base_ref, s32[512,1]{1,0:T(8,128)} %copy.45.rows_ref, s32[1,512]{1,0:T(1,128)} %add_add_fusion.top_ref, s32[1,512]{1,0:T(1,128)} %bitcast.309, bf16[768,512]{1,0:T(8,128)(2,1)} %qkv_rotary.2.q_ref.refs_0_.refs_1_, ...), custom_call_target="tpu_custom_call" | custom-call | tf_op jit(solution)/shard_map/attention_forward/pallas_call | solution.py:229
  71.9 8.8 %collective-permute-done.4 = bf16[128,1536]{1,0:T(8,128)(2,1)S(1)} collective-permute-done((bf16[128,1536]{1,0:T(8,128)(2,1)S(1)}, bf16[128,1536]{1,0:T(8,128)(2,1)S(1)}, u32[]{:S(2)}, u32[]{:S(2)}) %collective-permute-start.4) | collective-permute-done | bytes 393248 | tf_op jit(solution)/shard_map/ppermute | solution.py:28
  83.5 8.6 collective-permute-done.5
  106.3 9.6 %collective-permute-done.8 = bf16[128,1536]{1,0:T(8,128)(2,1)S(1)} collective-permute-done((bf16[128,1536]{1,0:T(8,128)(2,1)S(1)}, bf16[128,1536]{1,0:T(8,128)(2,1)S(1)}, u32[]{:S(2)}, u32[]{:S(2)}) %collective-permute-start.8) | collective-permute-done | bytes 393248 | tf_op jit(solution)/shard_map/ppermute | solution.py:28
  118.2 8.7 %collective-permute-done.9 = bf16[128,1536]{1,0:T(8,128)(2,1)S(1)} collective-permute-done((bf16[128,1536]{1,0:T(8,128)(2,1)S(1)}, bf16[128,1536]{1,0:T(8,128)(2,1)S(1)}, u32[]{:S(2)}, u32[]{:S(2)}) %collective-permute-start.9) | collective-permute-done | bytes 393248 | tf_op jit(solution)/shard_map/ppermute | solution.py:28
  140.2 11.6 %collective-permute-done.12.refs_4_.refs_5_ = bf16[384,512]{1,0:T(8,128)(2,1)S(1)} collective-permute-done((bf16[384,512]{1,0:T(8,128)(2,1)S(1)}, bf16[384,512]{1,0:T(8,128)(2,1)S(1)}, u32[]{:S(2)}, u32[]{:S(2)}) %collective-permute-start.12) | collective-permute-done | bytes 393248 | tf_op jit(solution)/shard_map/ppermute | solution.py:80
  155.4 8.6 collective-permute-done.13.refs_6_.refs_7_
  164.7 11.0 %attention_forward.3 = (bf16[384,512]{1,0:T(8,128)(2,1)}, f32[2,1,1024]{2,1,0:T(1,128)}) custom-call(s32[4]{0:T(128)} %add_multiply_fusion.base_ref, s32[512,1]{1,0:T(8,128)} %copy.45.rows_ref, s32[1,512]{1,0:T(1,128)} %add_add_fusion.top_ref, s32[1,512]{1,0:T(1,128)} %bitcast.310, bf16[768,512]{1,0:T(8,128)(2,1)} %qkv_rotary.3.q_ref.refs_0_.refs_1_, ...), custom_call_target="tpu_custom_call" | custom-call | tf_op jit(solution)/shard_map/attention_forward/pallas_call | solution.py:229
  193.0 6.6 collective-permute-done.15
  281.3 57.0 %collective-permute-done.84 = bf16[768,512]{1,0:T(8,128)(2,1)S(1)} collective-permute-done((bf16[768,512]{1,0:T(8,128)(2,1)S(1)}, bf16[768,512]{1,0:T(8,128)(2,1)S(1)}, u32[]{:S(2)}, u32[]{:S(2)}) %collective-permute-start.84) | collective-permute-done | bytes 786464 | tf_op jit(solution)/shard_map/ppermute | solution.py:28
  351.5 7.0 collective-permute-done.24
  358.6 7.0 collective-permute-done.20
  377.1 13.1 %collective-permute-done.87 = bf16[1,2,192,1024]{3,2,1,0:T(8,128)(2,1)S(1)} collective-permute-done((bf16[1,2,192,1024]{3,2,1,0:T(8,128)(2,1)S(1)}, bf16[1,2,192,1024]{3,2,1,0:T(8,128)(2,1)S(1)}, u32[]{:S(2)}, u32[]{:S(2)}) %collective-permute-start.87) | collective-permute-done | bytes 786464 | tf_op jit(solution)/shard_map/ppermute | solution.py:112
  394.5 16.8 %attention_backward.2 = (bf16[384,512]{1,0:T(8,128)(2,1)}, f32[2,192,512]{2,1,0:T(8,128)}, bf16[2,192,512]{2,1,0:T(8,128)(2,1)}, bf16[2,192,512]{2,1,0:T(8,128)(2,1)}, bf16[2,192,512]{2,1,0:T(8,128)(2,1)}) custom-call(s32[4]{0:T(128)} %add_multiply_fusion.base_ref, s32[512,1]{1,0:T(8,128)} %copy.45.rows_ref, s32[1,512]{1,0:T(1,128)} %add_add_fusion.top_ref, ...), custom_call_target="tpu_custom_call" | custom-call | tf_op jit(solution)/shard_map/attention_backward/pallas_call | solution.py:290
  435.4 6.9 collective-permute-start.28
  457.2 22.7 %collective-permute-done.73 = bf16[512,384]{0,1:T(8,128)(2,1)} collective-permute-done((bf16[512,384]{0,1:T(8,128)(2,1)S(1)}, bf16[512,384]{0,1:T(8,128)(2,1)}, u32[]{:S(2)}, u32[]{:S(2)}) %collective-permute-start.73) | collective-permute-done | bytes 393248 | tf_op jit(solution)/shard_map/ppermute | solution.py:28
  488.0 6.0 collective-permute-done.75
  518.6 9.4 %collective-permute-done.63 = bf16[1,2,192,768]{3,2,1,0:T(8,128)(2,1)S(1)} collective-permute-done((bf16[1,2,192,768]{3,2,1,0:T(8,128)(2,1)S(1)}, bf16[1,2,192,768]{3,2,1,0:T(8,128)(2,1)S(1)}, u32[]{:S(2)}, u32[]{:S(2)}) %collective-permute-start.63) | collective-permute-done | bytes 589856 | tf_op jit(solution)/shard_map/ppermute | solution.py:112
  534.3 6.4 collective-permute-start.74
  542.3 7.9 collective-permute-start.62
  591.9 44.5 %collective-permute-done.100 = bf16[768,512]{1,0:T(8,128)(2,1)S(1)} collective-permute-done((bf16[768,512]{1,0:T(8,128)(2,1)S(1)}, bf16[768,512]{1,0:T(8,128)(2,1)S(1)}, u32[]{:S(2)}, u32[]{:S(2)}) %collective-permute-start.100) | collective-permute-done | bytes 786464 | tf_op jit(solution)/shard_map/ppermute | solution.py:28
  649.9 8.3 collective-permute-done.79
  667.0 8.8 %collective-permute-done.52 = f32[3,1536]{1,0:T(4,128)S(1)} collective-permute-done((f32[3,1536]{1,0:T(4,128)S(1)}, f32[3,1536]{1,0:T(4,128)S(1)}, u32[]{:S(2)}, u32[]{:S(2)}) %collective-permute-start.52) | collective-permute-done | bytes 18464 | tf_op jit(solution)/shard_map/ppermute | solution.py:28
  685.3 9.4 %collective-permute-done.81 = bf16[1,2,192,1024]{3,2,1,0:T(8,128)(2,1)S(1)} collective-permute-done((bf16[1,2,192,1024]{3,2,1,0:T(8,128)(2,1)S(1)}, bf16[1,2,192,1024]{3,2,1,0:T(8,128)(2,1)S(1)}, u32[]{:S(2)}, u32[]{:S(2)}) %collective-permute-start.81) | collective-permute-done | bytes 786464 | tf_op jit(solution)/shard_map/ppermute | solution.py:112
  698.8 11.3 %collective-permute-start.102 = (bf16[1,1,192,1024]{3,2,1,0:T(8,128)(2,1)}, bf16[1,1,192,1024]{3,2,1,0:T(8,128)(2,1)}, u32[]{:S(2)}, u32[]{:S(2)}) collective-permute-start(bf16[1,1,192,1024]{3,2,1,0:T(8,128)(2,1)} %get-tuple-element.52), channel_id=1, source_target_pairs={{0,8},{4,12},{24,16},{28,20},{1,9},{5,13},{25,17},{29,21},{2,10},{... | collective-permute-start | bytes 1179656 | tf_op jit(solution)/shard_map/ppermute | solution.py:113
  723.1 16.3 %attention_backward.3 = (bf16[384,512]{1,0:T(8,128)(2,1)}, f32[2,192,512]{2,1,0:T(8,128)}, bf16[2,192,512]{2,1,0:T(8,128)(2,1)}, bf16[2,192,512]{2,1,0:T(8,128)(2,1)}, bf16[2,192,512]{2,1,0:T(8,128)(2,1)}) custom-call(s32[4]{0:T(128)} %add_multiply_fusion.base_ref, s32[512,1]{1,0:T(8,128)} %copy.45.rows_ref, s32[1,512]{1,0:T(1,128)} %add_add_fusion.top_ref, ...), custom_call_target="tpu_custom_call" | custom-call | tf_op jit(solution)/shard_map/attention_backward/pallas_call | solution.py:290
  765.5 9.2 %collective-permute-start.39 = (bf16[2,192,512]{2,1,0:T(8,128)(2,1)S(1)}, bf16[2,192,512]{2,1,0:T(8,128)(2,1)S(1)}, u32[]{:S(2)}, u32[]{:S(2)}) collective-permute-start(bf16[2,192,512]{2,1,0:T(8,128)(2,1)S(1)} %add_convert_fusion.22), channel_id=1, source_target_pairs={{0,24},{4,28},{16,8},{20,12},{1,25},{5,29},{17,9},{21,13},{2,26},{... | collective-permute-start | bytes 1179656 | tf_op jit(solution)/shard_map/ppermute | solution.py:91
  796.2 13.2 %collective-permute-start.68 = (bf16[1,1,192,384]{3,2,1,0:T(8,128)(2,1)S(1)}, bf16[1,1,192,384]{3,2,1,0:T(8,128)(2,1)S(1)}, u32[]{:S(2)}, u32[]{:S(2)}) collective-permute-start(bf16[1,1,192,384]{3,2,1,0:T(8,128)(2,1)S(1)} %get-tuple-element.64), channel_id=1, source_target_pairs={{0,8},{4,12},{24,16},{28,20},{1,9},{5,13},{25,17},{29,21},{2,10},{... | collective-permute-start | bytes 442376 | tf_op jit(solution)/shard_map/ppermute | solution.py:113
  833.2 6.5 collective-permute-start.47
  843.1 9.7 %collective-permute-start.56 = (bf16[1,1,192,768]{3,2,1,0:T(8,128)(2,1)S(1)}, bf16[1,1,192,768]{3,2,1,0:T(8,128)(2,1)S(1)}, u32[]{:S(2)}, u32[]{:S(2)}) collective-permute-start(bf16[1,1,192,768]{3,2,1,0:T(8,128)(2,1)S(1)} %get-tuple-element.70), channel_id=1, source_target_pairs={{0,8},{4,12},{24,16},{28,20},{1,9},{5,13},{25,17},{29,21},{2,10},{... | collective-permute-start | bytes 884744 | tf_op jit(solution)/shard_map/ppermute | solution.py:113
  (665 shorter events, 463.1 us)
Async XLA Ops:
  191.5 82.1 %collective-permute-start.106 = (bf16[768,512]{1,0:T(8,128)(2,1)}, bf16[768,512]{1,0:T(8,128)(2,1)}, u32[]{:S(2)}, u32[]{:S(2)}) collective-permute-start(bf16[768,512]{1,0:T(8,128)(2,1)} %bitcast.83), channel_id=1, source_target_pairs={{0,4},{4,0},{8,12},{12,8},{16,20},{20,16},{24,28},{28,24},{1,5},{5... | collective-permute-start | bytes 2359304 | tf_op jit(solution)/shard_map/ppermute | solution.py:28
  252.4 87.2 %collective-permute-start.95 = (bf16[512,1024]{1,0:T(8,128)(2,1)}, bf16[512,1024]{1,0:T(8,128)(2,1)}, u32[]{:S(2)}, u32[]{:S(2)}) collective-permute-start(bf16[512,1024]{1,0:T(8,128)(2,1)} %get-tuple-element.89), channel_id=1, source_target_pairs={{0,4},{4,0},{8,12},{12,8},{16,20},{20,16},{24,28},{28,24},{1,5},{5... | collective-permute-start | bytes 3145736 | tf_op jit(solution)/shard_map/ppermute | solution.py:28
  270.3 78.2 %collective-permute-start.85 = (bf16[512,1024]{1,0:T(8,128)(2,1)S(1)}, bf16[512,1024]{1,0:T(8,128)(2,1)S(1)}, u32[]{:S(2)}, u32[]{:S(2)}) collective-permute-start(bf16[512,1024]{1,0:T(8,128)(2,1)S(1)} %copy-done.43), channel_id=1, source_target_pairs={{0,4},{4,0},{8,12},{12,8},{16,20},{20,16},{24,28},{28,24},{1,5},{5... | collective-permute-start | bytes 3145736 | tf_op jit(solution)/shard_map/ppermute | solution.py:28
  273.1 65.2 %collective-permute-start.84 = (bf16[768,512]{1,0:T(8,128)(2,1)S(1)}, bf16[768,512]{1,0:T(8,128)(2,1)S(1)}, u32[]{:S(2)}, u32[]{:S(2)}) collective-permute-start(bf16[768,512]{1,0:T(8,128)(2,1)S(1)} %bitcast.307), channel_id=1, source_target_pairs={{0,4},{4,0},{8,12},{12,8},{16,20},{20,16},{24,28},{28,24},{1,5},{5... | collective-permute-start | bytes 2359304 | tf_op jit(solution)/shard_map/ppermute | solution.py:28
  273.6 70.1 %collective-permute-start.19 = (bf16[128,1536]{1,0:T(8,128)(2,1)S(1)}, bf16[128,1536]{1,0:T(8,128)(2,1)S(1)}, u32[]{:S(2)}, u32[]{:S(2)}) collective-permute-start(bf16[128,1536]{1,0:T(8,128)(2,1)S(1)} %fusion.104), channel_id=1, source_target_pairs={{0,2},{1,3},{2,0},{3,1},{4,6},{5,7},{6,4},{7,5},{8,10},{9,11},{10,... | collective-permute-start | bytes 1179656 | tf_op jit(solution)/shard_map/ppermute | solution.py:28
  277.0 66.3 %collective-permute-start.23 = (bf16[128,1536]{1,0:T(8,128)(2,1)S(1)}, bf16[128,1536]{1,0:T(8,128)(2,1)S(1)}, u32[]{:S(2)}, u32[]{:S(2)}) collective-permute-start(bf16[128,1536]{1,0:T(8,128)(2,1)S(1)} %fusion.102), channel_id=1, source_target_pairs={{0,2},{1,3},{2,0},{3,1},{4,6},{5,7},{6,4},{7,5},{8,10},{9,11},{10,... | collective-permute-start | bytes 1179656 | tf_op jit(solution)/shard_map/ppermute | solution.py:28
  349.6 40.7 %collective-permute-start.87 = (bf16[1,2,192,1024]{3,2,1,0:T(8,128)(2,1)S(1)}, bf16[1,2,192,1024]{3,2,1,0:T(8,128)(2,1)S(1)}, u32[]{:S(2)}, u32[]{:S(2)}) collective-permute-start(bf16[1,2,192,1024]{3,2,1,0:T(8,128)(2,1)S(1)} %constant_dynamic-slice_fusion.12), channel_id=1, source_target_pairs={{0,8},{4,12},{24,16},{28,20},{1,9},{5,13},{25,17},{29,21},{2,10},{... | collective-permute-start | bytes 2359304 | tf_op jit(solution)/shard_map/ppermute | solution.py:112
  366.5 48.4 %collective-permute-start.21 = (bf16[256,1536]{1,0:T(8,128)(2,1)}, bf16[256,1536]{1,0:T(8,128)(2,1)}, u32[]{:S(2)}, u32[]{:S(2)}) collective-permute-start(bf16[256,1536]{1,0:T(8,128)(2,1)} %pad_maximum_fusion.17), channel_id=1, source_target_pairs={{0,1},{1,0},{2,3},{3,2},{4,5},{5,4},{6,7},{7,6},{8,9},{9,8},{10,11... | collective-permute-start | bytes 2359304 | tf_op jit(solution)/shard_map/ppermute | solution.py:28
  367.8 57.4 %collective-permute-start.110 = (bf16[1,2,192,1024]{3,2,1,0:T(8,128)(2,1)}, bf16[1,2,192,1024]{3,2,1,0:T(8,128)(2,1)}, u32[]{:S(2)}, u32[]{:S(2)}) collective-permute-start(bf16[1,2,192,1024]{3,2,1,0:T(8,128)(2,1)} %add_convert_fusion.8), channel_id=1, source_target_pairs={{8,16},{12,20},{16,8},{20,12},{9,17},{13,21},{17,9},{21,13},{10,18... | collective-permute-start | bytes 2359304 | tf_op jit(solution)/shard_map/ppermute | solution.py:114
  375.6 54.7 %collective-permute-start.98 = (bf16[1,2,192,1024]{3,2,1,0:T(8,128)(2,1)}, bf16[1,2,192,1024]{3,2,1,0:T(8,128)(2,1)}, u32[]{:S(2)}, u32[]{:S(2)}) collective-permute-start(bf16[1,2,192,1024]{3,2,1,0:T(8,128)(2,1)} %add_convert_fusion.10), channel_id=1, source_target_pairs={{8,16},{12,20},{16,8},{20,12},{9,17},{13,21},{17,9},{21,13},{10,18... | collective-permute-start | bytes 2359304 | tf_op jit(solution)/shard_map/ppermute | solution.py:114
  391.4 44.0 %collective-permute-start.88 = (bf16[1,2,192,1024]{3,2,1,0:T(8,128)(2,1)}, bf16[1,2,192,1024]{3,2,1,0:T(8,128)(2,1)}, u32[]{:S(2)}, u32[]{:S(2)}) collective-permute-start(bf16[1,2,192,1024]{3,2,1,0:T(8,128)(2,1)} %add_convert_fusion.12), channel_id=1, source_target_pairs={{8,16},{12,20},{16,8},{20,12},{9,17},{13,21},{17,9},{21,13},{10,18... | collective-permute-start | bytes 2359304 | tf_op jit(solution)/shard_map/ppermute | solution.py:114
  433.8 46.1 %collective-permute-start.72 = (bf16[768,512]{1,0:T(8,128)(2,1)}, bf16[768,512]{1,0:T(8,128)(2,1)}, u32[]{:S(2)}, u32[]{:S(2)}) collective-permute-start(bf16[768,512]{1,0:T(8,128)(2,1)} %bitcast.49), channel_id=1, source_target_pairs={{0,4},{4,0},{8,12},{12,8},{16,20},{20,16},{24,28},{28,24},{1,5},{5... | collective-permute-start | bytes 2359304 | tf_op jit(solution)/shard_map/ppermute | solution.py:28
  444.3 55.9 %collective-permute-start.60 = (bf16[768,512]{1,0:T(8,128)(2,1)}, bf16[768,512]{1,0:T(8,128)(2,1)}, u32[]{:S(2)}, u32[]{:S(2)}) collective-permute-start(bf16[768,512]{1,0:T(8,128)(2,1)} %bitcast.34), channel_id=1, source_target_pairs={{0,4},{4,0},{8,12},{12,8},{16,20},{20,16},{24,28},{28,24},{1,5},{5... | collective-permute-start | bytes 2359304 | tf_op jit(solution)/shard_map/ppermute | solution.py:28
  444.7 35.2 %collective-permute-start.73 = (bf16[512,384]{0,1:T(8,128)(2,1)S(1)}, bf16[512,384]{0,1:T(8,128)(2,1)}, u32[]{:S(2)}, u32[]{:S(2)}) collective-permute-start(bf16[512,384]{0,1:T(8,128)(2,1)S(1)} %bitcast.306), channel_id=1, source_target_pairs={{0,4},{4,0},{8,12},{12,8},{16,20},{20,16},{24,28},{28,24},{1,5},{5... | collective-permute-start | bytes 1179656 | tf_op jit(solution)/shard_map/ppermute | solution.py:28
  448.6 81.3 %collective-permute-start.96 = (bf16[1,1,192,1024]{3,2,1,0:T(8,128)(2,1)}, bf16[1,1,192,1024]{3,2,1,0:T(8,128)(2,1)}, u32[]{:S(2)}, u32[]{:S(2)}) collective-permute-start(bf16[1,1,192,1024]{3,2,1,0:T(8,128)(2,1)} %get-tuple-element.58), channel_id=1, source_target_pairs={{0,8},{4,12},{24,16},{28,20},{1,9},{5,13},{25,17},{29,21},{2,10},{... | collective-permute-start | bytes 1179656 | tf_op jit(solution)/shard_map/ppermute | solution.py:113
  454.1 47.0 %collective-permute-start.61 = (bf16[512,768]{1,0:T(8,128)(2,1)}, bf16[512,768]{1,0:T(8,128)(2,1)S(1)}, u32[]{:S(2)}, u32[]{:S(2)}) collective-permute-start(bf16[512,768]{1,0:T(8,128)(2,1)} %join_gradients.2), channel_id=1, source_target_pairs={{0,4},{4,0},{8,12},{12,8},{16,20},{20,16},{24,28},{28,24},{1,5},{5... | collective-permute-start | bytes 2359304 | tf_op jit(solution)/shard_map/ppermute | solution.py:28
  494.0 37.3 %collective-permute-start.99 = (bf16[1,1,192,1024]{3,2,1,0:T(8,128)(2,1)S(1)}, bf16[1,1,192,1024]{3,2,1,0:T(8,128)(2,1)S(1)}, u32[]{:S(2)}, u32[]{:S(2)}) collective-permute-start(bf16[1,1,192,1024]{3,2,1,0:T(8,128)(2,1)S(1)} %copy-done.73), channel_id=1, source_target_pairs={{8,0},{12,4},{16,24},{20,28},{9,1},{13,5},{17,25},{21,29},{10,2},{... | collective-permute-start | bytes 1179656 | tf_op jit(solution)/shard_map/ppermute | solution.py:116
  495.4 46.8 %collective-permute-start.86 = (bf16[1,1,192,1024]{3,2,1,0:T(8,128)(2,1)S(1)}, bf16[1,1,192,1024]{3,2,1,0:T(8,128)(2,1)S(1)}, u32[]{:S(2)}, u32[]{:S(2)}) collective-permute-start(bf16[1,1,192,1024]{3,2,1,0:T(8,128)(2,1)S(1)} %copy-done.72), channel_id=1, source_target_pairs={{0,8},{4,12},{24,16},{28,20},{1,9},{5,13},{25,17},{29,21},{2,10},{... | collective-permute-start | bytes 1179656 | tf_op jit(solution)/shard_map/ppermute | solution.py:113
  554.0 37.3 %collective-permute-start.101 = (bf16[512,1024]{1,0:T(8,128)(2,1)}, bf16[512,1024]{1,0:T(8,128)(2,1)}, u32[]{:S(2)}, u32[]{:S(2)}) collective-permute-start(bf16[512,1024]{1,0:T(8,128)(2,1)} %get-tuple-element.139), channel_id=1, source_target_pairs={{0,4},{4,0},{8,12},{12,8},{16,20},{20,16},{24,28},{28,24},{1,5},{5... | collective-permute-start | bytes 3145736 | tf_op jit(solution)/shard_map/ppermute | solution.py:28
  555.5 88.0 %collective-permute-start.78 = (bf16[768,512]{1,0:T(8,128)(2,1)}, bf16[768,512]{1,0:T(8,128)(2,1)S(1)}, u32[]{:S(2)}, u32[]{:S(2)}) collective-permute-start(bf16[768,512]{1,0:T(8,128)(2,1)} %bitcast.58), channel_id=1, source_target_pairs={{0,4},{4,0},{8,12},{12,8},{16,20},{20,16},{24,28},{28,24},{1,5},{5... | collective-permute-start | bytes 2359304 | tf_op jit(solution)/shard_map/ppermute | solution.py:28
  566.2 78.2 %collective-permute-start.90 = (bf16[512,1024]{1,0:T(8,128)(2,1)}, bf16[512,1024]{1,0:T(8,128)(2,1)}, u32[]{:S(2)}, u32[]{:S(2)}) collective-permute-start(bf16[512,1024]{1,0:T(8,128)(2,1)} %get-tuple-element.86), channel_id=1, source_target_pairs={{0,4},{4,0},{8,12},{12,8},{16,20},{20,16},{24,28},{28,24},{1,5},{5... | collective-permute-start | bytes 3145736 | tf_op jit(solution)/shard_map/ppermute | solution.py:28
  577.6 58.8 %collective-permute-start.100 = (bf16[768,512]{1,0:T(8,128)(2,1)S(1)}, bf16[768,512]{1,0:T(8,128)(2,1)S(1)}, u32[]{:S(2)}, u32[]{:S(2)}) collective-permute-start(bf16[768,512]{1,0:T(8,128)(2,1)S(1)} %bitcast.308), channel_id=1, source_target_pairs={{0,4},{4,0},{8,12},{12,8},{16,20},{20,16},{24,28},{28,24},{1,5},{5... | collective-permute-start | bytes 2359304 | tf_op jit(solution)/shard_map/ppermute | solution.py:28
  589.7 68.5 %collective-permute-start.79 = (bf16[512,1024]{1,0:T(8,128)(2,1)S(1)}, bf16[512,1024]{1,0:T(8,128)(2,1)S(1)}, u32[]{:S(2)}, u32[]{:S(2)}) collective-permute-start(bf16[512,1024]{1,0:T(8,128)(2,1)S(1)} %copy-done.44), channel_id=1, source_target_pairs={{0,4},{4,0},{8,12},{12,8},{16,20},{20,16},{24,28},{28,24},{1,5},{5... | collective-permute-start | bytes 3145736 | tf_op jit(solution)/shard_map/ppermute | solution.py:28
  591.3 55.6 %collective-permute-start.34 = (bf16[128,1536]{1,0:T(8,128)(2,1)S(1)}, bf16[128,1536]{1,0:T(8,128)(2,1)S(1)}, u32[]{:S(2)}, u32[]{:S(2)}) collective-permute-start(bf16[128,1536]{1,0:T(8,128)(2,1)S(1)} %fusion.98), channel_id=1, source_target_pairs={{0,2},{1,3},{2,0},{3,1},{4,6},{5,7},{6,4},{7,5},{8,10},{9,11},{10,... | collective-permute-start | bytes 1179656 | tf_op jit(solution)/shard_map/ppermute | solution.py:28
  638.7 42.0 %collective-permute-start.103 = (bf16[1,2,192,1024]{3,2,1,0:T(8,128)(2,1)S(1)}, bf16[1,2,192,1024]{3,2,1,0:T(8,128)(2,1)S(1)}, u32[]{:S(2)}, u32[]{:S(2)}) collective-permute-start(bf16[1,2,192,1024]{3,2,1,0:T(8,128)(2,1)S(1)} %constant_dynamic-slice_fusion.4), channel_id=1, source_target_pairs={{0,8},{4,12},{24,16},{28,20},{1,9},{5,13},{25,17},{29,21},{2,10},{... | collective-permute-start | bytes 2359304 | tf_op jit(solution)/shard_map/ppermute | solution.py:112
  683.7 55.7 %collective-permute-start.93 = (bf16[1,2,192,1024]{3,2,1,0:T(8,128)(2,1)}, bf16[1,2,192,1024]{3,2,1,0:T(8,128)(2,1)}, u32[]{:S(2)}, u32[]{:S(2)}) collective-permute-start(bf16[1,2,192,1024]{3,2,1,0:T(8,128)(2,1)} %add_convert_fusion.11), channel_id=1, source_target_pairs={{8,16},{12,20},{16,8},{20,12},{9,17},{13,21},{17,9},{21,13},{10,18... | collective-permute-start | bytes 2359304 | tf_op jit(solution)/shard_map/ppermute | solution.py:114
  696.0 47.2 %collective-permute-start.82 = (bf16[1,2,192,1024]{3,2,1,0:T(8,128)(2,1)}, bf16[1,2,192,1024]{3,2,1,0:T(8,128)(2,1)}, u32[]{:S(2)}, u32[]{:S(2)}) collective-permute-start(bf16[1,2,192,1024]{3,2,1,0:T(8,128)(2,1)} %add_convert_fusion.13), channel_id=1, source_target_pairs={{8,16},{12,20},{16,8},{20,12},{9,17},{13,21},{17,9},{21,13},{10,18... | collective-permute-start | bytes 2359304 | tf_op jit(solution)/shard_map/ppermute | solution.py:114
  698.8 49.3 %collective-permute-start.102 = (bf16[1,1,192,1024]{3,2,1,0:T(8,128)(2,1)}, bf16[1,1,192,1024]{3,2,1,0:T(8,128)(2,1)}, u32[]{:S(2)}, u32[]{:S(2)}) collective-permute-start(bf16[1,1,192,1024]{3,2,1,0:T(8,128)(2,1)} %get-tuple-element.52), channel_id=1, source_target_pairs={{0,8},{4,12},{24,16},{28,20},{1,9},{5,13},{25,17},{29,21},{2,10},{... | collective-permute-start | bytes 1179656 | tf_op jit(solution)/shard_map/ppermute | solution.py:113
  710.1 39.4 %collective-permute-start.105 = (bf16[1,1,192,1024]{3,2,1,0:T(8,128)(2,1)}, bf16[1,1,192,1024]{3,2,1,0:T(8,128)(2,1)}, u32[]{:S(2)}, u32[]{:S(2)}) collective-permute-start(bf16[1,1,192,1024]{3,2,1,0:T(8,128)(2,1)} %get-tuple-element.51), channel_id=1, source_target_pairs={{8,0},{12,4},{16,24},{20,28},{9,1},{13,5},{17,25},{21,29},{10,2},{... | collective-permute-start | bytes 1179656 | tf_op jit(solution)/shard_map/ppermute | solution.py:116
  718.9 61.4 %collective-permute-start.66 = (bf16[768,512]{1,0:T(8,128)(2,1)}, bf16[768,512]{1,0:T(8,128)(2,1)}, u32[]{:S(2)}, u32[]{:S(2)}) collective-permute-start(bf16[768,512]{1,0:T(8,128)(2,1)} %bitcast.40), channel_id=1, source_target_pairs={{0,4},{4,0},{8,12},{12,8},{16,20},{20,16},{24,28},{28,24},{1,5},{5... | collective-permute-start | bytes 2359304 | tf_op jit(solution)/shard_map/ppermute | solution.py:28
  758.5 52.8 %collective-permute-start.54 = (bf16[768,512]{1,0:T(8,128)(2,1)}, bf16[768,512]{1,0:T(8,128)(2,1)}, u32[]{:S(2)}, u32[]{:S(2)}) collective-permute-start(bf16[768,512]{1,0:T(8,128)(2,1)} %bitcast.28), channel_id=1, source_target_pairs={{0,4},{4,0},{8,12},{12,8},{16,20},{20,16},{24,28},{28,24},{1,5},{5... | collective-permute-start | bytes 2359304 | tf_op jit(solution)/shard_map/ppermute | solution.py:28
  796.2 43.5 %collective-permute-start.68 = (bf16[1,1,192,384]{3,2,1,0:T(8,128)(2,1)S(1)}, bf16[1,1,192,384]{3,2,1,0:T(8,128)(2,1)S(1)}, u32[]{:S(2)}, u32[]{:S(2)}) collective-permute-start(bf16[1,1,192,384]{3,2,1,0:T(8,128)(2,1)S(1)} %get-tuple-element.64), channel_id=1, source_target_pairs={{0,8},{4,12},{24,16},{28,20},{1,9},{5,13},{25,17},{29,21},{2,10},{... | collective-permute-start | bytes 442376 | tf_op jit(solution)/shard_map/ppermute | solution.py:113
  (203 other events, 2615.1 us)

commit v2 on v1

--- a/solution.py
+++ b/solution.py
@@ -19,8 +19,38 @@
 VMEM_BYTES = 56 * 2**20
 
 
+def takes(us):
+    return pl.CostEstimate(flops=int(us * 1.1e9), transcendentals=0, bytes_accessed=int(us * 1e6))
+
+
 def mm(a, b, ca, cb):
     return lax.dot_general(a, b, (((ca,), (cb,)), ((), ())), preferred_element_type=F32)
+
+
+def after(x, token):
+    if token is None:
+        return x
+    return lax.optimization_barrier((x, token))[0]
+
+
+def need(*values):
+    return lax.optimization_barrier(values)
+
+
+class Job:
+    def __init__(self, make):
+        self.make = make
+        self.out = None
+
+
+def window(start, end, jobs):
+    if not jobs:
+        return end
+    leaves, tree = jax.tree.flatten([job.make(start) for job in jobs])
+    end, *leaves = need(end, *leaves)
+    for job, out in zip(jobs, jax.tree.unflatten(tree, leaves)):
+        job.out = out
+    return end
 
 
 def swap(block, axis, mask):
@@ -32,17 +62,18 @@
     return lax.reduce_precision(x, 8, 7).astype(BF)
 
 
-def gather_rows(own):
-    pair = jnp.concatenate([own, swap(own, "tensor", 2)], axis=0)
+def gather_rows(own, jobs=()):
+    beside = window(own, swap(own, "tensor", 2), jobs)
+    pair = jnp.concatenate([own, beside], axis=0)
     return jnp.concatenate([pair, swap(pair, "tensor", 1)], axis=0)
 
 
-def reduce_rows(keep, send):
+def reduce_rows(keep, send, jobs=()):
     quarter = keep.shape[0] // 2
     got = swap(send, "tensor", 1)
     far = (keep[quarter:] + got[quarter:].astype(F32)).astype(BF)
     near = keep[:quarter] + got[:quarter].astype(F32)
-    return near + swap(far, "tensor", 2).astype(F32)
+    return near + window(far, swap(far, "tensor", 2), jobs).astype(F32)
 
 
 RELATIVE = (0, 2, 1, 3)
@@ -76,56 +107,25 @@
 
 def keys_onward(kv):
     n = lax.axis_size("dp")
-    beside = swap(kv, "dp", 1)
-    behind = lax.ppermute(kv, "dp", in_stretches(lambda s: 2 if s < 2 else None, n))
-    across = lax.ppermute(behind, "dp", [(i, i ^ 1) for i in range(n) if (i + 2) % 4 >= 2])
-    return beside, behind, across
+    across = lax.ppermute(kv, "dp", in_stretches(lambda s: (3, 1, None, None)[s], n))
+    behind = lax.ppermute(kv, "dp", in_stretches(lambda s: (2, 2, None, None)[s], n))
+    return swap(kv, "dp", 1), behind, across
 
 
 def keys_back(beside, behind, across):
     n = lax.axis_size("dp")
-    late = [i for i in range(n) if (i + 2) % 4 >= 2]
-    got = lax.ppermute(across, "dp", [(i, i ^ 1) for i in late])
-    from_beside = swap(beside, "dp", 1)
-    total = (behind.astype(F32) + got.astype(F32)).astype(BF)
-    from_behind = lax.ppermute(total, "dp", in_stretches(lambda s: -2 if s >= 2 else None, n))
-    return from_beside, from_behind
-
-
-def scatter_line(grad):
+    across = lax.ppermute(across, "dp", in_stretches(lambda s: (None, None, -1, -3)[s], n))
+    behind = lax.ppermute(behind, "dp", in_stretches(lambda s: (None, None, -2, -2)[s], n))
+    return swap(beside, "dp", 1), behind, across
+
+
+def scatter_grad(grad):
     n = lax.axis_size("dp")
-    outer = n // 8
-    r = grad.shape[0] * 2 // n
-    z = lax.axis_index("dp") // 2 % 4
-    g4 = grad.reshape(outer, 4, r, grad.shape[1])
-    out_in, middle, in_out = [], [], []
-    for i in range(n):
-        zi = i // 2 % 4
-        if zi in (0, 3):
-            j = i + 2 if zi == 0 else i - 2
-            out_in.append((i, j))
-            in_out.append((j, i))
-        else:
-            middle.append((i, i + 2 if zi == 1 else i - 2))
-    cross = lax.dynamic_slice_in_dim(g4, 2 * (1 - z // 2), 2, 1)
-    beside = lax.dynamic_slice_in_dim(g4, z ^ 1, 1, 1)
-    got_cross = lax.ppermute(cross, "dp", out_in)
-    got_beside = lax.ppermute(beside, "dp", out_in)
-    over = lax.ppermute((cross.astype(F32) + got_cross.astype(F32)).astype(BF), "dp", middle)
-    on = beside.astype(F32) + lax.dynamic_slice_in_dim(over, (z ^ 1) & 1, 1, 1).astype(F32)
-    last = lax.ppermute(on.astype(BF), "dp", in_out)
-    own = lax.dynamic_slice_in_dim(g4, z, 1, 1).astype(F32)
-    own = own + got_beside.astype(F32)
-    own = own + lax.dynamic_slice_in_dim(over, z & 1, 1, 1).astype(F32) + last.astype(F32)
-    own = own[:, 0]
-    if outer == 1:
-        return own[0]
-    place = lax.axis_index("dp") // 8
-    total = lax.dynamic_index_in_dim(own, place, 0, keepdims=False)
-    for k in range(1, outer):
-        piece = lax.dynamic_index_in_dim(own, (place + k) % outer, 0, keepdims=False).astype(BF)
-        total = total + lax.ppermute(piece, "dp", [(i, (i + 8 * k) % n) for i in range(n)]).astype(F32)
-    return total
+    groups = [list(range(side, n, 2)) for side in range(2)]
+    out = lax.psum_scatter(
+        grad.astype(BF), "dp", scatter_dimension=0, tiled=True, axis_index_groups=groups
+    )
+    return out.astype(F32)
 
 
 def sum_everywhere(x):
@@ -164,6 +164,7 @@
         scratch_shapes=[pltpu.VMEM((cols, rows), F32)],
         compiler_params=pltpu.CompilerParams(vmem_limit_bytes=VMEM_BYTES),
         name="qkv_rotary",
+        cost_estimate=takes(4.5),
     )(x, w, cosine, sine)
 
 
@@ -241,6 +242,7 @@
         scratch_shapes=[pltpu.VMEM((4, rows, 2 * rows), F32)],
         compiler_params=pltpu.CompilerParams(vmem_limit_bytes=VMEM_BYTES),
         name="attention_forward",
+        cost_estimate=takes(11),
     )(*places, qkv_t, *operands)
     return mixed_t, log_total
 
@@ -300,26 +302,28 @@
         + [jax.ShapeDtypeStruct((2, kv * HD, rows), BF)] * 3,
         compiler_params=pltpu.CompilerParams(vmem_limit_bytes=VMEM_BYTES),
         name="attention_backward",
+        cost_estimate=takes(16.5),
     )(*places, *tables, qkv_t, *operands, log_total, mixed_t, grad_t)
     return outs
 
 
-def join_kernel(kv, dq_ref, own_ref, one_ref, two_ref, cos_ref, sin_ref, out_ref, t_ref):
+def join_kernel(kv, dq_ref, own_ref, one_ref, two_ref, three_ref, cos_ref, sin_ref, out_ref, t_ref):
     wide = dq_ref.shape[0]
     half = HD // 2
     cosine, sine = cos_ref[...], sin_ref[...]
     t_ref[:wide] = dq_ref[...].astype(F32)
-    dk = own_ref[0] + one_ref[0].astype(F32) + two_ref[0].astype(F32)
+    total = lambda i: own_ref[i] + sum(r[i].astype(F32) for r in (one_ref, two_ref, three_ref))
+    dk = total(0)
     for h in range(kv):
         a = h * HD
         top, low = turned_pair(dk[a : a + half], dk[a + half : a + HD], cosine, -sine)
         t_ref[wide + a : wide + a + half] = top
         t_ref[wide + a + half : wide + a + HD] = low
-    t_ref[wide + kv * HD :] = own_ref[1] + one_ref[1].astype(F32) + two_ref[1].astype(F32)
+    t_ref[wide + kv * HD :] = total(1)
     out_ref[...] = t_ref[...].T.astype(BF)
 
 
-def join_call(dq, own, one, two, tables, kv):
+def join_call(dq, own, far, tables, kv):
     rows = dq.shape[1]
     cols = dq.shape[0] + 2 * kv * HD
     return pl.pallas_call(
@@ -328,35 +332,87 @@
         scratch_shapes=[pltpu.VMEM((cols, rows), F32)],
         compiler_params=pltpu.CompilerParams(vmem_limit_bytes=VMEM_BYTES),
         name="join_gradients",
-    )(dq, own, one, two, *tables)
-
-
-def halves_of(x, n):
+        cost_estimate=takes(2.8),
+    )(dq, own, *far, *tables)
+
+
+def turned_halves(x, n):
     side = lax.axis_index("dp") % 2
-    cols = x.T.reshape(n // 2, 2, x.shape[1] // n, x.shape[0])
-    mine = lax.dynamic_index_in_dim(cols, side, 1, keepdims=False)
-    other = lax.dynamic_index_in_dim(cols, 1 - side, 1, keepdims=False)
-    return mine.reshape(-1, x.shape[0]), other.reshape(-1, x.shape[0])
-
-
-class Side:
-    def __init__(self, mine, theirs):
-        self.mine = mine
-        self.theirs = theirs
-
-
-def split_side(x, n):
-    mine, other = halves_of(x, n)
-    return Side(mine, swap(other, "dp", 1))
-
-
-def whole_side(x):
-    return Side(x, swap(x, "dp", 1))
-
-
-def weight_grad(left, right):
-    total = mm(left.mine, right.mine, 1, 0) + mm(left.theirs, right.theirs, 1, 0)
-    return scatter_line(total.astype(BF))
+    rows, cols = x.shape
+    r, half = cols // n, cols // 2
+
+    def kernel(side_ref, x_ref, mine_ref, other_ref, t_ref):
+        t_ref[...] = x_ref[...].astype(F32).T.astype(BF)
+        for odd in range(2):
+
+            @pl.when(side_ref[0] == odd)
+            def _():
+                for b in range(n):
+                    to = slice(b // 2 * r, (b // 2 + 1) * r)
+                    block = t_ref[b * r : (b + 1) * r]
+                    if b % 2 == odd:
+                        mine_ref[to] = block
+                    else:
+                        other_ref[to] = block[:, : rows // 2]
+
+    whole = pl.BlockSpec(memory_space=pltpu.VMEM)
+    return pl.pallas_call(
+        kernel,
+        in_specs=[pl.BlockSpec(memory_space=pltpu.SMEM), whole],
+        out_specs=[whole, whole],
+        out_shape=[jax.ShapeDtypeStruct((half, rows), BF), jax.ShapeDtypeStruct((half, rows // 2), BF)],
+        scratch_shapes=[pltpu.VMEM((cols, rows), BF)],
+        compiler_params=pltpu.CompilerParams(vmem_limit_bytes=VMEM_BYTES),
+        name="turned_halves",
+        cost_estimate=takes(3),
+    )(side[None].astype(jnp.int32), x)
+
+
+class Turned:
+    def __init__(self, read, n):
+        self.turn = Job(lambda token: turned_halves(after(read(), token), n))
+        self.send = Job(lambda token: swap(after(self.turn.out[1], token), "dp", 1))
+        self.whole = None
+
+    def parts(self):
+        if self.whole is None:
+            got = self.send.out
+            self.whole = jnp.concatenate([got, swap(got, "tensor", 1)], axis=1)
+        return self.turn.out[0], self.whole
+
+
+class Sent:
+    def __init__(self, read, chunks):
+        self.read = read
+        self.sends = [self.chunk(i, chunks) for i in range(chunks)]
+
+    def chunk(self, i, chunks):
+        def make(token):
+            x = self.read()
+            rows = x.shape[0] // chunks
+            return swap(after(x[i * rows : (i + 1) * rows], token), "dp", 1)
+
+        return Job(make)
+
+    def parts(self):
+        got = [job.out for job in self.sends]
+        return self.read(), got[0] if len(got) == 1 else jnp.concatenate(got, axis=0)
+
+
+def product(left, right, cb=0):
+    def make(token):
+        (a, b), (c, d) = left.parts(), right.parts()
+        return (mm(a, after(c, token), 1, cb) + mm(b, after(d, token), 1, cb)).astype(BF)
+
+    return Job(make)
+
+
+def scatter(*products):
+    def make(token):
+        parts = [p.out for p in products]
+        return scatter_grad(parts[0] if len(parts) == 1 else jnp.concatenate(parts, axis=1))
+
+    return Job(make)
 
 
 def inverse_rms(x):
@@ -414,68 +470,124 @@
     def own_rows(x):
         return lax.dynamic_slice_in_dim(x, t * quarter, quarter, 0)
 
+    value = {}
+
+    def later(name, l):
+        return lambda: value[name, l]
+
+    layers = range(LAYERS)
+    down_left = [Turned(later("down_in", l), n) for l in layers]
+    attn_left = [Turned(later("normed", l), n) for l in layers]
+    mlp_left = [Turned(later("normed_mlp", l), n) for l in layers]
+    out_left = [Turned(later("out_in", l), n) for l in layers]
+    act_right = [Sent(later("act", l), 2) for l in layers]
+    mixed_right = [Sent(later("mixed", l), 1) for l in layers]
+    both_right = [Sent(later("both", l), 4) for l in layers]
+    qkv_right = [Sent(later("d_qkv", l), 2) for l in layers]
+    g_down = [product(down_left[l], act_right[l]) for l in layers]
+    g_both = [product(mlp_left[l], both_right[l]) for l in layers]
+    g_out = [product(out_left[l], mixed_right[l], 1) for l in layers]
+    g_qkv = [product(attn_left[l], qkv_right[l]) for l in layers]
+    s_down = [scatter(g_down[l]) for l in layers]
+    s_both = [scatter(g_both[l]) for l in layers]
+    s_attn = [scatter(g_out[l], g_qkv[l]) for l in layers]
+    plan = {
+        ("keys", 0): [down_left[1].turn],
+        ("attn", 0): [down_left[1].send],
+        ("sum1", 0): [attn_left[0].turn, *mixed_right[0].sends],
+        ("all1", 0): [attn_left[0].send],
+        ("sum2", 0): [act_right[0].sends[0], mlp_left[0].turn],
+        ("all2", 0): [act_right[0].sends[1]],
+        ("attn", 1): [mlp_left[0].send],
+        ("sum1", 1): [attn_left[1].turn, *mixed_right[1].sends],
+        ("all1", 1): [attn_left[1].send],
+        ("back_sum1", 1): [both_right[1].sends[0], mlp_left[1].turn],
+        ("back_all1", 1): [both_right[1].sends[1]],
+        ("back_attn", 1): [both_right[1].sends[2], mlp_left[1].send],
+        ("back_keys", 1): [both_right[1].sends[3], out_left[1].turn],
+        ("back_join", 1): [act_right[1].sends[0]],
+        ("back_sum2", 1): [act_right[1].sends[1], g_both[1]],
+        ("back_all2", 1): [out_left[1].send, g_down[1]],
+        ("back_gate", 0): [qkv_right[1].sends[0]],
+        ("back_mlp", 0): [qkv_right[1].sends[1]],
+        ("back_sum1", 0): [both_right[0].sends[0], down_left[0].turn, g_qkv[1], g_out[1], s_both[1]],
+        ("back_all1", 0): [both_right[0].sends[1], s_down[1]],
+        ("back_attn", 0): both_right[0].sends[2:],
+        ("back_keys", 0): [out_left[0].turn, g_both[0], s_attn[1]],
+        ("back_join", 0): [down_left[0].send],
+        ("back_sum2", 0): [out_left[0].send, g_down[0]],
+        ("back_all2", 0): [*qkv_right[0].sends, s_both[0]],
+    }
+    jobs = lambda name, l: plan.get((name, l), [])
+
+    value["down_in", LAYERS - 1] = to_relative(cotangent.astype(BF), t)
     flow = own_rows(hidden_in)
     inverse = inverse_rms(flow)
     normed_all = to_relative((hidden_in * inverse_rms(hidden_in) * norm_attn[0]).astype(BF), t)
     records = []
-    for l in range(LAYERS):
+    for l in layers:
+        value["normed", l] = normed_all
         qkv_t = qkv_call(normed_all, w_qkv[l], *tables, heads + kv)
         far = keys_onward(qkv_t[heads * HD :])
+        far = far[:2] + (window(qkv_t, far[2], jobs("keys", l)),)
         mixed_t, log_total = attn_fwd(qkv_t, far, places, kv)
+        mixed_t = value["mixed", l] = window(far[2], mixed_t, jobs("attn", l))
         send = mm(mixed_t[:, pair:], w_out[l], 0, 0).astype(BF)
         keep = mm(mixed_t[:, :pair], w_out[l], 0, 0)
-        middle = flow + reduce_rows(keep, send)
+        middle = flow + reduce_rows(keep, send, jobs("sum1", l))
         inverse_mlp = inverse_rms(middle)
-        normed_mlp = gather_rows((middle * inverse_mlp * norm_mlp[l]).astype(BF))
+        normed_mlp = gather_rows((middle * inverse_mlp * norm_mlp[l]).astype(BF), jobs("all1", l))
+        value["normed_mlp", l] = normed_mlp
         gate = mm(normed_mlp, w_gate[l], 1, 0)
         up = mm(normed_mlp, w_up[l], 1, 0)
         activated = (jax.nn.silu(gate) * up).astype(BF)
+        activated = value["act", l] = window(normed_mlp, activated, jobs("mlp", l))
         send = mm(activated[pair:], w_down[l], 1, 0).astype(BF)
         keep = mm(activated[:pair], w_down[l], 1, 0)
-        after = middle + reduce_rows(keep, send)
-        records.append(
-            (flow, inverse, normed_all, qkv_t, far, mixed_t, log_total, middle, inverse_mlp, normed_mlp, gate, up, activated)
-        )
-        flow = after
+        records.append((flow, inverse, qkv_t, far, log_total, middle, inverse_mlp, gate, up))
+        flow = middle + reduce_rows(keep, send, jobs("sum2", l))
         if l + 1 < LAYERS:
             inverse = inverse_rms(flow)
-            normed_all = gather_rows((flow * inverse * norm_attn[l + 1]).astype(BF))
+            normed_all = gather_rows((flow * inverse * norm_attn[l + 1]).astype(BF), jobs("all2", l))
     hidden_out = to_absolute(gather_rows(bf16_of(flow)), t).astype(F32)
 
     flow = own_rows(cotangent)
-    down_in = to_relative(cotangent.astype(BF), t)
-    grads = [None] * LAYERS
     gains = [None] * LAYERS
-    for l in reversed(range(LAYERS)):
-        (before, inverse, normed_all, qkv_t, far, mixed_t, log_total, middle, inverse_mlp, normed_mlp, gate, up, activated) = records[l]
-        g_down = weight_grad(split_side(down_in, n), whole_side(activated))
+    for l in reversed(layers):
+        before, inverse, qkv_t, far, log_total, middle, inverse_mlp, gate, up = records[l]
+        down_in = value["down_in", l]
         hidden = mm(down_in, w_down[l], 1, 1)
         sig = jax.nn.sigmoid(gate)
         gate_grad = (hidden * up * sig * (1.0 + gate * (1.0 - sig))).astype(BF)
         up_grad = (hidden * gate * sig).astype(BF)
+        both = jnp.concatenate([gate_grad, up_grad], axis=1)
+        value["both", l] = window(down_in, both, jobs("back_gate", l))
         send = (mm(gate_grad[pair:], w_gate[l], 1, 1) + mm(up_grad[pair:], w_up[l], 1, 1)).astype(BF)
         keep = mm(gate_grad[:pair], w_gate[l], 1, 1) + mm(up_grad[:pair], w_up[l], 1, 1)
-        flow, gain_mlp = norm_back(middle, inverse_mlp, norm_mlp[l], reduce_rows(keep, send), flow)
-        normed_side = split_side(normed_mlp, n)
-        g_gate = weight_grad(normed_side, whole_side(gate_grad))
-        g_up = weight_grad(normed_side, whole_side(up_grad))
-        out_in = gather_rows(flow.astype(BF))
+        send = window(both, send, jobs("back_mlp", l))
+        total = reduce_rows(keep, send, jobs("back_sum1", l))
+        flow, gain_mlp = norm_back(middle, inverse_mlp, norm_mlp[l], total, flow)
+        out_in = value["out_in", l] = gather_rows(flow.astype(BF), jobs("back_all1", l))
         grad_t = mm(w_out[l], out_in, 1, 1).astype(BF)
-        dq, own, d_beside, d_behind, d_across = attn_bwd(
-            qkv_t, far, places, kv, tables, log_total, mixed_t, grad_t
-        )
-        g_out = weight_grad(split_side(out_in, n), whole_side(mixed_t.T))
-        from_beside, from_behind = keys_back(d_beside, d_behind, d_across)
-        d_qkv = join_call(dq, own, from_beside, from_behind, tables, kv)
+        dq, own, *d_far = attn_bwd(qkv_t, far, places, kv, tables, log_total, value["mixed", l], grad_t)
+        dq = window(out_in, dq, jobs("back_attn", l))
+        d_far = keys_back(*d_far)
+        d_far = d_far[:2] + (window(dq, d_far[2], jobs("back_keys", l)),)
+        d_qkv = value["d_qkv", l] = join_call(dq, own, d_far, tables, kv)
         send = mm(d_qkv[pair:], w_qkv[l], 1, 1).astype(BF)
         keep = mm(d_qkv[:pair], w_qkv[l], 1, 1)
-        flow, gain_attn = norm_back(before, inverse, norm_attn[l], reduce_rows(keep, send), flow)
-        g_qkv = weight_grad(split_side(normed_all, n), whole_side(d_qkv))
+        send = window(d_far[2], send, jobs("back_join", l))
+        if l + 1 == LAYERS:
+            send, hidden_out = need(send, hidden_out)
+        total = reduce_rows(keep, send, jobs("back_sum2", l))
+        flow, gain_attn = norm_back(before, inverse, norm_attn[l], total, flow)
+        gains[l] = (gain_attn, gain_mlp)
         if l > 0:
-            down_in = gather_rows(flow.astype(BF))
-        grads[l] = (g_qkv, g_out, g_gate, g_up, g_down)
-        gains[l] = (gain_attn, gain_mlp)
-    input_grad = to_absolute(gather_rows(bf16_of(flow)), t).astype(F32)
+            value["down_in", l - 1] = gather_rows(flow.astype(BF), jobs("back_all2", l))
+    last = gather_rows(bf16_of(flow), jobs("back_all2", 0))
+    for job in (s_down[0], g_qkv[0], g_out[0], s_attn[0]):
+        job.out = job.make(None)
+    input_grad = to_absolute(last, t).astype(F32)
 
     early = sum_everywhere(jnp.stack([gains[1][0], gains[1][1], gains[0][1]]))
     late = sum_everywhere(gains[0][0][None])
@@ -486,22 +598,29 @@
     norm_attn_grad = jnp.concatenate([late, early[:1]], axis=0)
     norm_mlp_grad = jnp.stack([early[2], early[1]])
 
-    stack = lambda i: jnp.stack([grads[l][i] for l in range(LAYERS)])
-    g_qkv = stack(0)
-    a, b = heads * HD, (heads + kv) * HD
-    turned = lambda i: jnp.stack([grads[l][i].T for l in range(LAYERS)])
-    return (
+    def stack(job, start, stop, turn=False):
+        parts = [job[l].out[:, start:stop] for l in layers]
+        return jnp.stack([p.T if turn else p for p in parts])
+
+    units = w_gate.shape[2]
+    a, b, c = heads * HD, 2 * heads * HD, (2 * heads + kv) * HD
+    early = (
         hidden_out,
         input_grad,
         norm_attn_grad,
         norm_mlp_grad,
-        g_qkv[:, :, :a],
-        g_qkv[:, :, a:b],
-        g_qkv[:, :, b:],
-        turned(1),
-        stack(2),
-        stack(3),
-        turned(4),
+        stack(s_both, 0, units),
+        stack(s_both, units, None),
+        stack(s_down, 0, None, True),
+    )
+    *early, s_attn[0].out = need(*early, s_attn[0].out)
+    return (
+        *early[:4],
+        stack(s_attn, a, b),
+        stack(s_attn, b, c),
+        stack(s_attn, c, None),
+        stack(s_attn, 0, a, True),
+        *early[4:],
     )
 
 

time: 873 us -> 686 us (0.79)
  starting transfers between devices: 219 us -> 95.9 us
  waiting for transfers between devices: 327 us -> 257 us
  Pallas kernels: 69.8 us -> 95.8 us
  local copies, waits for them, and re-layouts: 59.6 us -> 33.7 us
  matrix products: 108 us -> 86.4 us
  other arithmetic: 79.4 us -> 93.8 us
  between operations: 3.55 us -> 16.7 us
    ppermute x48 -> x8, starting transfers between devices: 155 us -> 20.5 us  [the longest x2 8.53 us: keys_back(): lax.ppermute(behind, 'dp', in_stretches(lambda s: (None, None, -2, -2)[s]...]
    ppermute x48 -> x8, waiting for transfers between devices: 96.8 us -> 34.5 us  [the longest x2 14.9 us: keys_onward(): lax.ppermute(kv, 'dp', in_stretches(lambda s: (3, 1, None, None)[s], n))]
    ppermute x64 -> x80, waiting for transfers between devices: 230 us -> 173 us  [swap(): return lax.ppermute(block, axis, [(i, i ^ mask) for i in range(n)])]
    reduce_scatter x0 -> x6, waiting for transfers between devices: none -> 49 us  [scatter_grad(): lax.psum_scatter(grad.astype(BF), 'dp', scatter_dimension=0, tiled=True,...]
    pallas_call x0 -> x8, Pallas kernels: none -> 25.4 us  [turned_halves(): pl.pallas_call(kernel, in_specs=[pl.BlockSpec(memory_space=pltpu.SMEM), w...]
    dot_general x48 -> x44, matrix products: 108 us -> 86.4 us  [mm(): lax.dot_general(a, b, (((ca,), (cb,)), ((), ())), preferred_element_type=...]
    transpose x7 -> x0, local copies, waits for them, and re-layouts: 16.6 us -> none  [halves_of(): cols = x.T.reshape(n // 2, 2, x.shape[1] // n, x.shape[0])]
    dynamic_slice x17 -> x0, local copies, waits for them, and re-layouts: 15.7 us -> none  [the longest x3 8.1 us: halves_of(): mine = lax.dynamic_index_in_dim(cols, side, 1, keepdims=False)]
  transfers between devices with their start and end apart: 112 -> 94, of which waited for: 42 -> 48; matrix products, arithmetic and copies ran while one was open for 23% -> 21% of each run, Pallas kernels for 4% -> 13%
where the time goes in v2:
time: 686 us; the launch traced here: 679 us
  waiting for transfers between devices  257 us (37%)
  starting transfers between devices  95.9 us (14%)
  Pallas kernels  95.8 us (14%)
  other arithmetic  93.8 us (14%)
  matrix products  86.4 us (13%)
  local copies, waits for them, and re-layouts  33.7 us (5%)
  between operations  16.7 us (2%)
    ppermute x80, waiting for transfers between devices, swap(): return lax.ppermute(block, axis, [(i, i ^ mask) for i in range(n)])  173 us
    dot_general x44, matrix products, mm(): lax.dot_general(a, b, (((ca,), (cb,)), ((), ())), preferred_element_type=...  86.4 us
    ppermute x80, starting transfers between devices, swap(): return lax.ppermute(block, axis, [(i, i ^ mask) for i in range(n)])  74.7 us
    reduce_scatter x6, waiting for transfers between devices, scatter_grad(): lax.psum_scatter(grad.astype(BF), 'dp', scatter_dimension=0, tiled=True,...  49 us
    pallas_call x2, Pallas kernels, attn_bwd(): pl.pallas_call(attn_bwd_kernel, grid=(kv,), in_specs=place_specs + [table...  32.8 us
    pallas_call x8, Pallas kernels, turned_halves(): pl.pallas_call(kernel, in_specs=[pl.BlockSpec(memory_space=pltpu.SMEM), w...  25.4 us
    pallas_call x2, Pallas kernels, attn_fwd(): pl.pallas_call(attn_fwd_kernel, grid=(kv,), in_specs=place_specs + [q_spe...  22.1 us
    unnamed x260, local copies, waits for them, and re-layouts  15.7 us
  transfers between devices with their start and end apart: 94, of which 48 were waited for; matrix products, arithmetic and copies ran while one was open for 21% of the time, Pallas kernels for 13%

profile of v2, /device:TPU:0, one launch (start us, length us, event | category | flops | bytes accessed | tf_op | source)
XLA Modules:
  0.0 678.8 jit_solution(16359242804372265397)
XLA Ops:
  28.7 4.6 qkv_rotary.2.q_ref.refs_0_.refs_1_
  60.8 11.1 %attention_forward.2 = (bf16[384,512]{1,0:T(8,128)(2,1)}, f32[2,1,1024]{2,1,0:T(1,128)}) custom-call(s32[4]{0:T(128)} %add_multiply_fusion.base_ref, s32[512,1]{1,0:T(8,128)} %copy.48.rows_ref, s32[1,512]{1,0:T(1,128)} %add_add_fusion.top_ref, s32[1,512]{1,0:T(1,128)} %bitcast.182, bf16[768,512]{1,0:T(8,128)(2,1)} %qkv_rotary.2.q_ref.refs_0_.refs_1_, ...), custom_call_target="tpu_custom_call" | custom-call | flops 12099999744 | bytes 11000000 | tf_op jit(solution)/shard_map/attention_forward/pallas_call | solution.py:230
  81.9 7.3 %collective-permute-done.6 = bf16[384,512]{1,0:T(8,128)(2,1)S(1)} collective-permute-done((bf16[384,512]{1,0:T(8,128)(2,1)S(1)}, bf16[384,512]{1,0:T(8,128)(2,1)S(1)}, u32[]{:S(2)}, u32[]{:S(2)}) %collective-permute-start.6) | collective-permute-done | bytes 393248 | tf_op jit(solution)/shard_map/ppermute | solution.py:58
  93.6 9.3 %collective-permute-done.8 = bf16[768,256]{1,0:T(8,128)(2,1)S(1)} collective-permute-done((bf16[768,256]{1,0:T(8,128)(2,1)S(1)}, bf16[768,256]{1,0:T(8,128)(2,1)S(1)}, u32[]{:S(2)}, u32[]{:S(2)}) %collective-permute-start.8) | collective-permute-done | bytes 393248 | tf_op jit(solution)/shard_map/ppermute | solution.py:58
  122.9 4.7 collective-permute-done.11
  136.2 8.4 %collective-permute-done.13 = bf16[128,1536]{1,0:T(8,128)(2,1)S(1)} collective-permute-done((bf16[128,1536]{1,0:T(8,128)(2,1)S(1)}, bf16[128,1536]{1,0:T(8,128)(2,1)S(1)}, u32[]{:S(2)}, u32[]{:S(2)}) %collective-permute-start.13) | collective-permute-done | bytes 393248 | tf_op jit(solution)/shard_map/ppermute | solution.py:58
  150.0 4.6 qkv_rotary.3.q_ref.refs_0_.refs_1_
  159.7 12.5 %collective-permute-done.18.refs_6_.refs_7_ = bf16[384,512]{1,0:T(8,128)(2,1)S(1)} collective-permute-done((bf16[384,512]{1,0:T(8,128)(2,1)S(1)}, bf16[384,512]{1,0:T(8,128)(2,1)S(1)}, u32[]{:S(2)}, u32[]{:S(2)}) %collective-permute-start.18) | collective-permute-done | bytes 393248 | tf_op jit(solution)/shard_map/ppermute | solution.py:110
  180.6 11.0 %attention_forward.3 = (bf16[384,512]{1,0:T(8,128)(2,1)}, f32[2,1,1024]{2,1,0:T(1,128)}) custom-call(s32[4]{0:T(128)} %add_multiply_fusion.base_ref, s32[512,1]{1,0:T(8,128)} %copy.48.rows_ref, s32[1,512]{1,0:T(1,128)} %add_add_fusion.top_ref, s32[1,512]{1,0:T(1,128)} %bitcast.183, bf16[768,512]{1,0:T(8,128)(2,1)} %qkv_rotary.3.q_ref.refs_0_.refs_1_, ...), custom_call_target="tpu_custom_call" | custom-call | flops 12099999744 | bytes 11000000 | tf_op jit(solution)/shard_map/attention_forward/pallas_call | solution.py:230
  200.7 6.1 collective-permute-done.22
  211.0 7.8 %collective-permute-done.24 = bf16[768,256]{1,0:T(8,128)(2,1)S(1)} collective-permute-done((bf16[768,256]{1,0:T(8,128)(2,1)S(1)}, bf16[768,256]{1,0:T(8,128)(2,1)S(1)}, u32[]{:S(2)}, u32[]{:S(2)}) %collective-permute-start.24) | collective-permute-done | bytes 393248 | tf_op jit(solution)/shard_map/ppermute | solution.py:58
  225.6 4.7 multiply_convert_fusion.3
  248.2 11.6 %collective-permute-done.27 = bf16[128,1536]{1,0:T(8,128)(2,1)S(1)} collective-permute-done((bf16[128,1536]{1,0:T(8,128)(2,1)}, bf16[128,1536]{1,0:T(8,128)(2,1)S(1)}, u32[]{:S(2)}, u32[]{:S(2)}) %collective-permute-start.27) | collective-permute-done | bytes 393248 | tf_op jit(solution)/shard_map/ppermute | solution.py:58
  267.9 6.7 collective-permute-done.41
  275.6 6.0 collective-permute-done.29
  293.3 16.4 %attention_backward.2 = (bf16[384,512]{1,0:T(8,128)(2,1)}, f32[2,192,512]{2,1,0:T(8,128)}, bf16[2,192,512]{2,1,0:T(8,128)(2,1)}, bf16[2,192,512]{2,1,0:T(8,128)(2,1)}, bf16[2,192,512]{2,1,0:T(8,128)(2,1)}) custom-call(s32[4]{0:T(128)} %add_multiply_fusion.base_ref, s32[512,1]{1,0:T(8,128)} %copy.48.rows_ref, s32[1,512]{1,0:T(1,128)} %add_add_fusion.top_ref, ...), custom_call_target="tpu_custom_call" | custom-call | flops 18150000640 | bytes 16500000 | tf_op jit(solution)/shard_map/attention_backward/pallas_call | solution.py:292
  323.2 11.4 %collective-permute-done.37 = bf16[128,2048]{1,0:T(8,128)(2,1)} collective-permute-done((bf16[128,2048]{1,0:T(8,128)(2,1)}, bf16[128,2048]{1,0:T(8,128)(2,1)}, u32[]{:S(2)}, u32[]{:S(2)}) %collective-permute-start.37) | collective-permute-done | bytes 524320 | tf_op jit(solution)/shard_map/ppermute | solution.py:58
  340.4 6.9 %collective-permute-done.38 = bf16[256,1024]{1,0:T(8,128)(2,1)} collective-permute-done((bf16[256,1024]{1,0:T(8,128)(2,1)S(1)}, bf16[256,1024]{1,0:T(8,128)(2,1)}, u32[]{:S(2)}, u32[]{:S(2)}) %collective-permute-start.38) | collective-permute-done | bytes 524320 | tf_op jit(solution)/shard_map/ppermute | solution.py:58
  377.1 7.0 %collective-permute-done.48 = bf16[768,256]{1,0:T(8,128)(2,1)S(1)} collective-permute-done((bf16[768,256]{1,0:T(8,128)(2,1)S(1)}, bf16[768,256]{1,0:T(8,128)(2,1)S(1)}, u32[]{:S(2)}, u32[]{:S(2)}) %collective-permute-start.48) | collective-permute-done | bytes 393248 | tf_op jit(solution)/shard_map/ppermute | solution.py:58
  387.6 5.7 multiply_convert_fusion.2
  404.7 7.7 %collective-permute-done.51 = bf16[256,768]{1,0:T(8,128)(2,1)S(1)} collective-permute-done((bf16[256,768]{1,0:T(8,128)(2,1)S(1)}, bf16[256,768]{1,0:T(8,128)(2,1)S(1)}, u32[]{:S(2)}, u32[]{:S(2)}) %collective-permute-start.51) | collective-permute-done | bytes 393248 | tf_op jit(solution)/shard_map/ppermute | solution.py:58
  413.4 6.5 collective-permute-done.54
  442.9 26.1 %reduce-scatter.9.cloned.1.call-done = bf16[192,1024]{1,0:T(8,128)(2,1)} async-done(((bf16[768,1024]{1,0:T(8,128)(2,1)}), bf16[192,1024]{1,0:T(8,128)(2,1)}) %reduce-scatter.9.cloned.1.call-update) | async-done | bytes 393232 | tf_op jit(solution)/shard_map/reduce_scatter | solution.py:125
  483.7 16.4 %attention_backward.3 = (bf16[384,512]{1,0:T(8,128)(2,1)}, f32[2,192,512]{2,1,0:T(8,128)}, bf16[2,192,512]{2,1,0:T(8,128)(2,1)}, bf16[2,192,512]{2,1,0:T(8,128)(2,1)}, bf16[2,192,512]{2,1,0:T(8,128)(2,1)}) custom-call(s32[4]{0:T(128)} %add_multiply_fusion.base_ref, s32[512,1]{1,0:T(8,128)} %copy.48.rows_ref, s32[1,512]{1,0:T(1,128)} %add_add_fusion.top_ref, ...), custom_call_target="tpu_custom_call" | custom-call | flops 18150000640 | bytes 16500000 | tf_op jit(solution)/shard_map/attention_backward/pallas_call | solution.py:292
  500.1 4.2 collective-permute-start.65
  519.2 6.5 collective-permute-start.64
  529.3 13.4 %collective-permute-done.64.two_ref = bf16[2,192,512]{2,1,0:T(8,128)(2,1)S(1)} collective-permute-done((bf16[2,192,512]{2,1,0:T(8,128)(2,1)S(1)}, bf16[2,192,512]{2,1,0:T(8,128)(2,1)S(1)}, u32[]{:S(2)}, u32[]{:S(2)}) %collective-permute-start.64) | collective-permute-done | bytes 393248 | tf_op jit(solution)/shard_map/ppermute | solution.py:118
  553.6 12.5 %collective-permute-start.84 = (f32[3,1536]{1,0:T(4,128)S(1)}, f32[3,1536]{1,0:T(4,128)S(1)}, u32[]{:S(2)}, u32[]{:S(2)}) collective-permute-start(f32[3,1536]{1,0:T(4,128)S(1)} %add.462), channel_id=1, source_target_pairs={{0,8},{4,12},{8,0},{12,4},{16,24},{20,28},{24,16},{28,20},{1,9},{5... | collective-permute-start | bytes 55304 | tf_op jit(solution)/shard_map/ppermute | solution.py:58
  576.1 4.9 collective-permute-done.70
  597.3 6.6 collective-permute-done.74
  603.9 7.6 %collective-permute-done.73 = bf16[256,768]{1,0:T(8,128)(2,1)} collective-permute-done((bf16[256,768]{1,0:T(8,128)(2,1)}, bf16[256,768]{1,0:T(8,128)(2,1)}, u32[]{:S(2)}, u32[]{:S(2)}) %collective-permute-start.73) | collective-permute-done | bytes 393248 | tf_op jit(solution)/shard_map/ppermute | solution.py:58
  644.1 22.8 %reduce-scatter.17.cloned.1.call-done = bf16[192,1152]{1,0:T(8,128)(2,1)} async-done(((bf16[768,1152]{1,0:T(8,128)(2,1)}), bf16[192,1152]{1,0:T(8,128)(2,1)}) %reduce-scatter.17.cloned.1.call-update) | async-done | bytes 442384 | tf_op jit(solution)/shard_map/reduce_scatter | solution.py:125
  (619 shorter events, 363.4 us)
Async XLA Ops:
  7.2 426.4 %reduce-scatter.7.cloned.1.call-start = ((), (), s32[]{:S(2)}) async-start(), calls=%async_computation.6 | async-start | bytes 3932160 | tf_op jit(solution)/shard_map/reduce_scatter | solution.py:125
  36.3 21.7 %collective-permute-start = (bf16[384,512]{1,0:T(8,128)(2,1)}, bf16[384,512]{1,0:T(8,128)(2,1)}, u32[]{:S(2)}, u32[]{:S(2)}) collective-permute-start(bf16[384,512]{1,0:T(8,128)(2,1)} %slice.397), channel_id=1, source_target_pairs={{0,4},{4,0},{8,12},{12,8},{16,20},{20,16},{24,28},{28,24},{1,5},{5... | collective-permute-start | bytes 1179656 | tf_op jit(solution)/shard_map/ppermute | solution.py:58
  39.3 21.4 %collective-permute-start.1 = (bf16[384,512]{1,0:T(8,128)(2,1)}, bf16[384,512]{1,0:T(8,128)(2,1)}, u32[]{:S(2)}, u32[]{:S(2)}) collective-permute-start(bf16[384,512]{1,0:T(8,128)(2,1)} %slice.397), channel_id=1, source_target_pairs={{8,16},{12,20},{24,0},{28,4},{9,17},{13,21},{25,1},{29,5},{10,18},... | collective-permute-start | bytes 1179656 | tf_op jit(solution)/shard_map/ppermute | solution.py:111
  52.6 19.3 %collective-permute-start.3 = (bf16[768,256]{1,0:T(8,128)(2,1)}, bf16[768,256]{1,0:T(8,128)(2,1)S(1)}, u32[]{:S(2)}, u32[]{:S(2)}) collective-permute-start(bf16[768,256]{1,0:T(8,128)(2,1)} %get-tuple-element.180), channel_id=1, source_target_pairs={{0,4},{4,0},{8,12},{12,8},{16,20},{20,16},{24,28},{28,24},{1,5},{5... | collective-permute-start | bytes 1179656 | tf_op jit(solution)/shard_map/ppermute | solution.py:58
  156.9 20.5 %collective-permute-start.16 = (bf16[384,512]{1,0:T(8,128)(2,1)S(1)}, bf16[384,512]{1,0:T(8,128)(2,1)S(1)}, u32[]{:S(2)}, u32[]{:S(2)}) collective-permute-start(bf16[384,512]{1,0:T(8,128)(2,1)S(1)} %slice.409), channel_id=1, source_target_pairs={{0,4},{4,0},{8,12},{12,8},{16,20},{20,16},{24,28},{28,24},{1,5},{5... | collective-permute-start | bytes 1179656 | tf_op jit(solution)/shard_map/ppermute | solution.py:58
  158.4 21.4 %collective-permute-start.17 = (bf16[384,512]{1,0:T(8,128)(2,1)S(1)}, bf16[384,512]{1,0:T(8,128)(2,1)S(1)}, u32[]{:S(2)}, u32[]{:S(2)}) collective-permute-start(bf16[384,512]{1,0:T(8,128)(2,1)S(1)} %slice.409), channel_id=1, source_target_pairs={{8,16},{12,20},{24,0},{28,4},{9,17},{13,21},{25,1},{29,5},{10,18},... | collective-permute-start | bytes 1179656 | tf_op jit(solution)/shard_map/ppermute | solution.py:111
  172.2 19.3 %collective-permute-start.19 = (bf16[768,256]{1,0:T(8,128)(2,1)S(1)}, bf16[768,256]{1,0:T(8,128)(2,1)}, u32[]{:S(2)}, u32[]{:S(2)}) collective-permute-start(bf16[768,256]{1,0:T(8,128)(2,1)S(1)} %copy-done.105), channel_id=1, source_target_pairs={{0,4},{4,0},{8,12},{12,8},{16,20},{20,16},{24,28},{28,24},{1,5},{5... | collective-permute-start | bytes 1179656 | tf_op jit(solution)/shard_map/ppermute | solution.py:58
  239.9 20.0 %collective-permute-start.40 = (bf16[128,1536]{1,0:T(8,128)(2,1)}, bf16[128,1536]{1,0:T(8,128)(2,1)}, u32[]{:S(2)}, u32[]{:S(2)}) collective-permute-start(bf16[128,1536]{1,0:T(8,128)(2,1)} %fusion.102), channel_id=1, source_target_pairs={{0,2},{1,3},{2,0},{3,1},{4,6},{5,7},{6,4},{7,5},{8,10},{9,11},{10,... | collective-permute-start | bytes 1179656 | tf_op jit(solution)/shard_map/ppermute | solution.py:58
  288.6 26.8 %collective-permute-start.33 = (bf16[768,256]{1,0:T(8,128)(2,1)}, bf16[768,256]{1,0:T(8,128)(2,1)}, u32[]{:S(2)}, u32[]{:S(2)}) collective-permute-start(bf16[768,256]{1,0:T(8,128)(2,1)} %get-tuple-element.220), channel_id=1, source_target_pairs={{0,4},{4,0},{8,12},{12,8},{16,20},{20,16},{24,28},{28,24},{1,5},{5... | collective-permute-start | bytes 1179656 | tf_op jit(solution)/shard_map/ppermute | solution.py:58
  289.6 25.8 %collective-permute-start.32 = (bf16[128,2048]{1,0:T(8,128)(2,1)}, bf16[128,2048]{1,0:T(8,128)(2,1)}, u32[]{:S(2)}, u32[]{:S(2)}) collective-permute-start(bf16[128,2048]{1,0:T(8,128)(2,1)} %get-tuple-element.218), channel_id=1, source_target_pairs={{0,4},{4,0},{8,12},{12,8},{16,20},{20,16},{24,28},{28,24},{1,5},{5... | collective-permute-start | bytes 1572872 | tf_op jit(solution)/shard_map/ppermute | solution.py:58
  312.3 23.2 %collective-permute-start.34 = (bf16[2,192,512]{2,1,0:T(8,128)(2,1)}, bf16[2,192,512]{2,1,0:T(8,128)(2,1)}, u32[]{:S(2)}, u32[]{:S(2)}) collective-permute-start(bf16[2,192,512]{2,1,0:T(8,128)(2,1)} %get-tuple-element.223), channel_id=1, source_target_pairs={{0,4},{4,0},{8,12},{12,8},{16,20},{20,16},{24,28},{28,24},{1,5},{5... | collective-permute-start | bytes 1179656 | tf_op jit(solution)/shard_map/ppermute | solution.py:58
  313.3 22.2 %collective-permute-start.35 = (bf16[2,192,512]{2,1,0:T(8,128)(2,1)}, bf16[2,192,512]{2,1,0:T(8,128)(2,1)}, u32[]{:S(2)}, u32[]{:S(2)}) collective-permute-start(bf16[2,192,512]{2,1,0:T(8,128)(2,1)} %get-tuple-element.224), channel_id=1, source_target_pairs={{0,24},{4,28},{16,8},{20,12},{1,25},{5,29},{17,9},{21,13},{2,26},{... | collective-permute-start | bytes 1179656 | tf_op jit(solution)/shard_map/ppermute | solution.py:118
  315.4 19.2 %collective-permute-start.37 = (bf16[128,2048]{1,0:T(8,128)(2,1)}, bf16[128,2048]{1,0:T(8,128)(2,1)}, u32[]{:S(2)}, u32[]{:S(2)}) collective-permute-start(bf16[128,2048]{1,0:T(8,128)(2,1)} %get-tuple-element.226), channel_id=1, source_target_pairs={{0,4},{4,0},{8,12},{12,8},{16,20},{20,16},{24,28},{28,24},{1,5},{5... | collective-permute-start | bytes 1572872 | tf_op jit(solution)/shard_map/ppermute | solution.py:58
  366.9 102.1 %reduce-scatter.9.cloned.1.call-start = ((), (), s32[]{:S(2)}) async-start(), calls=%async_computation.7 | async-start | bytes 1966080 | tf_op jit(solution)/shard_map/reduce_scatter | solution.py:125
  385.0 41.4 %collective-permute-start.56 = (bf16[768,256]{1,0:T(8,128)(2,1)}, bf16[768,256]{1,0:T(8,128)(2,1)}, u32[]{:S(2)}, u32[]{:S(2)}) collective-permute-start(bf16[768,256]{1,0:T(8,128)(2,1)} %copy-done.81), channel_id=1, source_target_pairs={{0,1},{1,0},{2,3},{3,2},{4,5},{5,4},{6,7},{7,6},{8,9},{9,8},{10,11... | collective-permute-start | bytes 1179656 | tf_op jit(solution)/shard_map/ppermute | solution.py:58
  386.4 38.4 %collective-permute-start.57 = (bf16[768,256]{1,0:T(8,128)(2,1)}, bf16[768,256]{1,0:T(8,128)(2,1)}, u32[]{:S(2)}, u32[]{:S(2)}) collective-permute-start(bf16[768,256]{1,0:T(8,128)(2,1)} %copy-done.77), channel_id=1, source_target_pairs={{0,1},{1,0},{2,3},{3,2},{4,5},{5,4},{6,7},{7,6},{8,9},{9,8},{10,11... | collective-permute-start | bytes 1179656 | tf_op jit(solution)/shard_map/ppermute | solution.py:58
  386.5 128.7 %reduce-scatter.11.cloned.1.call-start = ((), (), s32[]{:S(2)}) async-start(), calls=%async_computation.8 | async-start | bytes 2211840 | tf_op jit(solution)/shard_map/reduce_scatter | solution.py:125
  441.4 29.6 %collective-permute-start.59 = (bf16[128,2048]{1,0:T(8,128)(2,1)}, bf16[128,2048]{1,0:T(8,128)(2,1)S(1)}, u32[]{:S(2)}, u32[]{:S(2)}) collective-permute-start(bf16[128,2048]{1,0:T(8,128)(2,1)} %get-tuple-element.276), channel_id=1, source_target_pairs={{0,4},{4,0},{8,12},{12,8},{16,20},{20,16},{24,28},{28,24},{1,5},{5... | collective-permute-start | bytes 1572872 | tf_op jit(solution)/shard_map/ppermute | solution.py:58
  442.4 28.6 %collective-permute-start.58 = (bf16[128,1536]{1,0:T(8,128)(2,1)}, bf16[128,1536]{1,0:T(8,128)(2,1)S(1)}, u32[]{:S(2)}, u32[]{:S(2)}) collective-permute-start(bf16[128,1536]{1,0:T(8,128)(2,1)} %get-tuple-element.349), channel_id=1, source_target_pairs={{0,2},{1,3},{2,0},{3,1},{4,6},{5,7},{6,4},{7,5},{8,10},{9,11},{10,... | collective-permute-start | bytes 1179656 | tf_op jit(solution)/shard_map/ppermute | solution.py:58
  473.2 32.3 %collective-permute-start.66 = (bf16[768,256]{1,0:T(8,128)(2,1)}, bf16[768,256]{1,0:T(8,128)(2,1)}, u32[]{:S(2)}, u32[]{:S(2)}) collective-permute-start(bf16[768,256]{1,0:T(8,128)(2,1)} %collective-permute-done.19), channel_id=1, source_target_pairs={{0,1},{1,0},{2,3},{3,2},{4,5},{5,4},{6,7},{7,6},{8,9},{9,8},{10,11... | collective-permute-start | bytes 1179656 | tf_op jit(solution)/shard_map/ppermute | solution.py:58
  475.2 120.8 %reduce-scatter.13.cloned.1.call-start = ((), (), s32[]{:S(2)}) async-start(), calls=%async_computation.9 | async-start | bytes 3932160 | tf_op jit(solution)/shard_map/reduce_scatter | solution.py:125
  478.8 25.4 %collective-permute-start.62 = (bf16[128,2048]{1,0:T(8,128)(2,1)S(1)}, bf16[128,2048]{1,0:T(8,128)(2,1)S(1)}, u32[]{:S(2)}, u32[]{:S(2)}) collective-permute-start(bf16[128,2048]{1,0:T(8,128)(2,1)S(1)} %copy-done.68), channel_id=1, source_target_pairs={{0,4},{4,0},{8,12},{12,8},{16,20},{20,16},{24,28},{28,24},{1,5},{5... | collective-permute-start | bytes 1572872 | tf_op jit(solution)/shard_map/ppermute | solution.py:58
  480.3 24.0 %collective-permute-start.61 = (bf16[128,2048]{1,0:T(8,128)(2,1)S(1)}, bf16[128,2048]{1,0:T(8,128)(2,1)S(1)}, u32[]{:S(2)}, u32[]{:S(2)}) collective-permute-start(bf16[128,2048]{1,0:T(8,128)(2,1)S(1)} %copy-done.67), channel_id=1, source_target_pairs={{0,4},{4,0},{8,12},{12,8},{16,20},{20,16},{24,28},{28,24},{1,5},{5... | collective-permute-start | bytes 1572872 | tf_op jit(solution)/shard_map/ppermute | solution.py:58
  517.5 115.9 %reduce-scatter.15.cloned.1.call-start = ((), (), s32[]{:S(2)}) async-start(), calls=%async_computation.10 | async-start | bytes 1966080 | tf_op jit(solution)/shard_map/reduce_scatter | solution.py:125
  519.2 23.5 %collective-permute-start.64 = (bf16[2,192,512]{2,1,0:T(8,128)(2,1)S(1)}, bf16[2,192,512]{2,1,0:T(8,128)(2,1)S(1)}, u32[]{:S(2)}, u32[]{:S(2)}) collective-permute-start(bf16[2,192,512]{2,1,0:T(8,128)(2,1)S(1)} %copy-done.102), channel_id=1, source_target_pairs={{0,24},{4,28},{16,8},{20,12},{1,25},{5,29},{17,9},{21,13},{2,26},{... | collective-permute-start | bytes 1179656 | tf_op jit(solution)/shard_map/ppermute | solution.py:118
  525.7 24.0 %collective-permute-start.82 = (f32[3,1536]{1,0:T(4,128)S(1)}, f32[3,1536]{1,0:T(4,128)S(1)}, u32[]{:S(2)}, u32[]{:S(2)}) collective-permute-start(f32[3,1536]{1,0:T(4,128)S(1)} %fusion.186), channel_id=1, source_target_pairs={{0,2},{1,3},{2,0},{3,1},{4,6},{5,7},{6,4},{7,5},{8,10},{9,11},{10,... | collective-permute-start | bytes 55304 | tf_op jit(solution)/shard_map/ppermute | solution.py:58
  527.1 22.5 %collective-permute-start.67 = (bf16[768,256]{1,0:T(8,128)(2,1)S(1)}, bf16[768,256]{1,0:T(8,128)(2,1)}, u32[]{:S(2)}, u32[]{:S(2)}) collective-permute-start(bf16[768,256]{1,0:T(8,128)(2,1)S(1)} %copy-done.100), channel_id=1, source_target_pairs={{0,4},{4,0},{8,12},{12,8},{16,20},{20,16},{24,28},{28,24},{1,5},{5... | collective-permute-start | bytes 1179656 | tf_op jit(solution)/shard_map/ppermute | solution.py:58
  553.6 27.6 %collective-permute-start.84 = (f32[3,1536]{1,0:T(4,128)S(1)}, f32[3,1536]{1,0:T(4,128)S(1)}, u32[]{:S(2)}, u32[]{:S(2)}) collective-permute-start(f32[3,1536]{1,0:T(4,128)S(1)} %add.462), channel_id=1, source_target_pairs={{0,8},{4,12},{8,0},{12,4},{16,24},{20,28},{24,16},{28,20},{1,9},{5... | collective-permute-start | bytes 55304 | tf_op jit(solution)/shard_map/ppermute | solution.py:58
  581.0 85.9 %reduce-scatter.17.cloned.1.call-start = ((), (), s32[]{:S(2)}) async-start(), calls=%async_computation.11 | async-start | bytes 2211840 | tf_op jit(solution)/shard_map/reduce_scatter | solution.py:125
  581.1 30.4 %collective-permute-start.87 = (bf16[768,256]{1,0:T(8,128)(2,1)}, bf16[768,256]{1,0:T(8,128)(2,1)}, u32[]{:S(2)}, u32[]{:S(2)}) collective-permute-start(bf16[768,256]{1,0:T(8,128)(2,1)} %copy-done.96), channel_id=1, source_target_pairs={{0,1},{1,0},{2,3},{3,2},{4,5},{5,4},{6,7},{7,6},{8,9},{9,8},{10,11... | collective-permute-start | bytes 1179656 | tf_op jit(solution)/shard_map/ppermute | solution.py:58
  590.6 20.9 %collective-permute-start.72 = (bf16[128,1536]{1,0:T(8,128)(2,1)S(1)}, bf16[128,1536]{1,0:T(8,128)(2,1)}, u32[]{:S(2)}, u32[]{:S(2)}) collective-permute-start(bf16[128,1536]{1,0:T(8,128)(2,1)S(1)} %reduce-precision_convert_fusion), channel_id=1, source_target_pairs={{0,2},{1,3},{2,0},{3,1},{4,6},{5,7},{6,4},{7,5},{8,10},{9,11},{10,... | collective-permute-start | bytes 1179656 | tf_op jit(solution)/shard_map/ppermute | solution.py:58
  593.6 22.2 %collective-permute-start.76 = (f32[1,1536]{1,0:T(1,128)S(1)}, f32[1,1536]{1,0:T(1,128)S(1)}, u32[]{:S(2)}, u32[]{:S(2)}) collective-permute-start(f32[1,1536]{1,0:T(1,128)S(1)} %broadcast_in_dim.11), channel_id=1, source_target_pairs={{0,1},{1,0},{2,3},{3,2},{4,5},{5,4},{6,7},{7,6},{8,9},{9,8},{10,11... | collective-permute-start | bytes 18440 | tf_op jit(solution)/shard_map/ppermute | solution.py:58
  (191 other events, 1565.4 us)
Sparse Core Ops, SparseCore 0:
  367.0 63.7 reduce-scatter.6
  433.7 35.3 reduce-scatter.8
  475.3 39.0 reduce-scatter.10
  517.6 69.5 reduce-scatter.12
  590.1 37.0 reduce-scatter.14
  629.4 37.4 reduce-scatter.16

commit v3 on v2

v3 whole, which is shorter than its diff:
```python
import functools

import jax
import jax.numpy as jnp
from jax import lax
from jax.experimental import pallas as pl
from jax.experimental.pallas import tpu as pltpu
from jax.sharding import PartitionSpec as P

HD = 96
LAYERS = 2
STRETCHES = 4
EPS = 1e-05
BASE = 100000.0

BF = jnp.bfloat16
F32 = jnp.float32
NEG = -1e30
MIB = 2**20


def takes(us):
    return pl.CostEstimate(flops=int(us * 1.1e9), transcendentals=0, bytes_accessed=int(us * 1e6))


def mm(a, b, ca, cb):
    return lax.dot_general(a, b, (((ca,), (cb,)), ((), ())), preferred_element_type=F32)


def after(x, token):
    if token is None:
        return x
    return lax.optimization_barrier((x, token))[0]


def need(*values):
    return lax.optimization_barrier(values)


class Job:
    def __init__(self, make):
        self.make = make
        self.out = None
        self.raw = None


def window(start, end, jobs):
    if not jobs:
        return end
    for job in jobs:
        job.raw = job.make(start)
    leaves, tree = jax.tree.flatten((end, [job.raw for job in jobs]))
    end, outs = jax.tree.unflatten(tree, need(*leaves))
    for job, out in zip(jobs, outs):
        job.out = out
    return end


def swap(block, axis, mask):
    n = lax.axis_size(axis)
    return lax.ppermute(block, axis, [(i, i ^ mask) for i in range(n)])


def bf16_of(x):
    return lax.reduce_precision(x, 8, 7).astype(BF)


def gather_rows(own, jobs=()):
    beside = window(own, swap(own, "tensor", 2), jobs)
    pair = jnp.concatenate([own, beside], axis=0)
    return jnp.concatenate([pair, swap(pair, "tensor", 1)], axis=0)


def reduce_rows(keep, send, jobs=()):
    quarter = keep.shape[0] // 2
    got = swap(send, "tensor", 1)
    far = (keep[quarter:] + got[quarter:].astype(F32)).astype(BF)
    near = keep[:quarter] + got[:quarter].astype(F32)
    return near + window(far, swap(far, "tensor", 2), jobs).astype(F32)


RELATIVE = (0, 2, 1, 3)


def to_relative(rows, index):
    quarter = rows.shape[0] // 4
    return jnp.concatenate(
        [lax.dynamic_slice_in_dim(rows, (index ^ m) * quarter, quarter, 0) for m in RELATIVE], axis=0
    )


def to_absolute(rows, index):
    quarter = rows.shape[0] // 4
    parts = []
    for j in range(4):
        m = index ^ j
        place = ((m & 1) << 1) | (m >> 1)
        parts.append(lax.dynamic_slice_in_dim(rows, place * quarter, quarter, 0))
    return jnp.concatenate(parts, axis=0)


def in_stretches(pairs_of, n):
    pairs = []
    for i in range(n):
        offset = pairs_of((i + STRETCHES // 2) % STRETCHES)
        if offset is not None:
            pairs.append((i, (i + offset) % n))
    return pairs


def keys_onward(kv):
    n = lax.axis_size("dp")
    across = lax.ppermute(kv, "dp", in_stretches(lambda s: (3, 1, None, None)[s], n))
    behind = lax.ppermute(kv, "dp", in_stretches(lambda s: (2, 2, None, None)[s], n))
    return swap(kv, "dp", 1), behind, across


def keys_back(beside, behind, across):
    n = lax.axis_size("dp")
    late = [i for i in range(n) if (i + STRETCHES // 2) % STRETCHES >= 2]
    across = lax.ppermute(across, "dp", [(i, i ^ 1) for i in late])
    total = (behind.astype(F32) + across.astype(F32)).astype(BF)
    back = in_stretches(lambda s: (None, None, -2, -2)[s], n)
    return swap(beside, "dp", 1), lax.ppermute(total, "dp", back)


def scatter_grad(grad):
    n = lax.axis_size("dp")
    groups = [list(range(side, n, 2)) for side in range(2)]
    out = lax.psum_scatter(
        grad.astype(BF), "dp", scatter_dimension=0, tiled=True, axis_index_groups=groups
    )
    return out.astype(F32)


def sum_everywhere(x):
    x = x + swap(x, "tensor", 1)
    x = x + swap(x, "tensor", 2)
    n = lax.axis_size("dp")
    mask = 1
    while mask < n:
        x = x + swap(x, "dp", mask)
        mask *= 2
    return x


def turned_pair(top, low, cosine, sine):
    return top * cosine - low * sine, low * cosine + top * sine


def layer_block(w, l):
    return pl.BlockSpec((1, *w.shape[1:]), lambda *_: (l, 0, 0))


WHOLE = pl.BlockSpec(memory_space=pltpu.VMEM)


def rotated_rows(out_ref, t, heads, cosine, sine):
    half = HD // 2
    for h in range(heads):
        a = h * HD
        top, low = turned_pair(t[a : a + half], t[a + half : a + HD], cosine, sine)
        out_ref[a : a + half] = top.astype(out_ref.dtype)
        out_ref[a + half : a + HD] = low.astype(out_ref.dtype)


def qkv_kernel(heads, kv, x_ref, wq_ref, wk_ref, wv_ref, cos_ref, sin_ref, q_ref, kv_ref):
    x = x_ref[...]
    cosine, sine = cos_ref[...], sin_ref[...]
    rotated_rows(q_ref, mm(x, wq_ref[0], 1, 0).T, heads, cosine, sine)
    rotated_rows(kv_ref, mm(wk_ref[0], x, 1, 1), kv, cosine, sine)
    kv_ref[kv * HD :] = mm(wv_ref[0], x, 1, 1).astype(BF)


def qkv_call(x, weights, l, tables, heads, kv):
    rows = x.shape[0]
    whole = lambda v: pl.BlockSpec(v.shape, lambda i: (0,) * v.ndim)
    outs = [jax.ShapeDtypeStruct((count * HD, rows), BF) for count in (heads, 2 * kv)]
    return pl.pallas_call(
        functools.partial(qkv_kernel, heads, kv),
        grid=(1,),
        in_specs=[whole(x), *(layer_block(w, l) for w in weights), *(whole(v) for v in tables)],
        out_specs=[whole(v) for v in outs],
        out_shape=outs,
        compiler_params=pltpu.CompilerParams(vmem_limit_bytes=20 * MIB),
        name="qkv_rotary",
        cost_estimate=takes(4.5),
    )(x, *weights, *tables)


def mlp_kernel(x_ref, wg_ref, wu_ref, wd_ref, gate_ref, up_ref, act_ref, keep_ref, send_ref, acc_ref):
    j = pl.program_id(0)
    x = x_ref[...]
    gate, up = mm(x, wg_ref[0], 1, 0), mm(x, wu_ref[0], 1, 0)
    gate_ref[...] = gate
    up_ref[...] = up
    act = (jax.nn.silu(gate) * up).astype(BF)
    act_ref[...] = act
    part = mm(act, wd_ref[0], 1, 0)

    @pl.when(j == 0)
    def _():
        acc_ref[...] = part

    @pl.when(j > 0)
    def _():
        acc_ref[...] += part

    split_sum(j, acc_ref, keep_ref, send_ref)


def split_sum(j, acc_ref, keep_ref, send_ref):
    @pl.when(j == pl.num_programs(0) - 1)
    def _():
        half = keep_ref.shape[0]
        keep_ref[...] = acc_ref[:half]
        send_ref[...] = acc_ref[half:].astype(BF)


UNITS = 512


def mlp_specs(x, l):
    rows, width = x.shape
    whole = lambda shape: pl.BlockSpec(shape, lambda j: (0, 0))
    wide = pl.BlockSpec((1, width, UNITS), lambda j: (l, 0, j))
    tall = pl.BlockSpec((1, UNITS, width), lambda j: (l, j, 0))
    part = pl.BlockSpec((rows, UNITS), lambda j: (0, j))
    sums = [whole((rows // 2, width))] * 2
    sum_shapes = [jax.ShapeDtypeStruct((rows // 2, width), F32), jax.ShapeDtypeStruct((rows // 2, width), BF)]
    return whole((rows, width)), wide, tall, part, sums, sum_shapes


def mlp_call(x, w_gate, w_up, w_down, l):
    whole, wide, tall, part, sums, sum_shapes = mlp_specs(x, l)
    shape = (x.shape[0], w_gate.shape[2])
    return pl.pallas_call(
        mlp_kernel,
        grid=(w_gate.shape[2] // UNITS,),
        in_specs=[whole, wide, wide, tall],
        out_specs=[part, part, part, *sums],
        out_shape=[jax.ShapeDtypeStruct(shape, d) for d in (F32, F32, BF)] + sum_shapes,
        scratch_shapes=[pltpu.VMEM(x.shape, F32)],
        compiler_params=pltpu.CompilerParams(vmem_limit_bytes=30 * MIB),
        name="feed_forward",
        cost_estimate=takes(8),
    )(x, w_gate, w_up, w_down)


def mlp_back_kernel(x_ref, wd_ref, wg_ref, wu_ref, gate_ref, up_ref, gg_ref, ug_ref, keep_ref, send_ref, acc_ref):
    j = pl.program_id(0)
    hidden = mm(x_ref[...], wd_ref[0], 1, 1)
    gate = gate_ref[...]
    sig = jax.nn.sigmoid(gate)
    gg = (hidden * up_ref[...] * sig * (1.0 + gate * (1.0 - sig))).astype(BF)
    ug = (hidden * gate * sig).astype(BF)
    gg_ref[...] = gg
    ug_ref[...] = ug
    part = mm(gg, wg_ref[0], 1, 1) + mm(ug, wu_ref[0], 1, 1)

    @pl.when(j == 0)
    def _():
        acc_ref[...] = part

    @pl.when(j > 0)
    def _():
        acc_ref[...] += part

    split_sum(j, acc_ref, keep_ref, send_ref)


def mlp_back_call(x, w_down, w_gate, w_up, gate, up, l):
    whole, wide, tall, part, sums, sum_shapes = mlp_specs(x, l)
    return pl.pallas_call(
        mlp_back_kernel,
        grid=(w_gate.shape[2] // UNITS,),
        in_specs=[whole, tall, wide, wide, part, part],
        out_specs=[part, part, *sums],
        out_shape=[jax.ShapeDtypeStruct(gate.shape, BF)] * 2 + sum_shapes,
        scratch_shapes=[pltpu.VMEM(x.shape, F32)],
        compiler_params=pltpu.CompilerParams(vmem_limit_bytes=30 * MIB),
        name="feed_forward_back",
        cost_estimate=takes(9),
    )(x, w_down, w_gate, w_up, gate, up)


def both_heads(block):
    return jnp.concatenate([block[:HD], block[HD:]], axis=1)


def flip(block):
    return block.astype(F32).T.astype(BF)


LOG2E = 1.4426950408889634


def fill_bias(base_ref, rows_ref, top_ref, start_ref, bias_ref):
    @pl.when(pl.program_id(0) == 0)
    def _():
        for b in range(4):
            place = rows_ref[...] + base_ref[b]
            allowed = (place >= start_ref[...]) & (place <= top_ref[...])
            bias_ref[b] = jnp.where(allowed, 0.0, NEG)


def scores_of(key, qt, bias):
    return mm(flip(key), qt, 1, 0) * (HD ** (-0.5) * LOG2E) + jnp.concatenate([bias, bias], axis=1)


def attn_fwd_kernel(base_ref, rows_ref, top_ref, start_ref, q_ref, *refs):
    keys, values = refs[0:8:2], refs[1:8:2]
    mixed_t_ref, log_ref, s_ref, bias_ref = refs[8:]
    fill_bias(base_ref, rows_ref, top_ref, start_ref, bias_ref)
    qt = both_heads(q_ref[...])
    top = jnp.full((1, qt.shape[1]), NEG, F32)
    for b in range(4):
        scores = scores_of(keys[b][...], qt, bias_ref[b])
        s_ref[b] = scores
        top = jnp.maximum(top, jnp.max(scores, axis=0, keepdims=True))
    total = jnp.zeros_like(top)
    acc = jnp.zeros((HD, qt.shape[1]), F32)
    for b in range(4):
        weight = jnp.exp2(s_ref[b] - top)
        total = total + jnp.sum(weight, axis=0, keepdims=True)
        acc = acc + mm(values[b][...], weight.astype(BF), 1, 0)
    acc = acc / total
    log_ref[0] = top + jnp.log(total) * LOG2E
    half = qt.shape[1] // 2
    mixed_t_ref[:HD] = acc[:, :half].astype(BF)
    mixed_t_ref[HD:] = acc[:, half:].astype(BF)


def attn_specs(rows, kv):
    q_spec = pl.BlockSpec((2 * HD, rows), lambda g: (g, 0))
    far_k = pl.BlockSpec((HD, rows), lambda g: (g, 0))
    far_v = pl.BlockSpec((HD, rows), lambda g: (kv + g, 0))
    whole = lambda shape: pl.BlockSpec(shape, lambda g: (0,) * len(shape))
    places = [
        pl.BlockSpec(memory_space=pltpu.SMEM),
        whole((rows, 1)),
        whole((1, rows)),
        whole((1, rows)),
    ]
    return places, q_spec, [far_k, far_v] * 4


def attn_fwd(q_t, blocks, places, kv):
    rows = q_t.shape[1]
    place_specs, q_spec, kv_specs = attn_specs(rows, kv)
    operands = [block for block in blocks for _ in range(2)]
    mixed_t, log_total = pl.pallas_call(
        attn_fwd_kernel,
        grid=(kv,),
        in_specs=place_specs + [q_spec] + kv_specs,
        out_specs=[
            pl.BlockSpec((2 * HD, rows), lambda g: (g, 0)),
            pl.BlockSpec((1, 1, 2 * rows), lambda g: (g, 0, 0)),
        ],
        out_shape=[
            jax.ShapeDtypeStruct((2 * kv * HD, rows), BF),
            jax.ShapeDtypeStruct((kv, 1, 2 * rows), F32),
        ],
        scratch_shapes=[pltpu.VMEM((4, rows, 2 * rows), F32), pltpu.VMEM((4, rows, rows), F32)],
        compiler_params=pltpu.CompilerParams(vmem_limit_bytes=24 * MIB),
        name="attention_forward",
        cost_estimate=takes(11),
    )(*places, q_t, *operands)
    return mixed_t, log_total


def attn_bwd_kernel(base_ref, rows_ref, top_ref, start_ref, cos_ref, sin_ref, q_ref, *refs):
    keys, values = refs[0:8:2], refs[1:8:2]
    log_ref, mixed_ref, grad_ref = refs[8:11]
    dq_ref, own_ref, bias_ref = refs[11], refs[12], refs[16]
    far_refs = refs[13:16]
    fill_bias(base_ref, rows_ref, top_ref, start_ref, bias_ref)
    qt = both_heads(q_ref[...])
    grad_t = both_heads(grad_ref[...])
    q_rows, grad_rows = flip(qt), flip(grad_t)
    log_total = log_ref[0]
    centre = jnp.sum(
        grad_t.astype(F32) * both_heads(mixed_ref[...]).astype(F32), axis=0, keepdims=True
    )
    dq = jnp.zeros((HD, qt.shape[1]), F32)
    for b in range(4):
        probs = jnp.exp2(scores_of(keys[b][...], qt, bias_ref[b]) - log_total)
        prob_grad = mm(flip(values[b][...]), grad_t, 1, 0)
        score_grad = (probs * (prob_grad - centre)).astype(BF)
        dq = dq + mm(keys[b][...], score_grad, 1, 0)
        dv = mm(probs.astype(BF), grad_rows, 1, 0).T
        dk = mm(score_grad, q_rows, 1, 0).T * HD ** (-0.5)
        out = own_ref if b == 0 else far_refs[b - 1]
        out[0] = dk.astype(out.dtype)
        out[1] = dv.astype(out.dtype)
    dq = dq * HD ** (-0.5)
    half, rows = HD // 2, qt.shape[1] // 2
    cosine, sine = cos_ref[...], sin_ref[...]
    for h in range(2):
        part = dq[:, h * rows : (h + 1) * rows]
        top, low = turned_pair(part[:half], part[half:], cosine, -sine)
        dq_ref[h * HD : h * HD + half] = top.astype(BF)
        dq_ref[h * HD + half : (h + 1) * HD] = low.astype(BF)


def attn_bwd(q_t, blocks, places, kv, tables, log_total, mixed_t, grad_t):
    rows = q_t.shape[1]
    place_specs, q_spec, kv_specs = attn_specs(rows, kv)
    operands = [block for block in blocks for _ in range(2)]
    table = pl.BlockSpec((HD // 2, rows), lambda g: (0, 0))
    two = pl.BlockSpec((2 * HD, rows), lambda g: (g, 0))
    pair = pl.BlockSpec((2, HD, rows), lambda g: (0, g, 0))
    outs = pl.pallas_call(
        attn_bwd_kernel,
        grid=(kv,),
        in_specs=place_specs
        + [table, table, q_spec]
        + kv_specs
        + [pl.BlockSpec((1, 1, 2 * rows), lambda g: (g, 0, 0)), two, two],
        out_specs=[two, pair, pair, pair, pair],
        out_shape=[jax.ShapeDtypeStruct((2 * kv * HD, rows), BF)]
        + [jax.ShapeDtypeStruct((2, kv * HD, rows), F32)]
        + [jax.ShapeDtypeStruct((2, kv * HD, rows), BF)] * 3,
        scratch_shapes=[pltpu.VMEM((4, rows, rows), F32)],
        compiler_params=pltpu.CompilerParams(vmem_limit_bytes=24 * MIB),
        name="attention_backward",
        cost_estimate=takes(16.5),
    )(*places, *tables, q_t, *operands, log_total, mixed_t, grad_t)
    return outs


def join_kernel(
    kv, dq_ref, own_ref, one_ref, two_ref, cos_ref, sin_ref, wq_ref, wk_ref, wv_ref, *refs
):
    out_ref, keep_ref, send_ref, t_ref = refs
    wide = dq_ref.shape[0]
    cosine, sine = cos_ref[...], sin_ref[...]
    t_ref[:wide] = dq_ref[...].astype(F32)
    total = lambda i: own_ref[i] + sum(r[i].astype(F32) for r in (one_ref, two_ref))
    rotated_rows(t_ref.at[wide : wide + kv * HD], total(0), kv, cosine, -sine)
    t_ref[wide + kv * HD :] = total(1)
    out_ref[...] = t_ref[...].T.astype(BF)
    half = keep_ref.shape[0]
    parts = [
        (out_ref[:, :wide], wq_ref[0], 1),
        (t_ref[wide : wide + kv * HD].T.astype(BF), wk_ref[0], 0),
        (t_ref[wide + kv * HD :].T.astype(BF), wv_ref[0], 0),
    ]
    send_ref[...] = sum(mm(g[half:], w, 1, c) for g, w, c in parts).astype(BF)
    keep_ref[...] = sum(mm(g[:half], w, 1, c) for g, w, c in parts)


def join_call(dq, own, far, tables, weights, l, kv):
    rows = dq.shape[1]
    cols = dq.shape[0] + 2 * kv * HD
    width = weights[0].shape[1]
    whole = lambda v: pl.BlockSpec(v.shape, lambda i: (0,) * len(v.shape))
    outs = [
        jax.ShapeDtypeStruct((rows, cols), BF),
        jax.ShapeDtypeStruct((rows // 2, width), F32),
        jax.ShapeDtypeStruct((rows // 2, width), BF),
    ]
    given = (dq, own, *far, *tables)
    return pl.pallas_call(
        functools.partial(join_kernel, kv),
        grid=(1,),
        in_specs=[whole(v) for v in given] + [layer_block(w, l) for w in weights],
        out_specs=[whole(v) for v in outs],
        out_shape=outs,
        scratch_shapes=[pltpu.VMEM((cols, rows), F32)],
        compiler_params=pltpu.CompilerParams(vmem_limit_bytes=24 * MIB),
        name="join_gradients",
        cost_estimate=takes(5),
    )(*given, *weights)


def turned_halves(x, n):
    side = lax.axis_index("dp") % 2
    rows, cols = x.shape
    r, half = cols // n, cols // 2

    def kernel(side_ref, x_ref, mine_ref, other_ref, t_ref):
        t_ref[...] = x_ref[...].astype(F32).T.astype(BF)
        for odd in range(2):

            @pl.when(side_ref[0] == odd)
            def _():
                for b in range(n):
                    to = slice(b // 2 * r, (b // 2 + 1) * r)
                    block = t_ref[b * r : (b + 1) * r]
                    if b % 2 == odd:
                        mine_ref[to] = block
                    else:
                        other_ref[to] = block[:, : rows // 2]

    whole = pl.BlockSpec(memory_space=pltpu.VMEM)
    return pl.pallas_call(
        kernel,
        in_specs=[pl.BlockSpec(memory_space=pltpu.SMEM), whole],
        out_specs=[whole, whole],
        out_shape=[jax.ShapeDtypeStruct((half, rows), BF), jax.ShapeDtypeStruct((half, rows // 2), BF)],
        scratch_shapes=[pltpu.VMEM((cols, rows), BF)],
        compiler_params=pltpu.CompilerParams(vmem_limit_bytes=12 * MIB),
        name="turned_halves",
        cost_estimate=takes(3),
    )(side[None].astype(jnp.int32), x)


class Turned:
    def __init__(self, read, n):
        self.turn = Job(lambda token: turned_halves(after(read(), token), n))
        self.send = Job(lambda token: swap(after(self.turn.out[1], token), "dp", 1))
        self.whole = None

    def parts(self):
        if self.whole is None:
            got = self.send.out
            self.whole = jnp.concatenate([got, swap(got, "tensor", 1)], axis=1)
        return self.turn.out[0], self.whole


class Sent:
    def __init__(self, read, chunks):
        self.read = read
        self.sends = [self.chunk(i, chunks) for i in range(chunks)]

    def chunk(self, i, chunks):
        def make(token):
            x = self.read()
            rows = x.shape[0] // chunks
            return swap(after(x[i * rows : (i + 1) * rows], token), "dp", 1)

        return Job(make)

    def parts(self):
        got = [job.out for job in self.sends]
        return self.read(), got[0] if len(got) == 1 else jnp.concatenate(got, axis=0)


def product(left, right, cb=0):
    def make(token):
        (a, b), (c, d) = left.parts(), right.parts()
        return (mm(a, after(c, token), 1, cb) + mm(b, after(d, token), 1, cb)).astype(BF)

    return Job(make)


def joined(*products):
    def make(token):
        return jnp.concatenate([p.make(token) if p.raw is None else p.raw for p in products], axis=1)

    return Job(make)


def scatter(before, grad):
    return Job(lambda token: scatter_grad(after(grad.raw, None if before is None else before.raw)))


def inverse_rms(x):
    return lax.rsqrt(jnp.mean(x * x, axis=1, keepdims=True) + EPS)


def norm_back(x, inverse, gain, grad, incoming):
    normalized = x * inverse
    scaled = grad * gain
    gain_grad = jnp.sum(grad * normalized, axis=0)
    out = incoming + inverse * (
        scaled - normalized * jnp.mean(scaled * normalized, axis=1, keepdims=True)
    )
    return out, gain_grad


def shards(
    hidden_in,
    doc_lengths,
    norm_attn,
    norm_mlp,
    w_query,
    w_key,
    w_value,
    w_out,
    w_gate,
    w_up,
    w_down,
    cotangent,
):
    rows = hidden_in.shape[0]
    n = lax.axis_size("dp")
    quarter = rows // 4
    pair = rows // 2
    t = lax.axis_index("tensor")
    kv = w_key.shape[2] // HD
    heads = w_query.shape[2] // HD
    seq_count = n // STRETCHES
    shifted = lax.axis_index("dp") + STRETCHES // 2
    stretch = shifted % STRETCHES
    lengths = lax.dynamic_index_in_dim(doc_lengths, shifted // STRETCHES % seq_count, 0, keepdims=False)
    local = jnp.concatenate([(t ^ m) * quarter + jnp.arange(quarter, dtype=jnp.int32) for m in RELATIVE])
    place = stretch * rows + local
    ends = jnp.cumsum(lengths)
    passed = (place[:, None] >= ends[None, :]).astype(jnp.int32)
    start = jnp.sum(passed * lengths[None, :], axis=1)
    frequency = BASE ** (-(jnp.arange(HD // 2, dtype=F32) * 2.0 / HD))
    angles = frequency[:, None] * (place - start).astype(F32)[None, :]
    tables = (jnp.cos(angles), jnp.sin(angles))
    bases = jnp.stack([stretch, stretch ^ 1, stretch - 2, (stretch ^ 1) - 2]) * rows
    places = (bases.astype(jnp.int32), local[:, None], place[None, :], start[None, :])

    w_qkv = (w_query, jnp.swapaxes(w_key, 1, 2), jnp.swapaxes(w_value, 1, 2))

    def own_rows(x):
        return lax.dynamic_slice_in_dim(x, t * quarter, quarter, 0)

    value = {}

    def later(name, l):
        return lambda: value[name, l]

    layers = range(LAYERS)
    down_left = [Turned(later("down_in", l), n) for l in layers]
    attn_left = [Turned(later("normed", l), n) for l in layers]
    mlp_left = [Turned(later("normed_mlp", l), n) for l in layers]
    out_left = [Turned(later("out_in", l), n) for l in layers]
    act_right = [Sent(later("act", l), 2) for l in layers]
    mixed_right = [Sent(later("mixed", l), 1) for l in layers]
    gate_right = [Sent(later("gate", l), 2) for l in layers]
    up_right = [Sent(later("up", l), 2) for l in layers]
    qkv_right = [Sent(later("d_qkv", l), 2) for l in layers]
    g_down = [product(down_left[l], act_right[l]) for l in layers]
    g_gate = [product(mlp_left[l], gate_right[l]) for l in layers]
    g_up = [product(mlp_left[l], up_right[l]) for l in layers]
    g_out = [product(out_left[l], mixed_right[l], 1) for l in layers]
    g_qkv = [product(attn_left[l], qkv_right[l]) for l in layers]
    g_both = joined(g_gate[0], g_up[0])
    g_more = joined(g_up[1], g_down[1])
    g_attn = [joined(g_out[l], g_qkv[l]) for l in layers]
    s_gate = scatter(None, g_gate[1])
    s_more = scatter(s_gate, g_more)
    s_attn = [None, scatter(s_more, g_attn[1])]
    s_both = scatter(s_attn[1], g_both)
    s_down = scatter(s_both, g_down[0])
    s_attn[0] = scatter(s_down, g_attn[0])
    plan = {
        ("keys", 0): [down_left[1].turn],
        ("attn", 0): [down_left[1].send],
        ("sum1", 0): [attn_left[0].turn, *mixed_right[0].sends],
        ("all1", 0): [attn_left[0].send],
        ("sum2", 0): [act_right[0].sends[0], mlp_left[0].turn],
        ("all2", 0): [act_right[0].sends[1]],
        ("attn", 1): [mlp_left[0].send],
        ("sum1", 1): [attn_left[1].turn, *mixed_right[1].sends],
        ("all1", 1): [attn_left[1].send],
        ("back_sum1", 1): [gate_right[1].sends[0], mlp_left[1].turn],
        ("back_all1", 1): [gate_right[1].sends[1]],
        ("back_attn", 1): [mlp_left[1].send, up_right[1].sends[0]],
        ("back_keys", 1): [up_right[1].sends[1], out_left[1].turn, g_gate[1]],
        ("back_join", 1): [act_right[1].sends[0]],
        ("back_sum2", 1): [act_right[1].sends[1], g_up[1]],
        ("back_all2", 1): [out_left[1].send, g_more],
        ("back_mlp", 0): [qkv_right[1].sends[0], s_gate],
        ("back_sum1", 0): [qkv_right[1].sends[1], gate_right[0].sends[0], down_left[0].turn],
        ("back_all1", 0): [gate_right[0].sends[1], g_attn[1], s_more],
        ("back_attn", 0): [*up_right[0].sends],
        ("back_keys", 0): [g_both, out_left[0].turn, s_attn[1]],
        ("back_join", 0): [down_left[0].send],
        ("back_sum2", 0): [out_left[0].send, qkv_right[0].sends[0], g_down[0], s_both],
        ("back_all2", 0): [qkv_right[0].sends[1]],
    }
    jobs = lambda name, l: plan.get((name, l), [])

    value["down_in", LAYERS - 1] = to_relative(cotangent.astype(BF), t)
    flow = own_rows(hidden_in)
    inverse = inverse_rms(flow)
    normed_all = to_relative((hidden_in * inverse_rms(hidden_in) * norm_attn[0]).astype(BF), t)
    records = []
    for l in layers:
        value["normed", l] = normed_all
        q_t, kv_t = qkv_call(normed_all, w_qkv, l, tables, heads, kv)
        beside, behind, across = keys_onward(kv_t)
        across = window(kv_t, across, jobs("keys", l))
        blocks = (kv_t, beside, behind, across)
        mixed_t, log_total = attn_fwd(q_t, blocks, places, kv)
        mixed_t = value["mixed", l] = window(across, mixed_t, jobs("attn", l))
        send = mm(mixed_t[:, pair:], w_out[l], 0, 0).astype(BF)
        keep = mm(mixed_t[:, :pair], w_out[l], 0, 0)
        middle = flow + reduce_rows(keep, send, jobs("sum1", l))
        inverse_mlp = inverse_rms(middle)
        normed_mlp = gather_rows((middle * inverse_mlp * norm_mlp[l]).astype(BF), jobs("all1", l))
        value["normed_mlp", l] = normed_mlp
        gate, up, value["act", l], keep, send = mlp_call(normed_mlp, w_gate, w_up, w_down, l)
        send = window(normed_mlp, send, jobs("mlp", l))
        records.append((flow, inverse, q_t, blocks, log_total, middle, inverse_mlp, gate, up))
        if l + 1 < LAYERS:
            flow = middle + reduce_rows(keep, send, jobs("sum2", l))
            inverse = inverse_rms(flow)
            normed_all = gather_rows((flow * inverse * norm_attn[l + 1]).astype(BF), jobs("all2", l))

    def output_of(token):
        out = bf16_of(middle_last + reduce_rows(keep_last, after(send_last, token)))
        return to_absolute(gather_rows(out), t).astype(F32)

    middle_last, keep_last, send_last = middle, keep, send

    flow = own_rows(cotangent)
    gains = [None] * LAYERS
    for l in reversed(layers):
        before, inverse, q_t, blocks, log_total, middle, inverse_mlp, gate, up = records[l]
        down_in = value["down_in", l]
        gate_grad, up_grad, keep, send = mlp_back_call(down_in, w_down, w_gate, w_up, gate, up, l)
        value["gate", l], value["up", l] = gate_grad, up_grad
        send = window(down_in, send, jobs("back_mlp", l))
        total = reduce_rows(keep, send, jobs("back_sum1", l))
        flow, gain_mlp = norm_back(middle, inverse_mlp, norm_mlp[l], total, flow)
        out_in = value["out_in", l] = gather_rows(flow.astype(BF), jobs("back_all1", l))
        grad_t = mm(w_out[l], out_in, 1, 1).astype(BF)
        dq, own, *d_far = attn_bwd(q_t, blocks, places, kv, tables, log_total, value["mixed", l], grad_t)
        dq, d_far = window(out_in, (dq, d_far), jobs("back_attn", l))
        d_far = keys_back(*d_far)
        d_far = (d_far[0], window(dq, d_far[1], jobs("back_keys", l)))
        d_qkv, keep, send = join_call(dq, own, d_far, tables, w_qkv, l, kv)
        value["d_qkv", l] = d_qkv
        send = window(d_far[1], send, jobs("back_join", l))
        if l + 1 == LAYERS:
            send, hidden_out = need(send, output_of(out_in))
        total = reduce_rows(keep, send, jobs("back_sum2", l))
        flow, gain_attn = norm_back(before, inverse, norm_attn[l], total, flow)
        gains[l] = (gain_attn, gain_mlp)
        if l > 0:
            value["down_in", l - 1] = gather_rows(flow.astype(BF), jobs("back_all2", l))
    final = gather_rows(bf16_of(flow), jobs("back_all2", 0))
    for job in (s_down, g_attn[0], s_attn[0]):
        job.out = job.raw = job.make(None)
    input_grad = to_absolute(final, t).astype(F32)

    gain_grads = jnp.stack([gains[0][0], gains[1][0], gains[0][1], gains[1][1]])
    gain_grads = sum_everywhere(after(gain_grads, g_attn[0].raw))
    width = gain_grads.shape[1] // n
    gain_grads = lax.dynamic_slice_in_dim(gain_grads, lax.axis_index("dp") * width, width, 1)
    norm_attn_grad, norm_mlp_grad = gain_grads[:LAYERS], gain_grads[LAYERS:]

    def stack(parts, turn=False):
        return jnp.stack([p.T if turn else p for p in parts])

    units = w_gate.shape[2]
    a, b, c = heads * HD, 2 * heads * HD, (2 * heads + kv) * HD
    early = (
        hidden_out,
        input_grad,
        norm_attn_grad,
        norm_mlp_grad,
        stack([s_both.out[:, :units], s_gate.out]),
        stack([s_both.out[:, units:], s_more.out[:, :units]]),
        stack([s_down.out, s_more.out[:, units:]], True),
    )
    *early, s_attn[0].out = need(*early, s_attn[0].out)
    attn = lambda start, stop: [job.out[:, start:stop] for job in s_attn]
    return (
        *early[:4],
        stack(attn(a, b)),
        stack(attn(b, c)),
        stack(attn(c, None)),
        stack(attn(0, a), True),
        *early[4:],
    )


def solution(mesh):
    placed = (
        P("dp", None),
        P(),
        P(),
        P(),
        P(None, None, "tensor"),
        P(None, None, "tensor"),
        P(None, None, "tensor"),
        P(None, "tensor", None),
        P(None, None, "tensor"),
        P(None, None, "tensor"),
        P(None, "tensor", None),
        P("dp", None),
    )
    return jax.shard_map(
        shards,
        mesh=mesh,
        in_specs=placed,
        out_specs=(
            P("dp", None),
            P("dp", None),
            P(None, "dp"),
            P(None, "dp"),
            P(None, "dp", "tensor"),
            P(None, "dp", "tensor"),
            P(None, "dp", "tensor"),
            P(None, "tensor", "dp"),
            P(None, "dp", "tensor"),
            P(None, "dp", "tensor"),
            P(None, "tensor", "dp"),
        ),
        check_vma=False,
    )
```

time: 686 us -> 639 us (0.931)
  matrix products: 86.4 us -> 31.4 us
  other arithmetic: 93.8 us -> 65 us
  local copies, waits for them, and re-layouts: 33.7 us -> 62 us
  waiting for transfers between devices: 257 us -> 274 us
  starting transfers between devices: 95.9 us -> 86 us
    dot_general x44 -> x26, matrix products: 86.4 us -> 31.4 us  [mm(): lax.dot_general(a, b, (((ca,), (cb,)), ((), ())), preferred_element_type=...]
    unnamed x260 -> x286, local copies, waits for them, and re-layouts: 15.7 us -> 51 us
    reduce_scatter x6 -> x4, waiting for transfers between devices: 49 us -> 17.7 us  [scatter_grad(): lax.psum_scatter(grad.astype(BF), 'dp', scatter_dimension=0, tiled=True,...]
    pallas_call x4 -> x8, Pallas kernels: 15.5 us -> 42.1 us  [the longest x2 16.4 us: mlp_back_call(): pl.pallas_call(mlp_back_kernel, grid=(w_gate.shape[2] // UNITS,), in_spec...]
    pallas_call x8, Pallas kernels: 25.4 us -> 6.87 us  [turned_halves(): pl.pallas_call(kernel, in_specs=[pl.BlockSpec(memory_space=pltpu.SMEM), w...]
    ppermute x80 -> x75, waiting for transfers between devices: 173 us -> 190 us  [swap(): return lax.ppermute(block, axis, [(i, i ^ mask) for i in range(n)])]
    ppermute x4, waiting for transfers between devices: 14.5 us -> 29.3 us  [the longest x2 15.6 us: keys_back(): across = lax.ppermute(across, 'dp', [(i, i ^ 1) for i in late])]
    unnamed x6 -> x8, waiting for transfers between devices: 0.1 us -> 11.4 us
  transfers between devices with their start and end apart: 94 -> 89, of which waited for: 48 -> 54; matrix products, arithmetic and copies ran while one was open for 21% -> 15% of each run, Pallas kernels for 13% -> 10%
where the time goes in v3:
time: 639 us; the launch traced here: 629 us
  waiting for transfers between devices  274 us (43%)
  Pallas kernels  94.3 us (15%)
  starting transfers between devices  86 us (13%)
  other arithmetic  65 us (10%)
  local copies, waits for them, and re-layouts  62 us (10%)
  matrix products  31.4 us (5%)
  between operations  16.6 us (3%)
    ppermute x75, waiting for transfers between devices, swap(): return lax.ppermute(block, axis, [(i, i ^ mask) for i in range(n)])  190 us
    ppermute x75, starting transfers between devices, swap(): return lax.ppermute(block, axis, [(i, i ^ mask) for i in range(n)])  69.5 us
    unnamed x286, local copies, waits for them, and re-layouts  51 us
    dot_general x26, matrix products, mm(): lax.dot_general(a, b, (((ca,), (cb,)), ((), ())), preferred_element_type=...  31.4 us
    pallas_call x2, Pallas kernels, attn_bwd(): pl.pallas_call(attn_bwd_kernel, grid=(kv,), in_specs=place_specs + [table...  27.8 us
    ppermute x2, waiting for transfers between devices, keys_onward(): lax.ppermute(kv, 'dp', in_stretches(lambda s: (3, 1, None, None)[s], n))  20.9 us
    reduce_scatter x4, waiting for transfers between devices, scatter_grad(): lax.psum_scatter(grad.astype(BF), 'dp', scatter_dimension=0, tiled=True,...  17.7 us
    pallas_call x2, Pallas kernels, attn_fwd(): pl.pallas_call(attn_fwd_kernel, grid=(kv,), in_specs=place_specs + [q_spe...  17.5 us
  transfers between devices with their start and end apart: 89, of which 54 were waited for; matrix products, arithmetic and copies ran while one was open for 15% of the time, Pallas kernels for 10%

profile of v3, /device:TPU:0, one launch (start us, length us, event | category | flops | bytes accessed | tf_op | source)
XLA Modules:
  0.0 629.4 jit_solution(2020408399938888109)
XLA Ops:
  30.6 8.5 %collective-permute-done.2.refs_6_.refs_7_ = bf16[384,512]{1,0:T(8,128)(2,1)} collective-permute-done((bf16[384,512]{1,0:T(8,128)(2,1)}, bf16[384,512]{1,0:T(8,128)(2,1)}, u32[]{:S(2)}, u32[]{:S(2)}) %collective-permute-start.2) | collective-permute-done | bytes 393248 | tf_op jit(solution)/shard_map/ppermute | solution.py:113
  47.2 9.2 %attention_forward.2 = (bf16[384,512]{1,0:T(8,128)(2,1)S(1)}, f32[2,1,1024]{2,1,0:T(1,128)S(1)}) custom-call(s32[4]{0:T(128)S(1)} %add_multiply_fusion.base_ref, s32[512,1]{1,0:T(8,128)S(1)} %copy.52.rows_ref, s32[1,512]{1,0:T(1,128)S(1)} %add_add_fusion.1.top_ref, s32[1,512]{1,0:T(1,128)S(1)} %bitcast.110, bf16[384,512]{1,0:T(8,128)(2,1)S(1)} %copy-done.66, ...), custom_call_target="tpu_custom_call" | custom-call | flops 12099999744 | bytes 11000000 | tf_op jit(solution)/shard_map/attention_forward/pallas_call | solution.py:352
  63.5 8.4 %collective-permute-done.6 = bf16[384,512]{1,0:T(8,128)(2,1)S(1)} collective-permute-done((bf16[384,512]{1,0:T(8,128)(2,1)S(1)}, bf16[384,512]{1,0:T(8,128)(2,1)S(1)}, u32[]{:S(2)}, u32[]{:S(2)}) %collective-permute-start.6) | collective-permute-done | bytes 393248 | tf_op jit(solution)/shard_map/ppermute | solution.py:61
  75.2 9.1 %collective-permute-done.8 = bf16[768,256]{1,0:T(8,128)(2,1)S(1)} collective-permute-done((bf16[768,256]{1,0:T(8,128)(2,1)S(1)}, bf16[768,256]{1,0:T(8,128)(2,1)S(1)}, u32[]{:S(2)}, u32[]{:S(2)}) %collective-permute-start.8) | collective-permute-done | bytes 393248 | tf_op jit(solution)/shard_map/ppermute | solution.py:61
  87.6 7.9 %feed_forward.2 = (f32[512,1024]{1,0:T(8,128)S(1)}, f32[512,1024]{1,0:T(8,128)S(1)}, bf16[512,1024]{1,0:T(8,128)(2,1)S(1)}, f32[256,1536]{1,0:T(8,128)S(1)}, bf16[256,1536]{1,0:T(8,128)(2,1)S(1)}) custom-call(bf16[512,1536]{1,0:T(8,128)(2,1)S(1)} %pad_maximum_fusion.6.x_ref, bf16[2,1536,1024]{2,1,0:T(8,128)(2,1)S(1)} %bitcast.115, ...), custom_call_target="tpu_custom_call" | custom-call | flops 8800000000 | bytes 8000000 | tf_op jit(solution)/shard_map/feed_forward/pallas_call | solution.py:237
  101.5 9.8 %collective-permute-done.11 = bf16[128,1536]{1,0:T(8,128)(2,1)S(1)} collective-permute-done((bf16[128,1536]{1,0:T(8,128)(2,1)S(1)}, bf16[128,1536]{1,0:T(8,128)(2,1)S(1)}, u32[]{:S(2)}, u32[]{:S(2)}) %collective-permute-start.11) | collective-permute-done | bytes 393248 | tf_op jit(solution)/shard_map/ppermute | solution.py:61
  116.2 9.5 %collective-permute-done.13 = bf16[128,1536]{1,0:T(8,128)(2,1)S(1)} collective-permute-done((bf16[128,1536]{1,0:T(8,128)(2,1)S(1)}, bf16[128,1536]{1,0:T(8,128)(2,1)S(1)}, u32[]{:S(2)}, u32[]{:S(2)}) %collective-permute-start.13) | collective-permute-done | bytes 393248 | tf_op jit(solution)/shard_map/ppermute | solution.py:61
  137.4 12.4 %collective-permute-done.18.refs_6_.refs_7_ = bf16[384,512]{1,0:T(8,128)(2,1)S(1)} collective-permute-done((bf16[384,512]{1,0:T(8,128)(2,1)S(1)}, bf16[384,512]{1,0:T(8,128)(2,1)S(1)}, u32[]{:S(2)}, u32[]{:S(2)}) %collective-permute-start.18) | collective-permute-done | bytes 393248 | tf_op jit(solution)/shard_map/ppermute | solution.py:113
  156.9 8.3 %attention_forward.3 = (bf16[384,512]{1,0:T(8,128)(2,1)S(1)}, f32[2,1,1024]{2,1,0:T(1,128)S(1)}) custom-call(s32[4]{0:T(128)S(1)} %add_multiply_fusion.base_ref, s32[512,1]{1,0:T(8,128)S(1)} %copy.52.rows_ref, s32[1,512]{1,0:T(1,128)S(1)} %add_add_fusion.1.top_ref, s32[1,512]{1,0:T(1,128)S(1)} %bitcast.111, bf16[384,512]{1,0:T(8,128)(2,1)S(1)} %get-tuple-element.240.q_ref, ...), custom_call_target="tpu_custom_call" | custom-call | flops 12099999744 | bytes 11000000 | tf_op jit(solution)/shard_map/attention_forward/pallas_call | solution.py:352
  171.5 8.0 %collective-permute-done.22 = bf16[384,512]{1,0:T(8,128)(2,1)S(1)} collective-permute-done((bf16[384,512]{1,0:T(8,128)(2,1)S(1)}, bf16[384,512]{1,0:T(8,128)(2,1)S(1)}, u32[]{:S(2)}, u32[]{:S(2)}) %collective-permute-start.22) | collective-permute-done | bytes 393248 | tf_op jit(solution)/shard_map/ppermute | solution.py:61
  182.3 8.5 %collective-permute-done.24 = bf16[768,256]{1,0:T(8,128)(2,1)S(1)} collective-permute-done((bf16[768,256]{1,0:T(8,128)(2,1)S(1)}, bf16[768,256]{1,0:T(8,128)(2,1)S(1)}, u32[]{:S(2)}, u32[]{:S(2)}) %collective-permute-start.24) | collective-permute-done | bytes 393248 | tf_op jit(solution)/shard_map/ppermute | solution.py:61
  194.2 8.0 %feed_forward.3 = (f32[512,1024]{1,0:T(8,128)S(1)}, f32[512,1024]{1,0:T(8,128)S(1)}, bf16[512,1024]{1,0:T(8,128)(2,1)S(1)}, f32[256,1536]{1,0:T(8,128)S(1)}, bf16[256,1536]{1,0:T(8,128)(2,1)S(1)}) custom-call(bf16[512,1536]{1,0:T(8,128)(2,1)S(1)} %pad_maximum_fusion.8.x_ref, bf16[2,1536,1024]{2,1,0:T(8,128)(2,1)S(1)} %bitcast.117, ...), custom_call_target="tpu_custom_call" | custom-call | flops 8800000000 | bytes 8000000 | tf_op jit(solution)/shard_map/feed_forward/pallas_call | solution.py:237
  205.0 8.2 %feed_forward_back.2 = (bf16[512,1024]{1,0:T(8,128)(2,1)S(1)}, bf16[512,1024]{1,0:T(8,128)(2,1)S(1)}, f32[256,1536]{1,0:T(8,128)S(1)}, bf16[256,1536]{1,0:T(8,128)(2,1)S(1)}) custom-call(bf16[512,1536]{1,0:T(8,128)(2,1)S(1)} %copy-done.10, bf16[2,1024,1536]{2,1,0:T(8,128)(2,1)S(1)} %copy-done.39, bf16[2,1536,1024]{2,1,0:T(8,128)(2,1)S(1)} %bitcast.117, ...), custom_call_target="tpu_custom_call" | custom-call | flops 9900000256 | bytes 9000000 | tf_op jit(solution)/shard_map/feed_forward_back/pallas_call | solution.py:274
  218.0 9.6 %collective-permute-done.27 = bf16[128,1536]{1,0:T(8,128)(2,1)S(1)} collective-permute-done((bf16[128,1536]{1,0:T(8,128)(2,1)S(1)}, bf16[128,1536]{1,0:T(8,128)(2,1)S(1)}, u32[]{:S(2)}, u32[]{:S(2)}) %collective-permute-start.27) | collective-permute-done | bytes 393248 | tf_op jit(solution)/shard_map/ppermute | solution.py:61
  234.5 9.5 %collective-permute-done.29 = bf16[128,1536]{1,0:T(8,128)(2,1)S(1)} collective-permute-done((bf16[128,1536]{1,0:T(8,128)(2,1)S(1)}, bf16[128,1536]{1,0:T(8,128)(2,1)S(1)}, u32[]{:S(2)}, u32[]{:S(2)}) %collective-permute-start.29) | collective-permute-done | bytes 393248 | tf_op jit(solution)/shard_map/ppermute | solution.py:61
  251.8 13.6 %attention_backward.2 = (bf16[384,512]{1,0:T(8,128)(2,1)S(1)}, f32[2,192,512]{2,1,0:T(8,128)S(1)}, bf16[2,192,512]{2,1,0:T(8,128)(2,1)}, bf16[2,192,512]{2,1,0:T(8,128)(2,1)S(1)}, bf16[2,192,512]{2,1,0:T(8,128)(2,1)S(1)}) custom-call(s32[4]{0:T(128)S(1)} %add_multiply_fusion.base_ref, s32[512,1]{1,0:T(8,128)S(1)} %copy.52.rows_ref, ...), custom_call_target="tpu_custom_call" | custom-call | flops 18150000640 | bytes 16500000 | tf_op jit(solution)/shard_map/attention_backward/pallas_call | solution.py:413
  265.3 6.1 collective-permute-done.32
  279.3 6.0 collective-permute-done.35
  290.4 6.5 %collective-permute-done.42 = bf16[128,1536]{1,0:T(8,128)(2,1)S(1)} collective-permute-done((bf16[128,1536]{1,0:T(8,128)(2,1)S(1)}, bf16[128,1536]{1,0:T(8,128)(2,1)S(1)}, u32[]{:S(2)}, u32[]{:S(2)}) %collective-permute-start.42) | collective-permute-done | bytes 393248 | tf_op jit(solution)/shard_map/ppermute | solution.py:61
  326.4 7.6 %collective-permute-done.45 = bf16[128,1536]{1,0:T(8,128)(2,1)S(1)} collective-permute-done((bf16[128,1536]{1,0:T(8,128)(2,1)S(1)}, bf16[128,1536]{1,0:T(8,128)(2,1)S(1)}, u32[]{:S(2)}, u32[]{:S(2)}) %collective-permute-start.45) | collective-permute-done | bytes 393248 | tf_op jit(solution)/shard_map/ppermute | solution.py:61
  367.4 8.2 %feed_forward_back.3 = (bf16[512,1024]{1,0:T(8,128)(2,1)S(1)}, bf16[512,1024]{1,0:T(8,128)(2,1)S(1)}, f32[256,1536]{1,0:T(8,128)S(1)}, bf16[256,1536]{1,0:T(8,128)(2,1)S(1)}) custom-call(bf16[512,1536]{1,0:T(8,128)(2,1)S(1)} %pad_maximum_fusion.11.x_ref, bf16[2,1024,1536]{2,1,0:T(8,128)(2,1)S(1)} %copy-done.40, bf16[2,1536,1024]{2,1,0:T(8,128)(2,1)S(1)} %copy-done.38, ...), custom_call_target="tpu_custom_call" | custom-call | flops 9900000256 | bytes 9000000 | tf_op jit(solution)/shard_map/feed_forward_back/pallas_call | solution.py:274
  383.3 17.6 %collective-permute-done.54 = bf16[256,768]{1,0:T(8,128)(2,1)S(1)} collective-permute-done((bf16[256,768]{1,0:T(8,128)(2,1)S(1)}, bf16[256,768]{1,0:T(8,128)(2,1)S(1)}, u32[]{:S(2)}, u32[]{:S(2)}) %collective-permute-start.54) | collective-permute-done | bytes 393248 | tf_op jit(solution)/shard_map/ppermute | solution.py:61
  437.1 14.2 %attention_backward.3 = (bf16[384,512]{1,0:T(8,128)(2,1)S(1)}, f32[2,192,512]{2,1,0:T(8,128)S(1)}, bf16[2,192,512]{2,1,0:T(8,128)(2,1)}, bf16[2,192,512]{2,1,0:T(8,128)(2,1)S(1)}, bf16[2,192,512]{2,1,0:T(8,128)(2,1)S(1)}) custom-call(s32[4]{0:T(128)S(1)} %add_multiply_fusion.base_ref, s32[512,1]{1,0:T(8,128)S(1)} %copy.52.rows_ref, ...), custom_call_target="tpu_custom_call" | custom-call | flops 18150000640 | bytes 16500000 | tf_op jit(solution)/shard_map/attention_backward/pallas_call | solution.py:413
  451.3 7.0 %collective-permute-done.61 = bf16[256,1024]{1,0:T(8,128)(2,1)S(1)} collective-permute-done((bf16[256,1024]{1,0:T(8,128)(2,1)S(1)}, bf16[256,1024]{1,0:T(8,128)(2,1)S(1)}, u32[]{:S(2)}, u32[]{:S(2)}) %collective-permute-start.61) | collective-permute-done | bytes 524320 | tf_op jit(solution)/shard_map/ppermute | solution.py:61
  473.2 9.5 %collective-permute-done.64 = bf16[2,192,512]{2,1,0:T(8,128)(2,1)S(1)} collective-permute-done((bf16[2,192,512]{2,1,0:T(8,128)(2,1)S(1)}, bf16[2,192,512]{2,1,0:T(8,128)(2,1)S(1)}, u32[]{:S(2)}, u32[]{:S(2)}) %collective-permute-start.64) | collective-permute-done | bytes 393248 | tf_op jit(solution)/shard_map/ppermute | solution.py:121
  488.1 13.7 %collective-permute-done.65.two_ref = bf16[2,192,512]{2,1,0:T(8,128)(2,1)S(1)} collective-permute-done((bf16[2,192,512]{2,1,0:T(8,128)(2,1)S(1)}, bf16[2,192,512]{2,1,0:T(8,128)(2,1)S(1)}, u32[]{:S(2)}, u32[]{:S(2)}) %collective-permute-start.65) | collective-permute-done | bytes 393248 | tf_op jit(solution)/shard_map/ppermute | solution.py:124
  504.8 6.5 %collective-permute-done.67 = bf16[768,256]{1,0:T(8,128)(2,1)S(1)} collective-permute-done((bf16[768,256]{1,0:T(8,128)(2,1)S(1)}, bf16[768,256]{1,0:T(8,128)(2,1)S(1)}, u32[]{:S(2)}, u32[]{:S(2)}) %collective-permute-start.67) | collective-permute-done | bytes 393248 | tf_op jit(solution)/shard_map/ppermute | solution.py:61
  521.5 13.4 %reduce-scatter.15.cloned.1.call-done = bf16[192,2048]{1,0:T(8,128)(2,1)} async-done(((bf16[768,2048]{1,0:T(8,128)(2,1)}), bf16[192,2048]{1,0:T(8,128)(2,1)}) %reduce-scatter.15.cloned.1.call-update) | async-done | bytes 786448 | tf_op jit(solution)/shard_map/reduce_scatter | solution.py:130
  544.8 7.4 %collective-permute-done.74 = bf16[256,768]{1,0:T(8,128)(2,1)S(1)} collective-permute-done((bf16[256,768]{1,0:T(8,128)(2,1)S(1)}, bf16[256,768]{1,0:T(8,128)(2,1)S(1)}, u32[]{:S(2)}, u32[]{:S(2)}) %collective-permute-start.74) | collective-permute-done | bytes 393248 | tf_op jit(solution)/shard_map/ppermute | solution.py:61
  574.0 17.0 %collective-permute-start.81 = (f32[4,1536]{1,0:T(4,128)S(1)}, f32[4,1536]{1,0:T(4,128)S(1)}, u32[]{:S(2)}, u32[]{:S(2)}) collective-permute-start(f32[4,1536]{1,0:T(4,128)S(1)} %add.423), channel_id=1, source_target_pairs={{0,8},{4,12},{8,0},{12,4},{16,24},{20,28},{24,16},{28,20},{1,9},{5... | collective-permute-start | bytes 73736 | tf_op jit(solution)/shard_map/ppermute | solution.py:61
  595.6 4.5 collective-permute-done.82
  605.4 11.3 %reduce-scatter.21.cloned.1.call-done = bf16[192,1152]{1,0:T(8,128)(2,1)} async-done(((bf16[768,1152]{1,0:T(8,128)(2,1)}), bf16[192,1152]{1,0:T(8,128)(2,1)}) %reduce-scatter.21.cloned.1.call-update) | async-done | bytes 442384
  (614 shorter events, 307.6 us)
Async XLA Ops:
  7.2 348.3 %reduce-scatter.11.cloned.1.call-start = ((), (), s32[]{:S(2)}) async-start(), calls=%async_computation.6 | async-start | bytes 1966080 | tf_op jit(solution)/shard_map/reduce_scatter | solution.py:130
  21.5 17.5 %collective-permute-start.2 = (bf16[384,512]{1,0:T(8,128)(2,1)}, bf16[384,512]{1,0:T(8,128)(2,1)}, u32[]{:S(2)}, u32[]{:S(2)}) collective-permute-start(bf16[384,512]{1,0:T(8,128)(2,1)} %get-tuple-element.213.refs_0_.refs_1_), channel_id=1, source_target_pairs={{8,20},{12,16},{24,4},{28,0},{9,21},{13,17},{25,5},{29,1},{10,22},... | collective-permute-start | bytes 1179656 | tf_op jit(solution)/shard_map/ppermute | solution.py:113
  22.8 21.7 %collective-permute-start = (bf16[384,512]{1,0:T(8,128)(2,1)}, bf16[384,512]{1,0:T(8,128)(2,1)}, u32[]{:S(2)}, u32[]{:S(2)}) collective-permute-start(bf16[384,512]{1,0:T(8,128)(2,1)} %get-tuple-element.213.refs_0_.refs_1_), channel_id=1, source_target_pairs={{0,4},{4,0},{8,12},{12,8},{16,20},{20,16},{24,28},{28,24},{1,5},{5... | collective-permute-start | bytes 1179656 | tf_op jit(solution)/shard_map/ppermute | solution.py:61
  25.8 21.4 %collective-permute-start.1 = (bf16[384,512]{1,0:T(8,128)(2,1)}, bf16[384,512]{1,0:T(8,128)(2,1)}, u32[]{:S(2)}, u32[]{:S(2)}) collective-permute-start(bf16[384,512]{1,0:T(8,128)(2,1)} %get-tuple-element.213.refs_0_.refs_1_), channel_id=1, source_target_pairs={{8,16},{12,20},{24,0},{28,4},{9,17},{13,21},{25,1},{29,5},{10,18},... | collective-permute-start | bytes 1179656 | tf_op jit(solution)/shard_map/ppermute | solution.py:114
  39.0 17.4 %collective-permute-start.3 = (bf16[768,256]{1,0:T(8,128)(2,1)S(1)}, bf16[768,256]{1,0:T(8,128)(2,1)}, u32[]{:S(2)}, u32[]{:S(2)}) collective-permute-start(bf16[768,256]{1,0:T(8,128)(2,1)S(1)} %get-tuple-element.220), channel_id=1, source_target_pairs={{0,4},{4,0},{8,12},{12,8},{16,20},{20,16},{24,28},{28,24},{1,5},{5... | collective-permute-start | bytes 1179656 | tf_op jit(solution)/shard_map/ppermute | solution.py:61
  134.5 20.5 %collective-permute-start.16 = (bf16[384,512]{1,0:T(8,128)(2,1)S(1)}, bf16[384,512]{1,0:T(8,128)(2,1)S(1)}, u32[]{:S(2)}, u32[]{:S(2)}) collective-permute-start(bf16[384,512]{1,0:T(8,128)(2,1)S(1)} %get-tuple-element.241.refs_0_.refs_1_), channel_id=1, source_target_pairs={{0,4},{4,0},{8,12},{12,8},{16,20},{20,16},{24,28},{28,24},{1,5},{5... | collective-permute-start | bytes 1179656 | tf_op jit(solution)/shard_map/ppermute | solution.py:61
  135.6 21.4 %collective-permute-start.17 = (bf16[384,512]{1,0:T(8,128)(2,1)S(1)}, bf16[384,512]{1,0:T(8,128)(2,1)S(1)}, u32[]{:S(2)}, u32[]{:S(2)}) collective-permute-start(bf16[384,512]{1,0:T(8,128)(2,1)S(1)} %get-tuple-element.241.refs_0_.refs_1_), channel_id=1, source_target_pairs={{8,16},{12,20},{24,0},{28,4},{9,17},{13,21},{25,1},{29,5},{10,18},... | collective-permute-start | bytes 1179656 | tf_op jit(solution)/shard_map/ppermute | solution.py:114
  248.6 25.7 %collective-permute-start.40 = (bf16[256,1536]{1,0:T(8,128)(2,1)S(1)}, bf16[256,1536]{1,0:T(8,128)(2,1)S(1)}, u32[]{:S(2)}, u32[]{:S(2)}) collective-permute-start(bf16[256,1536]{1,0:T(8,128)(2,1)S(1)} %get-tuple-element.297), channel_id=1, source_target_pairs={{0,1},{1,0},{2,3},{3,2},{4,5},{5,4},{6,7},{7,6},{8,9},{9,8},{10,11... | collective-permute-start | bytes 2359304 | tf_op jit(solution)/shard_map/ppermute | solution.py:61
  248.9 22.5 %collective-permute-start.33 = (bf16[256,1024]{1,0:T(8,128)(2,1)S(1)}, bf16[256,1024]{1,0:T(8,128)(2,1)S(1)}, u32[]{:S(2)}, u32[]{:S(2)}) collective-permute-start(bf16[256,1024]{1,0:T(8,128)(2,1)S(1)} %get-tuple-element.274), channel_id=1, source_target_pairs={{0,4},{4,0},{8,12},{12,8},{16,20},{20,16},{24,28},{28,24},{1,5},{5... | collective-permute-start | bytes 1572872 | tf_op jit(solution)/shard_map/ppermute | solution.py:61
  249.9 21.5 %collective-permute-start.32 = (bf16[768,256]{1,0:T(8,128)(2,1)S(1)}, bf16[768,256]{1,0:T(8,128)(2,1)S(1)}, u32[]{:S(2)}, u32[]{:S(2)}) collective-permute-start(bf16[768,256]{1,0:T(8,128)(2,1)S(1)} %get-tuple-element.272), channel_id=1, source_target_pairs={{0,4},{4,0},{8,12},{12,8},{16,20},{20,16},{24,28},{28,24},{1,5},{5... | collective-permute-start | bytes 1179656 | tf_op jit(solution)/shard_map/ppermute | solution.py:61
  277.3 22.7 %collective-permute-start.37 = (bf16[256,1024]{1,0:T(8,128)(2,1)}, bf16[256,1024]{1,0:T(8,128)(2,1)}, u32[]{:S(2)}, u32[]{:S(2)}) collective-permute-start(bf16[256,1024]{1,0:T(8,128)(2,1)} %get-tuple-element.280), channel_id=1, source_target_pairs={{0,4},{4,0},{8,12},{12,8},{16,20},{20,16},{24,28},{28,24},{1,5},{5... | collective-permute-start | bytes 1572872 | tf_op jit(solution)/shard_map/ppermute | solution.py:61
  278.3 25.4 %collective-permute-start.34 = (bf16[2,192,512]{2,1,0:T(8,128)(2,1)}, bf16[2,192,512]{2,1,0:T(8,128)(2,1)}, u32[]{:S(2)}, u32[]{:S(2)}) collective-permute-start(bf16[2,192,512]{2,1,0:T(8,128)(2,1)} %get-tuple-element.277), channel_id=1, source_target_pairs={{0,4},{4,0},{8,12},{12,8},{16,20},{20,16},{24,28},{28,24},{1,5},{5... | collective-permute-start | bytes 1179656 | tf_op jit(solution)/shard_map/ppermute | solution.py:61
  319.1 26.0 %collective-permute-start.49 = (bf16[768,256]{1,0:T(8,128)(2,1)}, bf16[768,256]{1,0:T(8,128)(2,1)}, u32[]{:S(2)}, u32[]{:S(2)}) collective-permute-start(bf16[768,256]{1,0:T(8,128)(2,1)} %collective-permute-done.3), channel_id=1, source_target_pairs={{0,1},{1,0},{2,3},{3,2},{4,5},{5,4},{6,7},{7,6},{8,9},{9,8},{10,11... | collective-permute-start | bytes 1179656 | tf_op jit(solution)/shard_map/ppermute | solution.py:61
  319.6 95.1 %reduce-scatter.13.cloned.1.call-start = ((), (), s32[]{:S(2)}) async-start(), calls=%async_computation.7 | async-start | bytes 3932160 | tf_op jit(solution)/shard_map/reduce_scatter | solution.py:130
  357.5 109.2 %reduce-scatter.19.cloned.1.call-start = ((), (), s32[]{:S(2)}) async-start(), calls=%async_computation.10 | async-start | bytes 2211840
  378.2 22.7 %collective-permute-start.55 = (bf16[256,1024]{1,0:T(8,128)(2,1)S(1)}, bf16[256,1024]{1,0:T(8,128)(2,1)}, u32[]{:S(2)}, u32[]{:S(2)}) collective-permute-start(bf16[256,1024]{1,0:T(8,128)(2,1)S(1)} %get-tuple-element.325), channel_id=1, source_target_pairs={{0,4},{4,0},{8,12},{12,8},{16,20},{20,16},{24,28},{28,24},{1,5},{5... | collective-permute-start | bytes 1572872 | tf_op jit(solution)/shard_map/ppermute | solution.py:61
  379.0 21.9 %collective-permute-start.54 = (bf16[256,768]{1,0:T(8,128)(2,1)S(1)}, bf16[256,768]{1,0:T(8,128)(2,1)S(1)}, u32[]{:S(2)}, u32[]{:S(2)}) collective-permute-start(bf16[256,768]{1,0:T(8,128)(2,1)S(1)} %get-tuple-element.323), channel_id=1, source_target_pairs={{0,4},{4,0},{8,12},{12,8},{16,20},{20,16},{24,28},{28,24},{1,5},{5... | collective-permute-start | bytes 1179656 | tf_op jit(solution)/shard_map/ppermute | solution.py:61
  380.3 20.6 %collective-permute-start.53 = (bf16[128,1536]{1,0:T(8,128)(2,1)S(1)}, bf16[128,1536]{1,0:T(8,128)(2,1)S(1)}, u32[]{:S(2)}, u32[]{:S(2)}) collective-permute-start(bf16[128,1536]{1,0:T(8,128)(2,1)S(1)} %add_convert_fusion.10), channel_id=1, source_target_pairs={{0,2},{1,3},{2,0},{3,1},{4,6},{5,7},{6,4},{7,5},{8,10},{9,11},{10,... | collective-permute-start | bytes 1179656 | tf_op jit(solution)/shard_map/ppermute | solution.py:61
  380.5 41.2 %collective-permute-start.66 = (bf16[768,256]{1,0:T(8,128)(2,1)}, bf16[768,256]{1,0:T(8,128)(2,1)}, u32[]{:S(2)}, u32[]{:S(2)}) collective-permute-start(bf16[768,256]{1,0:T(8,128)(2,1)} %collective-permute-done.19), channel_id=1, source_target_pairs={{0,1},{1,0},{2,3},{3,2},{4,5},{5,4},{6,7},{7,6},{8,9},{9,8},{10,11... | collective-permute-start | bytes 1179656 | tf_op jit(solution)/shard_map/ppermute | solution.py:61
  380.5 25.7 %collective-permute-start.59 = (bf16[768,256]{1,0:T(8,128)(2,1)S(1)}, bf16[768,256]{1,0:T(8,128)(2,1)S(1)}, u32[]{:S(2)}, u32[]{:S(2)}) collective-permute-start(bf16[768,256]{1,0:T(8,128)(2,1)S(1)} %copy-done.116), channel_id=1, source_target_pairs={{0,1},{1,0},{2,3},{3,2},{4,5},{5,4},{6,7},{7,6},{8,9},{9,8},{10,11... | collective-permute-start | bytes 1179656 | tf_op jit(solution)/shard_map/ppermute | solution.py:61
  428.4 106.6 %reduce-scatter.15.cloned.1.call-start = ((), (), s32[]{:S(2)}) async-start(), calls=%async_computation.8 | async-start | bytes 3932160 | tf_op jit(solution)/shard_map/reduce_scatter | solution.py:130
  432.7 18.6 %collective-permute-start.62 = (bf16[256,1024]{1,0:T(8,128)(2,1)S(1)}, bf16[256,1024]{1,0:T(8,128)(2,1)S(1)}, u32[]{:S(2)}, u32[]{:S(2)}) collective-permute-start(bf16[256,1024]{1,0:T(8,128)(2,1)S(1)} %copy-done.107), channel_id=1, source_target_pairs={{0,4},{4,0},{8,12},{12,8},{16,20},{20,16},{24,28},{28,24},{1,5},{5... | collective-permute-start | bytes 1572872 | tf_op jit(solution)/shard_map/ppermute | solution.py:61
  433.9 24.4 %collective-permute-start.61 = (bf16[256,1024]{1,0:T(8,128)(2,1)S(1)}, bf16[256,1024]{1,0:T(8,128)(2,1)S(1)}, u32[]{:S(2)}, u32[]{:S(2)}) collective-permute-start(bf16[256,1024]{1,0:T(8,128)(2,1)S(1)} %copy-done.106), channel_id=1, source_target_pairs={{0,4},{4,0},{8,12},{12,8},{16,20},{20,16},{24,28},{28,24},{1,5},{5... | collective-permute-start | bytes 1572872 | tf_op jit(solution)/shard_map/ppermute | solution.py:61
  469.0 134.0 %reduce-scatter.17.cloned.1.call-start = ((), (), s32[]{:S(2)}) async-start(), calls=%async_computation.9 | async-start | bytes 1966080 | tf_op jit(solution)/shard_map/reduce_scatter | solution.py:130
  482.9 18.9 %collective-permute-start.65 = (bf16[2,192,512]{2,1,0:T(8,128)(2,1)S(1)}, bf16[2,192,512]{2,1,0:T(8,128)(2,1)S(1)}, u32[]{:S(2)}, u32[]{:S(2)}) collective-permute-start(bf16[2,192,512]{2,1,0:T(8,128)(2,1)S(1)} %add_convert_fusion.9), channel_id=1, source_target_pairs={{0,24},{4,28},{16,8},{20,12},{1,25},{5,29},{17,9},{21,13},{2,26},{... | collective-permute-start | bytes 1179656 | tf_op jit(solution)/shard_map/ppermute | solution.py:124
  484.5 18.4 %collective-permute-start.63 = (bf16[2,192,512]{2,1,0:T(8,128)(2,1)}, bf16[2,192,512]{2,1,0:T(8,128)(2,1)S(1)}, u32[]{:S(2)}, u32[]{:S(2)}) collective-permute-start(bf16[2,192,512]{2,1,0:T(8,128)(2,1)} %get-tuple-element.354), channel_id=1, source_target_pairs={{0,4},{4,0},{8,12},{12,8},{16,20},{20,16},{24,28},{28,24},{1,5},{5... | collective-permute-start | bytes 1179656 | tf_op jit(solution)/shard_map/ppermute | solution.py:61
  514.6 23.0 %collective-permute-start.69 = (bf16[128,1536]{1,0:T(8,128)(2,1)}, bf16[128,1536]{1,0:T(8,128)(2,1)S(1)}, u32[]{:S(2)}, u32[]{:S(2)}) collective-permute-start(bf16[128,1536]{1,0:T(8,128)(2,1)} %add_convert_fusion.8), channel_id=1, source_target_pairs={{0,2},{1,3},{2,0},{3,1},{4,6},{5,7},{6,4},{7,5},{8,10},{9,11},{10,... | collective-permute-start | bytes 1179656 | tf_op jit(solution)/shard_map/ppermute | solution.py:61
  516.3 21.2 %collective-permute-start.71 = (bf16[256,768]{1,0:T(8,128)(2,1)}, bf16[256,768]{1,0:T(8,128)(2,1)}, u32[]{:S(2)}, u32[]{:S(2)}) collective-permute-start(bf16[256,768]{1,0:T(8,128)(2,1)} %get-tuple-element.380), channel_id=1, source_target_pairs={{0,4},{4,0},{8,12},{12,8},{16,20},{20,16},{24,28},{28,24},{1,5},{5... | collective-permute-start | bytes 1179656 | tf_op jit(solution)/shard_map/ppermute | solution.py:61
  516.9 20.6 %collective-permute-start.70 = (bf16[768,256]{1,0:T(8,128)(2,1)}, bf16[768,256]{1,0:T(8,128)(2,1)}, u32[]{:S(2)}, u32[]{:S(2)}) collective-permute-start(bf16[768,256]{1,0:T(8,128)(2,1)} %get-tuple-element.378), channel_id=1, source_target_pairs={{0,4},{4,0},{8,12},{12,8},{16,20},{20,16},{24,28},{28,24},{1,5},{5... | collective-permute-start | bytes 1179656 | tf_op jit(solution)/shard_map/ppermute | solution.py:61
  537.4 79.3 %reduce-scatter.21.cloned.1.call-start = ((), (), s32[]{:S(2)}) async-start(), calls=%async_computation.11 | async-start | bytes 2211840
  567.8 32.9 %collective-permute-start.75 = (bf16[256,1536]{1,0:T(8,128)(2,1)S(1)}, bf16[256,1536]{1,0:T(8,128)(2,1)S(1)}, u32[]{:S(2)}, u32[]{:S(2)}) collective-permute-start(bf16[256,1536]{1,0:T(8,128)(2,1)S(1)} %pad_maximum_fusion.31), channel_id=1, source_target_pairs={{0,1},{1,0},{2,3},{3,2},{4,5},{5,4},{6,7},{7,6},{8,9},{9,8},{10,11... | collective-permute-start | bytes 2359304 | tf_op jit(solution)/shard_map/ppermute | solution.py:61
  574.0 20.2 %collective-permute-start.81 = (f32[4,1536]{1,0:T(4,128)S(1)}, f32[4,1536]{1,0:T(4,128)S(1)}, u32[]{:S(2)}, u32[]{:S(2)}) collective-permute-start(f32[4,1536]{1,0:T(4,128)S(1)} %add.423), channel_id=1, source_target_pairs={{0,8},{4,12},{8,0},{12,4},{16,24},{20,28},{24,16},{28,20},{1,9},{5... | collective-permute-start | bytes 73736 | tf_op jit(solution)/shard_map/ppermute | solution.py:61
  (195 other events, 1948.9 us)
Sparse Core Ops, SparseCore 0:
  319.8 32.0 reduce-scatter.10
  357.6 57.1 reduce-scatter.12
  428.5 37.9 reduce-scatter.18
  469.3 65.6 reduce-scatter.14
  537.6 38.3 reduce-scatter.16
  578.2 38.4 reduce-scatter.20

commit v4 on v3

--- a/solution.py
+++ b/solution.py
@@ -115,13 +115,13 @@
     return swap(kv, "dp", 1), behind, across
 
 
-def keys_back(beside, behind, across):
+def keys_back(beside, behind, across, jobs):
     n = lax.axis_size("dp")
     late = [i for i in range(n) if (i + STRETCHES // 2) % STRETCHES >= 2]
-    across = lax.ppermute(across, "dp", [(i, i ^ 1) for i in late])
+    across = window(across, lax.ppermute(across, "dp", [(i, i ^ 1) for i in late]), jobs)
     total = (behind.astype(F32) + across.astype(F32)).astype(BF)
     back = in_stretches(lambda s: (None, None, -2, -2)[s], n)
-    return swap(beside, "dp", 1), lax.ppermute(total, "dp", back)
+    return total, swap(beside, "dp", 1), lax.ppermute(total, "dp", back)
 
 
 def scatter_grad(grad):
@@ -633,13 +633,13 @@
     g_qkv = [product(attn_left[l], qkv_right[l]) for l in layers]
     g_both = joined(g_gate[0], g_up[0])
     g_more = joined(g_up[1], g_down[1])
-    g_attn = [joined(g_out[l], g_qkv[l]) for l in layers]
+    g_attn = joined(g_out[1], g_qkv[1])
     s_gate = scatter(None, g_gate[1])
     s_more = scatter(s_gate, g_more)
-    s_attn = [None, scatter(s_more, g_attn[1])]
-    s_both = scatter(s_attn[1], g_both)
-    s_down = scatter(s_both, g_down[0])
-    s_attn[0] = scatter(s_down, g_attn[0])
+    s_attn = scatter(s_more, g_attn)
+    s_both = scatter(s_attn, g_both)
+    g_tail = joined(g_out[0], g_qkv[0], g_down[0])
+    s_tail = scatter(s_both, g_tail)
     plan = {
         ("keys", 0): [down_left[1].turn],
         ("attn", 0): [down_left[1].send],
@@ -653,18 +653,20 @@
         ("back_sum1", 1): [gate_right[1].sends[0], mlp_left[1].turn],
         ("back_all1", 1): [gate_right[1].sends[1]],
         ("back_attn", 1): [mlp_left[1].send, up_right[1].sends[0]],
-        ("back_keys", 1): [up_right[1].sends[1], out_left[1].turn, g_gate[1]],
+        ("back_hop", 1): [out_left[1].turn],
+        ("back_keys", 1): [up_right[1].sends[1], g_gate[1]],
         ("back_join", 1): [act_right[1].sends[0]],
         ("back_sum2", 1): [act_right[1].sends[1], g_up[1]],
         ("back_all2", 1): [out_left[1].send, g_more],
         ("back_mlp", 0): [qkv_right[1].sends[0], s_gate],
         ("back_sum1", 0): [qkv_right[1].sends[1], gate_right[0].sends[0], down_left[0].turn],
-        ("back_all1", 0): [gate_right[0].sends[1], g_attn[1], s_more],
+        ("back_all1", 0): [gate_right[0].sends[1], g_attn, s_more],
         ("back_attn", 0): [*up_right[0].sends],
-        ("back_keys", 0): [g_both, out_left[0].turn, s_attn[1]],
-        ("back_join", 0): [down_left[0].send],
-        ("back_sum2", 0): [out_left[0].send, qkv_right[0].sends[0], g_down[0], s_both],
-        ("back_all2", 0): [qkv_right[0].sends[1]],
+        ("back_hop", 0): [g_gate[0], out_left[0].turn],
+        ("back_keys", 0): [down_left[0].send, g_both, s_attn],
+        ("back_join", 0): [out_left[0].send],
+        ("back_sum2", 0): [*qkv_right[0].sends, g_down[0]],
+        ("back_all2", 0): [g_tail],
     }
     jobs = lambda name, l: plan.get((name, l), [])
 
@@ -715,8 +717,8 @@
         grad_t = mm(w_out[l], out_in, 1, 1).astype(BF)
         dq, own, *d_far = attn_bwd(q_t, blocks, places, kv, tables, log_total, value["mixed", l], grad_t)
         dq, d_far = window(out_in, (dq, d_far), jobs("back_attn", l))
-        d_far = keys_back(*d_far)
-        d_far = (d_far[0], window(dq, d_far[1], jobs("back_keys", l)))
+        total, *d_far = keys_back(*d_far, jobs("back_hop", l))
+        d_far = window(total, d_far, jobs("back_keys", l))
         d_qkv, keep, send = join_call(dq, own, d_far, tables, w_qkv, l, kv)
         value["d_qkv", l] = d_qkv
         send = window(d_far[1], send, jobs("back_join", l))
@@ -728,12 +730,12 @@
         if l > 0:
             value["down_in", l - 1] = gather_rows(flow.astype(BF), jobs("back_all2", l))
     final = gather_rows(bf16_of(flow), jobs("back_all2", 0))
-    for job in (s_down, g_attn[0], s_attn[0]):
+    for job in (s_both, s_tail):
         job.out = job.raw = job.make(None)
     input_grad = to_absolute(final, t).astype(F32)
 
     gain_grads = jnp.stack([gains[0][0], gains[1][0], gains[0][1], gains[1][1]])
-    gain_grads = sum_everywhere(after(gain_grads, g_attn[0].raw))
+    gain_grads = sum_everywhere(after(gain_grads, g_tail.raw))
     width = gain_grads.shape[1] // n
     gain_grads = lax.dynamic_slice_in_dim(gain_grads, lax.axis_index("dp") * width, width, 1)
     norm_attn_grad, norm_mlp_grad = gain_grads[:LAYERS], gain_grads[LAYERS:]
@@ -743,6 +745,7 @@
 
     units = w_gate.shape[2]
     a, b, c = heads * HD, 2 * heads * HD, (2 * heads + kv) * HD
+    d = c + kv * HD
     early = (
         hidden_out,
         input_grad,
@@ -750,17 +753,17 @@
         norm_mlp_grad,
         stack([s_both.out[:, :units], s_gate.out]),
         stack([s_both.out[:, units:], s_more.out[:, :units]]),
-        stack([s_down.out, s_more.out[:, units:]], True),
     )
-    *early, s_attn[0].out = need(*early, s_attn[0].out)
-    attn = lambda start, stop: [job.out[:, start:stop] for job in s_attn]
+    *early, s_tail.out = need(*early, s_tail.out)
+    attn = lambda start, stop: [job.out[:, start:stop] for job in (s_tail, s_attn)]
     return (
         *early[:4],
         stack(attn(a, b)),
         stack(attn(b, c)),
-        stack(attn(c, None)),
+        stack(attn(c, d)),
         stack(attn(0, a), True),
         *early[4:],
+        stack([s_tail.out[:, d:], s_more.out[:, units:]], True),
     )
 
 

time: 639 us -> 631 us (0.987)
  starting transfers between devices: 86 us -> 75.5 us
  waiting for transfers between devices: 274 us -> 284 us
  local copies, waits for them, and re-layouts: 62 us -> 54.3 us
    reduce_scatter x4 -> x5, waiting for transfers between devices: 17.7 us -> 37.6 us  [scatter_grad(): lax.psum_scatter(grad.astype(BF), 'dp', scatter_dimension=0, tiled=True,...]
    ppermute x75, waiting for transfers between devices: 190 us -> 209 us  [swap(): return lax.ppermute(block, axis, [(i, i ^ mask) for i in range(n)])]
    ppermute x4, waiting for transfers between devices: 29.3 us -> 11.9 us  [the longest x2 11.9 us: keys_back(): lax.ppermute(across, 'dp', [(i, i ^ 1) for i in late])]
    unnamed x8 -> x5, waiting for transfers between devices: 11.4 us -> 0.08 us
    ppermute x75, starting transfers between devices: 69.5 us -> 59.2 us  [swap(): return lax.ppermute(block, axis, [(i, i ^ mask) for i in range(n)])]
    unnamed x286 -> x262, local copies, waits for them, and re-layouts: 51 us -> 41 us
  transfers between devices with their start and end apart: 89 -> 88, of which waited for: 54 -> 56; matrix products, arithmetic and copies ran while one was open for 15% -> 14% of each run, Pallas kernels for 10% -> 10%
where the time goes in v4:
time: 631 us; the launch traced here: 621 us
  waiting for transfers between devices  284 us (45%)
  Pallas kernels  92.7 us (15%)
  starting transfers between devices  75.5 us (12%)
  other arithmetic  70.5 us (11%)
  local copies, waits for them, and re-layouts  54.3 us (9%)
  matrix products  28.4 us (5%)
  between operations  16 us (3%)
    ppermute x75, waiting for transfers between devices, swap(): return lax.ppermute(block, axis, [(i, i ^ mask) for i in range(n)])  209 us
    ppermute x75, starting transfers between devices, swap(): return lax.ppermute(block, axis, [(i, i ^ mask) for i in range(n)])  59.2 us
    unnamed x262, local copies, waits for them, and re-layouts  41 us
    reduce_scatter x5, waiting for transfers between devices, scatter_grad(): lax.psum_scatter(grad.astype(BF), 'dp', scatter_dimension=0, tiled=True,...  37.6 us
    dot_general x26, matrix products, mm(): lax.dot_general(a, b, (((ca,), (cb,)), ((), ())), preferred_element_type=...  28.4 us
    pallas_call x2, Pallas kernels, attn_bwd(): pl.pallas_call(attn_bwd_kernel, grid=(kv,), in_specs=place_specs + [table...  27.2 us
    ppermute x2, waiting for transfers between devices, keys_onward(): lax.ppermute(kv, 'dp', in_stretches(lambda s: (3, 1, None, None)[s], n))  20.8 us
    pallas_call x2, Pallas kernels, attn_fwd(): pl.pallas_call(attn_fwd_kernel, grid=(kv,), in_specs=place_specs + [q_spe...  17.5 us
  transfers between devices with their start and end apart: 88, of which 56 were waited for; matrix products, arithmetic and copies ran while one was open for 14% of the time, Pallas kernels for 10%

profile of v4, /device:TPU:0, one launch (start us, length us, event | category | flops | bytes accessed | tf_op | source)
XLA Modules:
  0.0 621.4 jit_solution(13419819580885509525)
XLA Ops:
  30.7 8.4 %collective-permute-done.2.refs_6_.refs_7_ = bf16[384,512]{1,0:T(8,128)(2,1)} collective-permute-done((bf16[384,512]{1,0:T(8,128)(2,1)}, bf16[384,512]{1,0:T(8,128)(2,1)}, u32[]{:S(2)}, u32[]{:S(2)}) %collective-permute-start.2) | collective-permute-done | bytes 393248 | tf_op jit(solution)/shard_map/ppermute | solution.py:113
  47.2 9.2 %attention_forward.2 = (bf16[384,512]{1,0:T(8,128)(2,1)S(1)}, f32[2,1,1024]{2,1,0:T(1,128)S(1)}) custom-call(s32[4]{0:T(128)S(1)} %add_multiply_fusion.base_ref, s32[512,1]{1,0:T(8,128)S(1)} %copy.50.rows_ref, s32[1,512]{1,0:T(1,128)S(1)} %add_add_fusion.1.top_ref, s32[1,512]{1,0:T(1,128)S(1)} %bitcast.109, bf16[384,512]{1,0:T(8,128)(2,1)S(1)} %copy-done.62, ...), custom_call_target="tpu_custom_call" | custom-call | flops 12099999744 | bytes 11000000 | tf_op jit(solution)/shard_map/attention_forward/pallas_call | solution.py:352
  63.5 8.4 %collective-permute-done.6 = bf16[384,512]{1,0:T(8,128)(2,1)S(1)} collective-permute-done((bf16[384,512]{1,0:T(8,128)(2,1)S(1)}, bf16[384,512]{1,0:T(8,128)(2,1)S(1)}, u32[]{:S(2)}, u32[]{:S(2)}) %collective-permute-start.6) | collective-permute-done | bytes 393248 | tf_op jit(solution)/shard_map/ppermute | solution.py:61
  75.3 9.1 %collective-permute-done.8 = bf16[768,256]{1,0:T(8,128)(2,1)S(1)} collective-permute-done((bf16[768,256]{1,0:T(8,128)(2,1)S(1)}, bf16[768,256]{1,0:T(8,128)(2,1)S(1)}, u32[]{:S(2)}, u32[]{:S(2)}) %collective-permute-start.8) | collective-permute-done | bytes 393248 | tf_op jit(solution)/shard_map/ppermute | solution.py:61
  87.7 7.9 %feed_forward.2 = (f32[512,1024]{1,0:T(8,128)S(1)}, f32[512,1024]{1,0:T(8,128)S(1)}, bf16[512,1024]{1,0:T(8,128)(2,1)S(1)}, f32[256,1536]{1,0:T(8,128)S(1)}, bf16[256,1536]{1,0:T(8,128)(2,1)S(1)}) custom-call(bf16[512,1536]{1,0:T(8,128)(2,1)S(1)} %pad_maximum_fusion.6.x_ref, bf16[2,1536,1024]{2,1,0:T(8,128)(2,1)S(1)} %bitcast.114, ...), custom_call_target="tpu_custom_call" | custom-call | flops 8800000000 | bytes 8000000 | tf_op jit(solution)/shard_map/feed_forward/pallas_call | solution.py:237
  101.5 9.8 %collective-permute-done.11 = bf16[128,1536]{1,0:T(8,128)(2,1)S(1)} collective-permute-done((bf16[128,1536]{1,0:T(8,128)(2,1)S(1)}, bf16[128,1536]{1,0:T(8,128)(2,1)S(1)}, u32[]{:S(2)}, u32[]{:S(2)}) %collective-permute-start.11) | collective-permute-done | bytes 393248 | tf_op jit(solution)/shard_map/ppermute | solution.py:61
  116.2 9.5 %collective-permute-done.13 = bf16[128,1536]{1,0:T(8,128)(2,1)S(1)} collective-permute-done((bf16[128,1536]{1,0:T(8,128)(2,1)S(1)}, bf16[128,1536]{1,0:T(8,128)(2,1)S(1)}, u32[]{:S(2)}, u32[]{:S(2)}) %collective-permute-start.13) | collective-permute-done | bytes 393248 | tf_op jit(solution)/shard_map/ppermute | solution.py:61
  137.3 12.4 %collective-permute-done.18.refs_6_.refs_7_ = bf16[384,512]{1,0:T(8,128)(2,1)S(1)} collective-permute-done((bf16[384,512]{1,0:T(8,128)(2,1)S(1)}, bf16[384,512]{1,0:T(8,128)(2,1)S(1)}, u32[]{:S(2)}, u32[]{:S(2)}) %collective-permute-start.18) | collective-permute-done | bytes 393248 | tf_op jit(solution)/shard_map/ppermute | solution.py:113
  156.9 8.3 %attention_forward.3 = (bf16[384,512]{1,0:T(8,128)(2,1)S(1)}, f32[2,1,1024]{2,1,0:T(1,128)S(1)}) custom-call(s32[4]{0:T(128)S(1)} %add_multiply_fusion.base_ref, s32[512,1]{1,0:T(8,128)S(1)} %copy.50.rows_ref, s32[1,512]{1,0:T(1,128)S(1)} %add_add_fusion.1.top_ref, s32[1,512]{1,0:T(1,128)S(1)} %bitcast.110, bf16[384,512]{1,0:T(8,128)(2,1)S(1)} %get-tuple-element.245.q_ref, ...), custom_call_target="tpu_custom_call" | custom-call | flops 12099999744 | bytes 11000000 | tf_op jit(solution)/shard_map/attention_forward/pallas_call | solution.py:352
  171.5 8.0 %collective-permute-done.22 = bf16[384,512]{1,0:T(8,128)(2,1)S(1)} collective-permute-done((bf16[384,512]{1,0:T(8,128)(2,1)S(1)}, bf16[384,512]{1,0:T(8,128)(2,1)S(1)}, u32[]{:S(2)}, u32[]{:S(2)}) %collective-permute-start.22) | collective-permute-done | bytes 393248 | tf_op jit(solution)/shard_map/ppermute | solution.py:61
  182.3 8.5 %collective-permute-done.24 = bf16[768,256]{1,0:T(8,128)(2,1)S(1)} collective-permute-done((bf16[768,256]{1,0:T(8,128)(2,1)S(1)}, bf16[768,256]{1,0:T(8,128)(2,1)S(1)}, u32[]{:S(2)}, u32[]{:S(2)}) %collective-permute-start.24) | collective-permute-done | bytes 393248 | tf_op jit(solution)/shard_map/ppermute | solution.py:61
  194.1 8.0 %feed_forward.3 = (f32[512,1024]{1,0:T(8,128)S(1)}, f32[512,1024]{1,0:T(8,128)S(1)}, bf16[512,1024]{1,0:T(8,128)(2,1)S(1)}, f32[256,1536]{1,0:T(8,128)S(1)}, bf16[256,1536]{1,0:T(8,128)(2,1)S(1)}) custom-call(bf16[512,1536]{1,0:T(8,128)(2,1)S(1)} %pad_maximum_fusion.8.x_ref, bf16[2,1536,1024]{2,1,0:T(8,128)(2,1)S(1)} %bitcast.116, ...), custom_call_target="tpu_custom_call" | custom-call | flops 8800000000 | bytes 8000000 | tf_op jit(solution)/shard_map/feed_forward/pallas_call | solution.py:237
  205.0 8.2 %feed_forward_back.2 = (bf16[512,1024]{1,0:T(8,128)(2,1)S(1)}, bf16[512,1024]{1,0:T(8,128)(2,1)S(1)}, f32[256,1536]{1,0:T(8,128)S(1)}, bf16[256,1536]{1,0:T(8,128)(2,1)S(1)}) custom-call(bf16[512,1536]{1,0:T(8,128)(2,1)S(1)} %copy-done.10, bf16[2,1024,1536]{2,1,0:T(8,128)(2,1)S(1)} %copy-done.36, bf16[2,1536,1024]{2,1,0:T(8,128)(2,1)S(1)} %bitcast.116, ...), custom_call_target="tpu_custom_call" | custom-call | flops 9900000256 | bytes 9000000 | tf_op jit(solution)/shard_map/feed_forward_back/pallas_call | solution.py:274
  218.0 9.6 %collective-permute-done.27 = bf16[128,1536]{1,0:T(8,128)(2,1)S(1)} collective-permute-done((bf16[128,1536]{1,0:T(8,128)(2,1)S(1)}, bf16[128,1536]{1,0:T(8,128)(2,1)S(1)}, u32[]{:S(2)}, u32[]{:S(2)}) %collective-permute-start.27) | collective-permute-done | bytes 393248 | tf_op jit(solution)/shard_map/ppermute | solution.py:61
  234.4 9.5 %collective-permute-done.29 = bf16[128,1536]{1,0:T(8,128)(2,1)S(1)} collective-permute-done((bf16[128,1536]{1,0:T(8,128)(2,1)S(1)}, bf16[128,1536]{1,0:T(8,128)(2,1)S(1)}, u32[]{:S(2)}, u32[]{:S(2)}) %collective-permute-start.29) | collective-permute-done | bytes 393248 | tf_op jit(solution)/shard_map/ppermute | solution.py:61
  251.7 13.6 %attention_backward.2 = (bf16[384,512]{1,0:T(8,128)(2,1)S(1)}, f32[2,192,512]{2,1,0:T(8,128)S(1)}, bf16[2,192,512]{2,1,0:T(8,128)(2,1)}, bf16[2,192,512]{2,1,0:T(8,128)(2,1)S(1)}, bf16[2,192,512]{2,1,0:T(8,128)(2,1)S(1)}) custom-call(s32[4]{0:T(128)S(1)} %add_multiply_fusion.base_ref, s32[512,1]{1,0:T(8,128)S(1)} %copy.50.rows_ref, ...), custom_call_target="tpu_custom_call" | custom-call | flops 18150000640 | bytes 16500000 | tf_op jit(solution)/shard_map/attention_backward/pallas_call | solution.py:413
  265.3 6.1 collective-permute-done.32
  278.3 7.1 %collective-permute-done.35 = bf16[2,192,512]{2,1,0:T(8,128)(2,1)S(1)} collective-permute-done((bf16[2,192,512]{2,1,0:T(8,128)(2,1)S(1)}, bf16[2,192,512]{2,1,0:T(8,128)(2,1)S(1)}, u32[]{:S(2)}, u32[]{:S(2)}) %collective-permute-start.35) | collective-permute-done | bytes 393248 | tf_op jit(solution)/shard_map/ppermute | solution.py:121
  291.4 6.2 collective-permute-done.42
  327.5 7.6 %collective-permute-done.45 = bf16[128,1536]{1,0:T(8,128)(2,1)S(1)} collective-permute-done((bf16[128,1536]{1,0:T(8,128)(2,1)S(1)}, bf16[128,1536]{1,0:T(8,128)(2,1)S(1)}, u32[]{:S(2)}, u32[]{:S(2)}) %collective-permute-start.45) | collective-permute-done | bytes 393248 | tf_op jit(solution)/shard_map/ppermute | solution.py:61
  368.6 8.2 %feed_forward_back.3 = (bf16[512,1024]{1,0:T(8,128)(2,1)S(1)}, bf16[512,1024]{1,0:T(8,128)(2,1)S(1)}, f32[256,1536]{1,0:T(8,128)S(1)}, bf16[256,1536]{1,0:T(8,128)(2,1)S(1)}) custom-call(bf16[512,1536]{1,0:T(8,128)(2,1)S(1)} %pad_maximum_fusion.11.x_ref, bf16[2,1024,1536]{2,1,0:T(8,128)(2,1)S(1)} %copy-done.37, bf16[2,1536,1024]{2,1,0:T(8,128)(2,1)S(1)} %copy-done.35, ...), custom_call_target="tpu_custom_call" | custom-call | flops 9900000256 | bytes 9000000 | tf_op jit(solution)/shard_map/feed_forward_back/pallas_call | solution.py:274
  384.5 17.5 %collective-permute-done.54 = bf16[256,768]{1,0:T(8,128)(2,1)S(1)} collective-permute-done((bf16[256,768]{1,0:T(8,128)(2,1)S(1)}, bf16[256,768]{1,0:T(8,128)(2,1)S(1)}, u32[]{:S(2)}, u32[]{:S(2)}) %collective-permute-start.54) | collective-permute-done | bytes 393248 | tf_op jit(solution)/shard_map/ppermute | solution.py:61
  433.3 13.6 %attention_backward.3 = (bf16[384,512]{1,0:T(8,128)(2,1)S(1)}, f32[2,192,512]{2,1,0:T(8,128)S(1)}, bf16[2,192,512]{2,1,0:T(8,128)(2,1)S(1)}, bf16[2,192,512]{2,1,0:T(8,128)(2,1)S(1)}, bf16[2,192,512]{2,1,0:T(8,128)(2,1)S(1)}) custom-call(s32[4]{0:T(128)S(1)} %add_multiply_fusion.base_ref, s32[512,1]{1,0:T(8,128)S(1)} %copy.50.rows_ref, ...), custom_call_target="tpu_custom_call" | custom-call | flops 18150000640 | bytes 16500000 | tf_op jit(solution)/shard_map/attention_backward/pallas_call | solution.py:413
  447.0 7.5 %collective-permute-done.61 = bf16[256,1024]{1,0:T(8,128)(2,1)S(1)} collective-permute-done((bf16[256,1024]{1,0:T(8,128)(2,1)S(1)}, bf16[256,1024]{1,0:T(8,128)(2,1)S(1)}, u32[]{:S(2)}, u32[]{:S(2)}) %collective-permute-start.61) | collective-permute-done | bytes 524320 | tf_op jit(solution)/shard_map/ppermute | solution.py:61
  462.5 4.8 collective-permute-done.64
  478.9 8.7 %collective-permute-done.63.one_ref = bf16[2,192,512]{2,1,0:T(8,128)(2,1)S(1)} collective-permute-done((bf16[2,192,512]{2,1,0:T(8,128)(2,1)}, bf16[2,192,512]{2,1,0:T(8,128)(2,1)S(1)}, u32[]{:S(2)}, u32[]{:S(2)}) %collective-permute-start.63) | collective-permute-done | bytes 393248 | tf_op jit(solution)/shard_map/ppermute | solution.py:61
  487.6 6.3 %collective-permute-done.67 = bf16[768,256]{1,0:T(8,128)(2,1)S(1)} collective-permute-done((bf16[768,256]{1,0:T(8,128)(2,1)}, bf16[768,256]{1,0:T(8,128)(2,1)S(1)}, u32[]{:S(2)}, u32[]{:S(2)}) %collective-permute-start.67) | collective-permute-done | bytes 393248 | tf_op jit(solution)/shard_map/ppermute | solution.py:61
  511.5 7.9 %collective-permute-done.72 = bf16[256,768]{1,0:T(8,128)(2,1)S(1)} collective-permute-done((bf16[256,768]{1,0:T(8,128)(2,1)S(1)}, bf16[256,768]{1,0:T(8,128)(2,1)S(1)}, u32[]{:S(2)}, u32[]{:S(2)}) %collective-permute-start.72) | collective-permute-done | bytes 393248 | tf_op jit(solution)/shard_map/ppermute | solution.py:61
  519.5 7.3 %collective-permute-done.71 = bf16[256,768]{1,0:T(8,128)(2,1)S(1)} collective-permute-done((bf16[256,768]{1,0:T(8,128)(2,1)S(1)}, bf16[256,768]{1,0:T(8,128)(2,1)S(1)}, u32[]{:S(2)}, u32[]{:S(2)}) %collective-permute-start.71) | collective-permute-done | bytes 393248 | tf_op jit(solution)/shard_map/ppermute | solution.py:61
  545.7 7.2 %collective-permute-done.79 = f32[4,1536]{1,0:T(4,128)} collective-permute-done((f32[4,1536]{1,0:T(4,128)}, f32[4,1536]{1,0:T(4,128)}, u32[]{:S(2)}, u32[]{:S(2)}) %collective-permute-start.79) | collective-permute-done | bytes 24608 | tf_op jit(solution)/shard_map/ppermute | solution.py:61
  557.5 6.1 collective-permute-start.81
  578.1 29.7 %reduce-scatter.14.cloned.1.call-done = bf16[192,2176]{1,0:T(8,128)(2,1)} async-done(((bf16[768,2176]{1,0:T(8,128)(2,1)}), bf16[192,2176]{1,0:T(8,128)(2,1)}) %reduce-scatter.14.cloned.1.call-update) | async-done | bytes 835600 | tf_op jit(solution)/shard_map/reduce_scatter | solution.py:130
  (588 shorter events, 305.0 us)
Async XLA Ops:
  7.2 349.4 %reduce-scatter.6.cloned.1.call-start = ((), (), s32[]{:S(2)}) async-start(), calls=%async_computation.5 | async-start | bytes 1966080 | tf_op jit(solution)/shard_map/reduce_scatter | solution.py:130
  21.5 17.5 %collective-permute-start.2 = (bf16[384,512]{1,0:T(8,128)(2,1)}, bf16[384,512]{1,0:T(8,128)(2,1)}, u32[]{:S(2)}, u32[]{:S(2)}) collective-permute-start(bf16[384,512]{1,0:T(8,128)(2,1)} %get-tuple-element.218.refs_0_.refs_1_), channel_id=1, source_target_pairs={{8,20},{12,16},{24,4},{28,0},{9,21},{13,17},{25,5},{29,1},{10,22},... | collective-permute-start | bytes 1179656 | tf_op jit(solution)/shard_map/ppermute | solution.py:113
  22.8 21.7 %collective-permute-start = (bf16[384,512]{1,0:T(8,128)(2,1)}, bf16[384,512]{1,0:T(8,128)(2,1)}, u32[]{:S(2)}, u32[]{:S(2)}) collective-permute-start(bf16[384,512]{1,0:T(8,128)(2,1)} %get-tuple-element.218.refs_0_.refs_1_), channel_id=1, source_target_pairs={{0,4},{4,0},{8,12},{12,8},{16,20},{20,16},{24,28},{28,24},{1,5},{5... | collective-permute-start | bytes 1179656 | tf_op jit(solution)/shard_map/ppermute | solution.py:61
  25.8 21.4 %collective-permute-start.1 = (bf16[384,512]{1,0:T(8,128)(2,1)}, bf16[384,512]{1,0:T(8,128)(2,1)}, u32[]{:S(2)}, u32[]{:S(2)}) collective-permute-start(bf16[384,512]{1,0:T(8,128)(2,1)} %get-tuple-element.218.refs_0_.refs_1_), channel_id=1, source_target_pairs={{8,16},{12,20},{24,0},{28,4},{9,17},{13,21},{25,1},{29,5},{10,18},... | collective-permute-start | bytes 1179656 | tf_op jit(solution)/shard_map/ppermute | solution.py:114
  39.0 17.4 %collective-permute-start.3 = (bf16[768,256]{1,0:T(8,128)(2,1)S(1)}, bf16[768,256]{1,0:T(8,128)(2,1)}, u32[]{:S(2)}, u32[]{:S(2)}) collective-permute-start(bf16[768,256]{1,0:T(8,128)(2,1)S(1)} %get-tuple-element.225), channel_id=1, source_target_pairs={{0,4},{4,0},{8,12},{12,8},{16,20},{20,16},{24,28},{28,24},{1,5},{5... | collective-permute-start | bytes 1179656 | tf_op jit(solution)/shard_map/ppermute | solution.py:61
  133.2 16.6 %collective-permute-start.18 = (bf16[384,512]{1,0:T(8,128)(2,1)S(1)}, bf16[384,512]{1,0:T(8,128)(2,1)S(1)}, u32[]{:S(2)}, u32[]{:S(2)}) collective-permute-start(bf16[384,512]{1,0:T(8,128)(2,1)S(1)} %get-tuple-element.246.refs_0_.refs_1_), channel_id=1, source_target_pairs={{8,20},{12,16},{24,4},{28,0},{9,21},{13,17},{25,5},{29,1},{10,22},... | collective-permute-start | bytes 1179656 | tf_op jit(solution)/shard_map/ppermute | solution.py:113
  134.5 20.5 %collective-permute-start.16 = (bf16[384,512]{1,0:T(8,128)(2,1)S(1)}, bf16[384,512]{1,0:T(8,128)(2,1)S(1)}, u32[]{:S(2)}, u32[]{:S(2)}) collective-permute-start(bf16[384,512]{1,0:T(8,128)(2,1)S(1)} %get-tuple-element.246.refs_0_.refs_1_), channel_id=1, source_target_pairs={{0,4},{4,0},{8,12},{12,8},{16,20},{20,16},{24,28},{28,24},{1,5},{5... | collective-permute-start | bytes 1179656 | tf_op jit(solution)/shard_map/ppermute | solution.py:61
  135.5 21.4 %collective-permute-start.17 = (bf16[384,512]{1,0:T(8,128)(2,1)S(1)}, bf16[384,512]{1,0:T(8,128)(2,1)S(1)}, u32[]{:S(2)}, u32[]{:S(2)}) collective-permute-start(bf16[384,512]{1,0:T(8,128)(2,1)S(1)} %get-tuple-element.246.refs_0_.refs_1_), channel_id=1, source_target_pairs={{8,16},{12,20},{24,0},{28,4},{9,17},{13,21},{25,1},{29,5},{10,18},... | collective-permute-start | bytes 1179656 | tf_op jit(solution)/shard_map/ppermute | solution.py:114
  248.6 25.7 %collective-permute-start.40 = (bf16[256,1536]{1,0:T(8,128)(2,1)S(1)}, bf16[256,1536]{1,0:T(8,128)(2,1)S(1)}, u32[]{:S(2)}, u32[]{:S(2)}) collective-permute-start(bf16[256,1536]{1,0:T(8,128)(2,1)S(1)} %get-tuple-element.304), channel_id=1, source_target_pairs={{0,1},{1,0},{2,3},{3,2},{4,5},{5,4},{6,7},{7,6},{8,9},{9,8},{10,11... | collective-permute-start | bytes 2359304 | tf_op jit(solution)/shard_map/ppermute | solution.py:61
  248.9 22.5 %collective-permute-start.33 = (bf16[256,1024]{1,0:T(8,128)(2,1)S(1)}, bf16[256,1024]{1,0:T(8,128)(2,1)S(1)}, u32[]{:S(2)}, u32[]{:S(2)}) collective-permute-start(bf16[256,1024]{1,0:T(8,128)(2,1)S(1)} %get-tuple-element.279), channel_id=1, source_target_pairs={{0,4},{4,0},{8,12},{12,8},{16,20},{20,16},{24,28},{28,24},{1,5},{5... | collective-permute-start | bytes 1572872 | tf_op jit(solution)/shard_map/ppermute | solution.py:61
  249.9 21.5 %collective-permute-start.32 = (bf16[768,256]{1,0:T(8,128)(2,1)S(1)}, bf16[768,256]{1,0:T(8,128)(2,1)S(1)}, u32[]{:S(2)}, u32[]{:S(2)}) collective-permute-start(bf16[768,256]{1,0:T(8,128)(2,1)S(1)} %get-tuple-element.277), channel_id=1, source_target_pairs={{0,4},{4,0},{8,12},{12,8},{16,20},{20,16},{24,28},{28,24},{1,5},{5... | collective-permute-start | bytes 1179656 | tf_op jit(solution)/shard_map/ppermute | solution.py:61
  277.2 23.5 %collective-permute-start.34 = (bf16[2,192,512]{2,1,0:T(8,128)(2,1)}, bf16[2,192,512]{2,1,0:T(8,128)(2,1)}, u32[]{:S(2)}, u32[]{:S(2)}) collective-permute-start(bf16[2,192,512]{2,1,0:T(8,128)(2,1)} %get-tuple-element.282), channel_id=1, source_target_pairs={{0,4},{4,0},{8,12},{12,8},{16,20},{20,16},{24,28},{28,24},{1,5},{5... | collective-permute-start | bytes 1179656 | tf_op jit(solution)/shard_map/ppermute | solution.py:61
  298.6 17.7 %collective-permute-start.43 = (bf16[256,1536]{1,0:T(8,128)(2,1)}, bf16[256,1536]{1,0:T(8,128)(2,1)}, u32[]{:S(2)}, u32[]{:S(2)}) collective-permute-start(bf16[256,1536]{1,0:T(8,128)(2,1)} %pad_maximum_fusion.27), channel_id=1, source_target_pairs={{0,1},{1,0},{2,3},{3,2},{4,5},{5,4},{6,7},{7,6},{8,9},{9,8},{10,11... | collective-permute-start | bytes 2359304 | tf_op jit(solution)/shard_map/ppermute | solution.py:61
  320.2 26.0 %collective-permute-start.49 = (bf16[768,256]{1,0:T(8,128)(2,1)}, bf16[768,256]{1,0:T(8,128)(2,1)}, u32[]{:S(2)}, u32[]{:S(2)}) collective-permute-start(bf16[768,256]{1,0:T(8,128)(2,1)} %collective-permute-done.3), channel_id=1, source_target_pairs={{0,1},{1,0},{2,3},{3,2},{4,5},{5,4},{6,7},{7,6},{8,9},{9,8},{10,11... | collective-permute-start | bytes 1179656 | tf_op jit(solution)/shard_map/ppermute | solution.py:61
  320.7 95.3 %reduce-scatter.8.cloned.1.call-start = ((), (), s32[]{:S(2)}) async-start(), calls=%async_computation.6 | async-start | bytes 3932160 | tf_op jit(solution)/shard_map/reduce_scatter | solution.py:130
  358.6 114.6 %reduce-scatter.10.cloned.1.call-start = ((), (), s32[]{:S(2)}) async-start(), calls=%async_computation.7 | async-start | bytes 2211840 | tf_op jit(solution)/shard_map/reduce_scatter | solution.py:130
  379.3 22.7 %collective-permute-start.55 = (bf16[256,1024]{1,0:T(8,128)(2,1)S(1)}, bf16[256,1024]{1,0:T(8,128)(2,1)}, u32[]{:S(2)}, u32[]{:S(2)}) collective-permute-start(bf16[256,1024]{1,0:T(8,128)(2,1)S(1)} %get-tuple-element.332), channel_id=1, source_target_pairs={{0,4},{4,0},{8,12},{12,8},{16,20},{20,16},{24,28},{28,24},{1,5},{5... | collective-permute-start | bytes 1572872 | tf_op jit(solution)/shard_map/ppermute | solution.py:61
  380.2 21.8 %collective-permute-start.54 = (bf16[256,768]{1,0:T(8,128)(2,1)S(1)}, bf16[256,768]{1,0:T(8,128)(2,1)S(1)}, u32[]{:S(2)}, u32[]{:S(2)}) collective-permute-start(bf16[256,768]{1,0:T(8,128)(2,1)S(1)} %get-tuple-element.330), channel_id=1, source_target_pairs={{0,4},{4,0},{8,12},{12,8},{16,20},{20,16},{24,28},{28,24},{1,5},{5... | collective-permute-start | bytes 1179656 | tf_op jit(solution)/shard_map/ppermute | solution.py:61
  381.4 20.6 %collective-permute-start.53 = (bf16[128,1536]{1,0:T(8,128)(2,1)S(1)}, bf16[128,1536]{1,0:T(8,128)(2,1)S(1)}, u32[]{:S(2)}, u32[]{:S(2)}) collective-permute-start(bf16[128,1536]{1,0:T(8,128)(2,1)S(1)} %add_convert_fusion.10), channel_id=1, source_target_pairs={{0,2},{1,3},{2,0},{3,1},{4,6},{5,7},{6,4},{7,5},{8,10},{9,11},{10,... | collective-permute-start | bytes 1179656 | tf_op jit(solution)/shard_map/ppermute | solution.py:61
  381.7 41.1 %collective-permute-start.65 = (bf16[768,256]{1,0:T(8,128)(2,1)}, bf16[768,256]{1,0:T(8,128)(2,1)}, u32[]{:S(2)}, u32[]{:S(2)}) collective-permute-start(bf16[768,256]{1,0:T(8,128)(2,1)} %collective-permute-done.19), channel_id=1, source_target_pairs={{0,1},{1,0},{2,3},{3,2},{4,5},{5,4},{6,7},{7,6},{8,9},{9,8},{10,11... | collective-permute-start | bytes 1179656 | tf_op jit(solution)/shard_map/ppermute | solution.py:61
  381.7 25.7 %collective-permute-start.59 = (bf16[768,256]{1,0:T(8,128)(2,1)S(1)}, bf16[768,256]{1,0:T(8,128)(2,1)S(1)}, u32[]{:S(2)}, u32[]{:S(2)}) collective-permute-start(bf16[768,256]{1,0:T(8,128)(2,1)S(1)} %copy-done.109), channel_id=1, source_target_pairs={{0,1},{1,0},{2,3},{3,2},{4,5},{5,4},{6,7},{7,6},{8,9},{9,8},{10,11... | collective-permute-start | bytes 1179656 | tf_op jit(solution)/shard_map/ppermute | solution.py:61
  425.6 112.7 %reduce-scatter.12.cloned.1.call-start = ((), (), s32[]{:S(2)}) async-start(), calls=%async_computation.8 | async-start | bytes 3932160 | tf_op jit(solution)/shard_map/reduce_scatter | solution.py:130
  428.9 18.2 %collective-permute-start.62 = (bf16[256,1024]{1,0:T(8,128)(2,1)S(1)}, bf16[256,1024]{1,0:T(8,128)(2,1)S(1)}, u32[]{:S(2)}, u32[]{:S(2)}) collective-permute-start(bf16[256,1024]{1,0:T(8,128)(2,1)S(1)} %copy-done.101), channel_id=1, source_target_pairs={{0,4},{4,0},{8,12},{12,8},{16,20},{20,16},{24,28},{28,24},{1,5},{5... | collective-permute-start | bytes 1572872 | tf_op jit(solution)/shard_map/ppermute | solution.py:61
  430.2 24.3 %collective-permute-start.61 = (bf16[256,1024]{1,0:T(8,128)(2,1)S(1)}, bf16[256,1024]{1,0:T(8,128)(2,1)S(1)}, u32[]{:S(2)}, u32[]{:S(2)}) collective-permute-start(bf16[256,1024]{1,0:T(8,128)(2,1)S(1)} %copy-done.100), channel_id=1, source_target_pairs={{0,4},{4,0},{8,12},{12,8},{16,20},{20,16},{24,28},{28,24},{1,5},{5... | collective-permute-start | bytes 1572872 | tf_op jit(solution)/shard_map/ppermute | solution.py:61
  475.2 132.5 %reduce-scatter.14.cloned.1.call-start = ((), (), s32[]{:S(2)}) async-start(), calls=%async_computation.9 | async-start | bytes 4177920 | tf_op jit(solution)/shard_map/reduce_scatter | solution.py:130
  476.5 17.4 %collective-permute-start.67 = (bf16[768,256]{1,0:T(8,128)(2,1)}, bf16[768,256]{1,0:T(8,128)(2,1)S(1)}, u32[]{:S(2)}, u32[]{:S(2)}) collective-permute-start(bf16[768,256]{1,0:T(8,128)(2,1)} %copy-done.50), channel_id=1, source_target_pairs={{0,4},{4,0},{8,12},{12,8},{16,20},{20,16},{24,28},{28,24},{1,5},{5... | collective-permute-start | bytes 1179656 | tf_op jit(solution)/shard_map/ppermute | solution.py:61
  477.3 16.6 %collective-permute-start.66 = (bf16[2,192,512]{2,1,0:T(8,128)(2,1)}, bf16[2,192,512]{2,1,0:T(8,128)(2,1)S(1)}, u32[]{:S(2)}, u32[]{:S(2)}) collective-permute-start(bf16[2,192,512]{2,1,0:T(8,128)(2,1)} %add_convert_fusion.9), channel_id=1, source_target_pairs={{0,24},{4,28},{16,8},{20,12},{1,25},{5,29},{17,9},{21,13},{2,26},{... | collective-permute-start | bytes 1179656 | tf_op jit(solution)/shard_map/ppermute | solution.py:124
  503.3 27.2 %collective-permute-start.76 = (bf16[768,256]{1,0:T(8,128)(2,1)S(1)}, bf16[768,256]{1,0:T(8,128)(2,1)S(1)}, u32[]{:S(2)}, u32[]{:S(2)}) collective-permute-start(bf16[768,256]{1,0:T(8,128)(2,1)S(1)} %copy-done.107), channel_id=1, source_target_pairs={{0,1},{1,0},{2,3},{3,2},{4,5},{5,4},{6,7},{7,6},{8,9},{9,8},{10,11... | collective-permute-start | bytes 1179656 | tf_op jit(solution)/shard_map/ppermute | solution.py:61
  504.1 24.7 %collective-permute-start.75 = (bf16[768,256]{1,0:T(8,128)(2,1)S(1)}, bf16[768,256]{1,0:T(8,128)(2,1)S(1)}, u32[]{:S(2)}, u32[]{:S(2)}) collective-permute-start(bf16[768,256]{1,0:T(8,128)(2,1)S(1)} %collective-permute-done.68), channel_id=1, source_target_pairs={{0,1},{1,0},{2,3},{3,2},{4,5},{5,4},{6,7},{7,6},{8,9},{9,8},{10,11... | collective-permute-start | bytes 1179656 | tf_op jit(solution)/shard_map/ppermute | solution.py:61
  505.7 21.1 %collective-permute-start.70 = (bf16[128,1536]{1,0:T(8,128)(2,1)S(1)}, bf16[128,1536]{1,0:T(8,128)(2,1)S(1)}, u32[]{:S(2)}, u32[]{:S(2)}) collective-permute-start(bf16[128,1536]{1,0:T(8,128)(2,1)S(1)} %add_convert_fusion.8), channel_id=1, source_target_pairs={{0,2},{1,3},{2,0},{3,1},{4,6},{5,7},{6,4},{7,5},{8,10},{9,11},{10,... | collective-permute-start | bytes 1179656 | tf_op jit(solution)/shard_map/ppermute | solution.py:61
  508.3 18.5 %collective-permute-start.71 = (bf16[256,768]{1,0:T(8,128)(2,1)S(1)}, bf16[256,768]{1,0:T(8,128)(2,1)S(1)}, u32[]{:S(2)}, u32[]{:S(2)}) collective-permute-start(bf16[256,768]{1,0:T(8,128)(2,1)S(1)} %get-tuple-element.389), channel_id=1, source_target_pairs={{0,4},{4,0},{8,12},{12,8},{16,20},{20,16},{24,28},{28,24},{1,5},{5... | collective-permute-start | bytes 1179656 | tf_op jit(solution)/shard_map/ppermute | solution.py:61
  541.1 22.5 %collective-permute-start.74 = (bf16[128,1536]{1,0:T(8,128)(2,1)S(1)}, bf16[128,1536]{1,0:T(8,128)(2,1)}, u32[]{:S(2)}, u32[]{:S(2)}) collective-permute-start(bf16[128,1536]{1,0:T(8,128)(2,1)S(1)} %copy-done.80), channel_id=1, source_target_pairs={{0,2},{1,3},{2,0},{3,1},{4,6},{5,7},{6,4},{7,5},{8,10},{9,11},{10,... | collective-permute-start | bytes 1179656 | tf_op jit(solution)/shard_map/ppermute | solution.py:61
  (186 other events, 1791.4 us)
Sparse Core Ops, SparseCore 0:
  320.8 32.0 reduce-scatter.5
  358.7 57.2 reduce-scatter.7
  425.8 37.9 reduce-scatter.9
  475.3 62.9 reduce-scatter.11
  540.6 67.0 reduce-scatter.13

commit v5 on v4

--- a/solution.py
+++ b/solution.py
@@ -624,7 +624,7 @@
     act_right = [Sent(later("act", l), 2) for l in layers]
     mixed_right = [Sent(later("mixed", l), 1) for l in layers]
     gate_right = [Sent(later("gate", l), 2) for l in layers]
-    up_right = [Sent(later("up", l), 2) for l in layers]
+    up_right = [Sent(later("up", l), 4 - 2 * l) for l in layers]
     qkv_right = [Sent(later("d_qkv", l), 2) for l in layers]
     g_down = [product(down_left[l], act_right[l]) for l in layers]
     g_gate = [product(mlp_left[l], gate_right[l]) for l in layers]
@@ -660,8 +660,8 @@
         ("back_all2", 1): [out_left[1].send, g_more],
         ("back_mlp", 0): [qkv_right[1].sends[0], s_gate],
         ("back_sum1", 0): [qkv_right[1].sends[1], gate_right[0].sends[0], down_left[0].turn],
-        ("back_all1", 0): [gate_right[0].sends[1], g_attn, s_more],
-        ("back_attn", 0): [*up_right[0].sends],
+        ("back_all1", 0): [gate_right[0].sends[1], up_right[0].sends[0], g_attn, s_more],
+        ("back_attn", 0): up_right[0].sends[1:],
         ("back_hop", 0): [g_gate[0], out_left[0].turn],
         ("back_keys", 0): [down_left[0].send, g_both, s_attn],
         ("back_join", 0): [out_left[0].send],

time: 631 us -> 627 us (level)
    ppermute x75 -> x77, starting transfers between devices: 59.2 us -> 54.6 us  [swap(): return lax.ppermute(block, axis, [(i, i ^ mask) for i in range(n)])]
    ppermute x75 -> x77, waiting for transfers between devices: 209 us -> 212 us  [swap(): return lax.ppermute(block, axis, [(i, i ^ mask) for i in range(n)])]
    unnamed x262 -> x270, local copies, waits for them, and re-layouts: 41 us -> 40.1 us
  transfers between devices with their start and end apart: 88 -> 90, of which waited for: 56 -> 59; matrix products, arithmetic and copies ran while one was open for 14% -> 13% of each run, Pallas kernels for 10% -> 10%
where the time goes in v5:
time: 627 us; the launch traced here: 617 us
  waiting for transfers between devices  286 us (46%)
  Pallas kernels  92.8 us (15%)
  other arithmetic  71.6 us (11%)
  starting transfers between devices  70.2 us (11%)
  local copies, waits for them, and re-layouts  52.2 us (8%)
  matrix products  28.3 us (5%)
  between operations  16.1 us (3%)
    ppermute x77, waiting for transfers between devices, swap(): return lax.ppermute(block, axis, [(i, i ^ mask) for i in range(n)])  212 us
    ppermute x77, starting transfers between devices, swap(): return lax.ppermute(block, axis, [(i, i ^ mask) for i in range(n)])  54.6 us
    unnamed x270, local copies, waits for them, and re-layouts  40.1 us
    reduce_scatter x5, waiting for transfers between devices, scatter_grad(): lax.psum_scatter(grad.astype(BF), 'dp', scatter_dimension=0, tiled=True,...  34.9 us
    dot_general x26, matrix products, mm(): lax.dot_general(a, b, (((ca,), (cb,)), ((), ())), preferred_element_type=...  28.3 us
    pallas_call x2, Pallas kernels, attn_bwd(): pl.pallas_call(attn_bwd_kernel, grid=(kv,), in_specs=place_specs + [table...  27.2 us
    ppermute x2, waiting for transfers between devices, keys_onward(): lax.ppermute(kv, 'dp', in_stretches(lambda s: (3, 1, None, None)[s], n))  20.8 us
    pallas_call x2, Pallas kernels, attn_fwd(): pl.pallas_call(attn_fwd_kernel, grid=(kv,), in_specs=place_specs + [q_spe...  17.5 us
  transfers between devices with their start and end apart: 90, of which 59 were waited for; matrix products, arithmetic and copies ran while one was open for 13% of the time, Pallas kernels for 10%

profile of v5, /device:TPU:0, one launch (start us, length us, event | category | flops | bytes accessed | tf_op | source)
XLA Modules:
  0.0 617.5 jit_solution(11438666711656141851)
XLA Ops:
  30.7 8.4 %collective-permute-done.2.refs_6_.refs_7_ = bf16[384,512]{1,0:T(8,128)(2,1)} collective-permute-done((bf16[384,512]{1,0:T(8,128)(2,1)}, bf16[384,512]{1,0:T(8,128)(2,1)}, u32[]{:S(2)}, u32[]{:S(2)}) %collective-permute-start.2) | collective-permute-done | bytes 393248 | tf_op jit(solution)/shard_map/ppermute | solution.py:113
  47.2 9.2 %attention_forward.2 = (bf16[384,512]{1,0:T(8,128)(2,1)S(1)}, f32[2,1,1024]{2,1,0:T(1,128)S(1)}) custom-call(s32[4]{0:T(128)S(1)} %add_multiply_fusion.base_ref, s32[512,1]{1,0:T(8,128)S(1)} %copy.50.rows_ref, s32[1,512]{1,0:T(1,128)S(1)} %add_add_fusion.1.top_ref, s32[1,512]{1,0:T(1,128)S(1)} %bitcast.109, bf16[384,512]{1,0:T(8,128)(2,1)S(1)} %copy-done.62, ...), custom_call_target="tpu_custom_call" | custom-call | flops 12099999744 | bytes 11000000 | tf_op jit(solution)/shard_map/attention_forward/pallas_call | solution.py:352
  63.5 8.4 %collective-permute-done.6 = bf16[384,512]{1,0:T(8,128)(2,1)S(1)} collective-permute-done((bf16[384,512]{1,0:T(8,128)(2,1)S(1)}, bf16[384,512]{1,0:T(8,128)(2,1)S(1)}, u32[]{:S(2)}, u32[]{:S(2)}) %collective-permute-start.6) | collective-permute-done | bytes 393248 | tf_op jit(solution)/shard_map/ppermute | solution.py:61
  75.2 9.1 %collective-permute-done.8 = bf16[768,256]{1,0:T(8,128)(2,1)S(1)} collective-permute-done((bf16[768,256]{1,0:T(8,128)(2,1)S(1)}, bf16[768,256]{1,0:T(8,128)(2,1)S(1)}, u32[]{:S(2)}, u32[]{:S(2)}) %collective-permute-start.8) | collective-permute-done | bytes 393248 | tf_op jit(solution)/shard_map/ppermute | solution.py:61
  87.7 7.9 %feed_forward.2 = (f32[512,1024]{1,0:T(8,128)S(1)}, f32[512,1024]{1,0:T(8,128)S(1)}, bf16[512,1024]{1,0:T(8,128)(2,1)S(1)}, f32[256,1536]{1,0:T(8,128)S(1)}, bf16[256,1536]{1,0:T(8,128)(2,1)S(1)}) custom-call(bf16[512,1536]{1,0:T(8,128)(2,1)S(1)} %pad_maximum_fusion.6.x_ref, bf16[2,1536,1024]{2,1,0:T(8,128)(2,1)S(1)} %bitcast.114, ...), custom_call_target="tpu_custom_call" | custom-call | flops 8800000000 | bytes 8000000 | tf_op jit(solution)/shard_map/feed_forward/pallas_call | solution.py:237
  101.4 9.8 %collective-permute-done.11 = bf16[128,1536]{1,0:T(8,128)(2,1)S(1)} collective-permute-done((bf16[128,1536]{1,0:T(8,128)(2,1)S(1)}, bf16[128,1536]{1,0:T(8,128)(2,1)S(1)}, u32[]{:S(2)}, u32[]{:S(2)}) %collective-permute-start.11) | collective-permute-done | bytes 393248 | tf_op jit(solution)/shard_map/ppermute | solution.py:61
  116.2 9.5 %collective-permute-done.13 = bf16[128,1536]{1,0:T(8,128)(2,1)S(1)} collective-permute-done((bf16[128,1536]{1,0:T(8,128)(2,1)S(1)}, bf16[128,1536]{1,0:T(8,128)(2,1)S(1)}, u32[]{:S(2)}, u32[]{:S(2)}) %collective-permute-start.13) | collective-permute-done | bytes 393248 | tf_op jit(solution)/shard_map/ppermute | solution.py:61
  137.3 12.4 %collective-permute-done.18.refs_6_.refs_7_ = bf16[384,512]{1,0:T(8,128)(2,1)S(1)} collective-permute-done((bf16[384,512]{1,0:T(8,128)(2,1)S(1)}, bf16[384,512]{1,0:T(8,128)(2,1)S(1)}, u32[]{:S(2)}, u32[]{:S(2)}) %collective-permute-start.18) | collective-permute-done | bytes 393248 | tf_op jit(solution)/shard_map/ppermute | solution.py:113
  150.8 4.2 collective-permute-done.16.refs_2_.refs_3_
  156.9 8.3 %attention_forward.3 = (bf16[384,512]{1,0:T(8,128)(2,1)S(1)}, f32[2,1,1024]{2,1,0:T(1,128)S(1)}) custom-call(s32[4]{0:T(128)S(1)} %add_multiply_fusion.base_ref, s32[512,1]{1,0:T(8,128)S(1)} %copy.50.rows_ref, s32[1,512]{1,0:T(1,128)S(1)} %add_add_fusion.1.top_ref, s32[1,512]{1,0:T(1,128)S(1)} %bitcast.110, bf16[384,512]{1,0:T(8,128)(2,1)S(1)} %get-tuple-element.249.q_ref, ...), custom_call_target="tpu_custom_call" | custom-call | flops 12099999744 | bytes 11000000 | tf_op jit(solution)/shard_map/attention_forward/pallas_call | solution.py:352
  171.5 8.0 %collective-permute-done.22 = bf16[384,512]{1,0:T(8,128)(2,1)S(1)} collective-permute-done((bf16[384,512]{1,0:T(8,128)(2,1)S(1)}, bf16[384,512]{1,0:T(8,128)(2,1)S(1)}, u32[]{:S(2)}, u32[]{:S(2)}) %collective-permute-start.22) | collective-permute-done | bytes 393248 | tf_op jit(solution)/shard_map/ppermute | solution.py:61
  182.3 8.5 %collective-permute-done.24 = bf16[768,256]{1,0:T(8,128)(2,1)S(1)} collective-permute-done((bf16[768,256]{1,0:T(8,128)(2,1)S(1)}, bf16[768,256]{1,0:T(8,128)(2,1)S(1)}, u32[]{:S(2)}, u32[]{:S(2)}) %collective-permute-start.24) | collective-permute-done | bytes 393248 | tf_op jit(solution)/shard_map/ppermute | solution.py:61
  194.2 8.0 %feed_forward.3 = (f32[512,1024]{1,0:T(8,128)S(1)}, f32[512,1024]{1,0:T(8,128)S(1)}, bf16[512,1024]{1,0:T(8,128)(2,1)S(1)}, f32[256,1536]{1,0:T(8,128)S(1)}, bf16[256,1536]{1,0:T(8,128)(2,1)S(1)}) custom-call(bf16[512,1536]{1,0:T(8,128)(2,1)S(1)} %pad_maximum_fusion.8.x_ref, bf16[2,1536,1024]{2,1,0:T(8,128)(2,1)S(1)} %bitcast.116, ...), custom_call_target="tpu_custom_call" | custom-call | flops 8800000000 | bytes 8000000 | tf_op jit(solution)/shard_map/feed_forward/pallas_call | solution.py:237
  205.0 8.2 %feed_forward_back.2 = (bf16[512,1024]{1,0:T(8,128)(2,1)S(1)}, bf16[512,1024]{1,0:T(8,128)(2,1)S(1)}, f32[256,1536]{1,0:T(8,128)S(1)}, bf16[256,1536]{1,0:T(8,128)(2,1)S(1)}) custom-call(bf16[512,1536]{1,0:T(8,128)(2,1)S(1)} %copy-done.10, bf16[2,1024,1536]{2,1,0:T(8,128)(2,1)S(1)} %copy-done.36, bf16[2,1536,1024]{2,1,0:T(8,128)(2,1)S(1)} %bitcast.116, ...), custom_call_target="tpu_custom_call" | custom-call | flops 9900000256 | bytes 9000000 | tf_op jit(solution)/shard_map/feed_forward_back/pallas_call | solution.py:274
  218.0 9.6 %collective-permute-done.27 = bf16[128,1536]{1,0:T(8,128)(2,1)S(1)} collective-permute-done((bf16[128,1536]{1,0:T(8,128)(2,1)S(1)}, bf16[128,1536]{1,0:T(8,128)(2,1)S(1)}, u32[]{:S(2)}, u32[]{:S(2)}) %collective-permute-start.27) | collective-permute-done | bytes 393248 | tf_op jit(solution)/shard_map/ppermute | solution.py:61
  234.4 9.5 %collective-permute-done.29 = bf16[128,1536]{1,0:T(8,128)(2,1)S(1)} collective-permute-done((bf16[128,1536]{1,0:T(8,128)(2,1)S(1)}, bf16[128,1536]{1,0:T(8,128)(2,1)S(1)}, u32[]{:S(2)}, u32[]{:S(2)}) %collective-permute-start.29) | collective-permute-done | bytes 393248 | tf_op jit(solution)/shard_map/ppermute | solution.py:61
  251.7 13.6 %attention_backward.2 = (bf16[384,512]{1,0:T(8,128)(2,1)S(1)}, f32[2,192,512]{2,1,0:T(8,128)S(1)}, bf16[2,192,512]{2,1,0:T(8,128)(2,1)}, bf16[2,192,512]{2,1,0:T(8,128)(2,1)S(1)}, bf16[2,192,512]{2,1,0:T(8,128)(2,1)S(1)}) custom-call(s32[4]{0:T(128)S(1)} %add_multiply_fusion.base_ref, s32[512,1]{1,0:T(8,128)S(1)} %copy.50.rows_ref, ...), custom_call_target="tpu_custom_call" | custom-call | flops 18150000640 | bytes 16500000 | tf_op jit(solution)/shard_map/attention_backward/pallas_call | solution.py:413
  265.3 6.1 collective-permute-done.32
  278.3 7.1 %collective-permute-done.35 = bf16[2,192,512]{2,1,0:T(8,128)(2,1)S(1)} collective-permute-done((bf16[2,192,512]{2,1,0:T(8,128)(2,1)S(1)}, bf16[2,192,512]{2,1,0:T(8,128)(2,1)S(1)}, u32[]{:S(2)}, u32[]{:S(2)}) %collective-permute-start.35) | collective-permute-done | bytes 393248 | tf_op jit(solution)/shard_map/ppermute | solution.py:121
  291.3 6.2 %collective-permute-done.42 = bf16[128,1536]{1,0:T(8,128)(2,1)S(1)} collective-permute-done((bf16[128,1536]{1,0:T(8,128)(2,1)S(1)}, bf16[128,1536]{1,0:T(8,128)(2,1)S(1)}, u32[]{:S(2)}, u32[]{:S(2)}) %collective-permute-start.42) | collective-permute-done | bytes 393248 | tf_op jit(solution)/shard_map/ppermute | solution.py:61
  327.5 7.6 %collective-permute-done.45 = bf16[128,1536]{1,0:T(8,128)(2,1)S(1)} collective-permute-done((bf16[128,1536]{1,0:T(8,128)(2,1)S(1)}, bf16[128,1536]{1,0:T(8,128)(2,1)S(1)}, u32[]{:S(2)}, u32[]{:S(2)}) %collective-permute-start.45) | collective-permute-done | bytes 393248 | tf_op jit(solution)/shard_map/ppermute | solution.py:61
  368.6 8.3 %feed_forward_back.3 = (bf16[512,1024]{1,0:T(8,128)(2,1)S(1)}, bf16[512,1024]{1,0:T(8,128)(2,1)S(1)}, f32[256,1536]{1,0:T(8,128)S(1)}, bf16[256,1536]{1,0:T(8,128)(2,1)S(1)}) custom-call(bf16[512,1536]{1,0:T(8,128)(2,1)S(1)} %pad_maximum_fusion.11.x_ref, bf16[2,1024,1536]{2,1,0:T(8,128)(2,1)S(1)} %copy-done.37, bf16[2,1536,1024]{2,1,0:T(8,128)(2,1)S(1)} %copy-done.35, ...), custom_call_target="tpu_custom_call" | custom-call | flops 9900000256 | bytes 9000000 | tf_op jit(solution)/shard_map/feed_forward_back/pallas_call | solution.py:274
  385.0 17.1 %collective-permute-done.54 = bf16[256,768]{1,0:T(8,128)(2,1)S(1)} collective-permute-done((bf16[256,768]{1,0:T(8,128)(2,1)S(1)}, bf16[256,768]{1,0:T(8,128)(2,1)S(1)}, u32[]{:S(2)}, u32[]{:S(2)}) %collective-permute-start.54) | collective-permute-done | bytes 393248 | tf_op jit(solution)/shard_map/ppermute | solution.py:61
  418.5 6.5 %collective-permute-done.57 = bf16[256,1024]{1,0:T(8,128)(2,1)} collective-permute-done((bf16[256,1024]{1,0:T(8,128)(2,1)}, bf16[256,1024]{1,0:T(8,128)(2,1)}, u32[]{:S(2)}, u32[]{:S(2)}) %collective-permute-start.57) | collective-permute-done | bytes 524320 | tf_op jit(solution)/shard_map/ppermute | solution.py:61
  438.7 13.7 %attention_backward.3 = (bf16[384,512]{1,0:T(8,128)(2,1)S(1)}, f32[2,192,512]{2,1,0:T(8,128)S(1)}, bf16[2,192,512]{2,1,0:T(8,128)(2,1)S(1)}, bf16[2,192,512]{2,1,0:T(8,128)(2,1)S(1)}, bf16[2,192,512]{2,1,0:T(8,128)(2,1)S(1)}) custom-call(s32[4]{0:T(128)S(1)} %add_multiply_fusion.base_ref, s32[512,1]{1,0:T(8,128)S(1)} %copy.50.rows_ref, ...), custom_call_target="tpu_custom_call" | custom-call | flops 18150000640 | bytes 16500000 | tf_op jit(solution)/shard_map/attention_backward/pallas_call | solution.py:413
  461.8 4.4 collective-permute-done.66
  477.8 8.7 %collective-permute-done.65.one_ref = bf16[2,192,512]{2,1,0:T(8,128)(2,1)S(1)} collective-permute-done((bf16[2,192,512]{2,1,0:T(8,128)(2,1)}, bf16[2,192,512]{2,1,0:T(8,128)(2,1)S(1)}, u32[]{:S(2)}, u32[]{:S(2)}) %collective-permute-start.65) | collective-permute-done | bytes 393248 | tf_op jit(solution)/shard_map/ppermute | solution.py:61
  486.6 6.3 %collective-permute-done.69 = bf16[768,256]{1,0:T(8,128)(2,1)S(1)} collective-permute-done((bf16[768,256]{1,0:T(8,128)(2,1)}, bf16[768,256]{1,0:T(8,128)(2,1)S(1)}, u32[]{:S(2)}, u32[]{:S(2)}) %collective-permute-start.69) | collective-permute-done | bytes 393248 | tf_op jit(solution)/shard_map/ppermute | solution.py:61
  510.5 7.9 %collective-permute-done.74 = bf16[256,768]{1,0:T(8,128)(2,1)S(1)} collective-permute-done((bf16[256,768]{1,0:T(8,128)(2,1)S(1)}, bf16[256,768]{1,0:T(8,128)(2,1)S(1)}, u32[]{:S(2)}, u32[]{:S(2)}) %collective-permute-start.74) | collective-permute-done | bytes 393248 | tf_op jit(solution)/shard_map/ppermute | solution.py:61
  518.4 7.6 %collective-permute-done.73 = bf16[256,768]{1,0:T(8,128)(2,1)S(1)} collective-permute-done((bf16[256,768]{1,0:T(8,128)(2,1)S(1)}, bf16[256,768]{1,0:T(8,128)(2,1)S(1)}, u32[]{:S(2)}, u32[]{:S(2)}) %collective-permute-start.73) | collective-permute-done | bytes 393248 | tf_op jit(solution)/shard_map/ppermute | solution.py:61
  544.5 7.2 %collective-permute-done.81 = f32[4,1536]{1,0:T(4,128)} collective-permute-done((f32[4,1536]{1,0:T(4,128)}, f32[4,1536]{1,0:T(4,128)}, u32[]{:S(2)}, u32[]{:S(2)}) %collective-permute-start.81) | collective-permute-done | bytes 24608 | tf_op jit(solution)/shard_map/ppermute | solution.py:61
  574.1 29.7 %reduce-scatter.14.cloned.1.call-done = bf16[192,2176]{1,0:T(8,128)(2,1)} async-done(((bf16[768,2176]{1,0:T(8,128)(2,1)}), bf16[192,2176]{1,0:T(8,128)(2,1)}) %reduce-scatter.14.cloned.1.call-update) | async-done | bytes 835600 | tf_op jit(solution)/shard_map/reduce_scatter | solution.py:130
  (600 shorter events, 304.3 us)
Async XLA Ops:
  7.2 349.4 %reduce-scatter.6.cloned.1.call-start = ((), (), s32[]{:S(2)}) async-start(), calls=%async_computation.5 | async-start | bytes 1966080 | tf_op jit(solution)/shard_map/reduce_scatter | solution.py:130
  21.5 17.5 %collective-permute-start.2 = (bf16[384,512]{1,0:T(8,128)(2,1)}, bf16[384,512]{1,0:T(8,128)(2,1)}, u32[]{:S(2)}, u32[]{:S(2)}) collective-permute-start(bf16[384,512]{1,0:T(8,128)(2,1)} %get-tuple-element.222.refs_0_.refs_1_), channel_id=1, source_target_pairs={{8,20},{12,16},{24,4},{28,0},{9,21},{13,17},{25,5},{29,1},{10,22},... | collective-permute-start | bytes 1179656 | tf_op jit(solution)/shard_map/ppermute | solution.py:113
  22.8 21.7 %collective-permute-start = (bf16[384,512]{1,0:T(8,128)(2,1)}, bf16[384,512]{1,0:T(8,128)(2,1)}, u32[]{:S(2)}, u32[]{:S(2)}) collective-permute-start(bf16[384,512]{1,0:T(8,128)(2,1)} %get-tuple-element.222.refs_0_.refs_1_), channel_id=1, source_target_pairs={{0,4},{4,0},{8,12},{12,8},{16,20},{20,16},{24,28},{28,24},{1,5},{5... | collective-permute-start | bytes 1179656 | tf_op jit(solution)/shard_map/ppermute | solution.py:61
  25.8 21.4 %collective-permute-start.1 = (bf16[384,512]{1,0:T(8,128)(2,1)}, bf16[384,512]{1,0:T(8,128)(2,1)}, u32[]{:S(2)}, u32[]{:S(2)}) collective-permute-start(bf16[384,512]{1,0:T(8,128)(2,1)} %get-tuple-element.222.refs_0_.refs_1_), channel_id=1, source_target_pairs={{8,16},{12,20},{24,0},{28,4},{9,17},{13,21},{25,1},{29,5},{10,18},... | collective-permute-start | bytes 1179656 | tf_op jit(solution)/shard_map/ppermute | solution.py:114
  134.5 20.4 %collective-permute-start.16 = (bf16[384,512]{1,0:T(8,128)(2,1)S(1)}, bf16[384,512]{1,0:T(8,128)(2,1)S(1)}, u32[]{:S(2)}, u32[]{:S(2)}) collective-permute-start(bf16[384,512]{1,0:T(8,128)(2,1)S(1)} %get-tuple-element.250.refs_0_.refs_1_), channel_id=1, source_target_pairs={{0,4},{4,0},{8,12},{12,8},{16,20},{20,16},{24,28},{28,24},{1,5},{5... | collective-permute-start | bytes 1179656 | tf_op jit(solution)/shard_map/ppermute | solution.py:61
  135.5 21.4 %collective-permute-start.17 = (bf16[384,512]{1,0:T(8,128)(2,1)S(1)}, bf16[384,512]{1,0:T(8,128)(2,1)S(1)}, u32[]{:S(2)}, u32[]{:S(2)}) collective-permute-start(bf16[384,512]{1,0:T(8,128)(2,1)S(1)} %get-tuple-element.250.refs_0_.refs_1_), channel_id=1, source_target_pairs={{8,16},{12,20},{24,0},{28,4},{9,17},{13,21},{25,1},{29,5},{10,18},... | collective-permute-start | bytes 1179656 | tf_op jit(solution)/shard_map/ppermute | solution.py:114
  248.6 25.7 %collective-permute-start.40 = (bf16[256,1536]{1,0:T(8,128)(2,1)S(1)}, bf16[256,1536]{1,0:T(8,128)(2,1)S(1)}, u32[]{:S(2)}, u32[]{:S(2)}) collective-permute-start(bf16[256,1536]{1,0:T(8,128)(2,1)S(1)} %get-tuple-element.308), channel_id=1, source_target_pairs={{0,1},{1,0},{2,3},{3,2},{4,5},{5,4},{6,7},{7,6},{8,9},{9,8},{10,11... | collective-permute-start | bytes 2359304 | tf_op jit(solution)/shard_map/ppermute | solution.py:61
  248.9 22.5 %collective-permute-start.33 = (bf16[256,1024]{1,0:T(8,128)(2,1)S(1)}, bf16[256,1024]{1,0:T(8,128)(2,1)S(1)}, u32[]{:S(2)}, u32[]{:S(2)}) collective-permute-start(bf16[256,1024]{1,0:T(8,128)(2,1)S(1)} %get-tuple-element.283), channel_id=1, source_target_pairs={{0,4},{4,0},{8,12},{12,8},{16,20},{20,16},{24,28},{28,24},{1,5},{5... | collective-permute-start | bytes 1572872 | tf_op jit(solution)/shard_map/ppermute | solution.py:61
  249.9 21.6 %collective-permute-start.32 = (bf16[768,256]{1,0:T(8,128)(2,1)S(1)}, bf16[768,256]{1,0:T(8,128)(2,1)S(1)}, u32[]{:S(2)}, u32[]{:S(2)}) collective-permute-start(bf16[768,256]{1,0:T(8,128)(2,1)S(1)} %get-tuple-element.281), channel_id=1, source_target_pairs={{0,4},{4,0},{8,12},{12,8},{16,20},{20,16},{24,28},{28,24},{1,5},{5... | collective-permute-start | bytes 1179656 | tf_op jit(solution)/shard_map/ppermute | solution.py:61
  277.2 23.5 %collective-permute-start.34 = (bf16[2,192,512]{2,1,0:T(8,128)(2,1)}, bf16[2,192,512]{2,1,0:T(8,128)(2,1)}, u32[]{:S(2)}, u32[]{:S(2)}) collective-permute-start(bf16[2,192,512]{2,1,0:T(8,128)(2,1)} %get-tuple-element.286), channel_id=1, source_target_pairs={{0,4},{4,0},{8,12},{12,8},{16,20},{20,16},{24,28},{28,24},{1,5},{5... | collective-permute-start | bytes 1179656 | tf_op jit(solution)/shard_map/ppermute | solution.py:61
  298.6 17.7 %collective-permute-start.43 = (bf16[256,1536]{1,0:T(8,128)(2,1)}, bf16[256,1536]{1,0:T(8,128)(2,1)}, u32[]{:S(2)}, u32[]{:S(2)}) collective-permute-start(bf16[256,1536]{1,0:T(8,128)(2,1)} %pad_maximum_fusion.27), channel_id=1, source_target_pairs={{0,1},{1,0},{2,3},{3,2},{4,5},{5,4},{6,7},{7,6},{8,9},{9,8},{10,11... | collective-permute-start | bytes 2359304 | tf_op jit(solution)/shard_map/ppermute | solution.py:61
  320.2 26.1 %collective-permute-start.49 = (bf16[768,256]{1,0:T(8,128)(2,1)}, bf16[768,256]{1,0:T(8,128)(2,1)}, u32[]{:S(2)}, u32[]{:S(2)}) collective-permute-start(bf16[768,256]{1,0:T(8,128)(2,1)} %collective-permute-done.3), channel_id=1, source_target_pairs={{0,1},{1,0},{2,3},{3,2},{4,5},{5,4},{6,7},{7,6},{8,9},{9,8},{10,11... | collective-permute-start | bytes 1179656 | tf_op jit(solution)/shard_map/ppermute | solution.py:61
  320.7 95.3 %reduce-scatter.8.cloned.1.call-start = ((), (), s32[]{:S(2)}) async-start(), calls=%async_computation.6 | async-start | bytes 3932160 | tf_op jit(solution)/shard_map/reduce_scatter | solution.py:130
  358.6 113.5 %reduce-scatter.10.cloned.1.call-start = ((), (), s32[]{:S(2)}) async-start(), calls=%async_computation.7 | async-start | bytes 2211840 | tf_op jit(solution)/shard_map/reduce_scatter | solution.py:130
  377.4 32.4 %collective-permute-start.60 = (bf16[768,256]{1,0:T(8,128)(2,1)S(1)}, bf16[768,256]{1,0:T(8,128)(2,1)S(1)}, u32[]{:S(2)}, u32[]{:S(2)}) collective-permute-start(bf16[768,256]{1,0:T(8,128)(2,1)S(1)} %copy-done.110), channel_id=1, source_target_pairs={{0,1},{1,0},{2,3},{3,2},{4,5},{5,4},{6,7},{7,6},{8,9},{9,8},{10,11... | collective-permute-start | bytes 1179656 | tf_op jit(solution)/shard_map/ppermute | solution.py:61
  377.5 30.7 %collective-permute-start.59 = (bf16[768,256]{1,0:T(8,128)(2,1)}, bf16[768,256]{1,0:T(8,128)(2,1)S(1)}, u32[]{:S(2)}, u32[]{:S(2)}) collective-permute-start(bf16[768,256]{1,0:T(8,128)(2,1)} %collective-permute-done.48), channel_id=1, source_target_pairs={{0,1},{1,0},{2,3},{3,2},{4,5},{5,4},{6,7},{7,6},{8,9},{9,8},{10,11... | collective-permute-start | bytes 1179656 | tf_op jit(solution)/shard_map/ppermute | solution.py:61
  379.4 22.8 %collective-permute-start.53 = (bf16[128,1536]{1,0:T(8,128)(2,1)S(1)}, bf16[128,1536]{1,0:T(8,128)(2,1)S(1)}, u32[]{:S(2)}, u32[]{:S(2)}) collective-permute-start(bf16[128,1536]{1,0:T(8,128)(2,1)S(1)} %add_convert_fusion.10), channel_id=1, source_target_pairs={{0,2},{1,3},{2,0},{3,1},{4,6},{5,7},{6,4},{7,5},{8,10},{9,11},{10,... | collective-permute-start | bytes 1179656 | tf_op jit(solution)/shard_map/ppermute | solution.py:61
  379.7 22.4 %collective-permute-start.55 = (bf16[256,1024]{1,0:T(8,128)(2,1)S(1)}, bf16[256,1024]{1,0:T(8,128)(2,1)S(1)}, u32[]{:S(2)}, u32[]{:S(2)}) collective-permute-start(bf16[256,1024]{1,0:T(8,128)(2,1)S(1)} %get-tuple-element.336), channel_id=1, source_target_pairs={{0,4},{4,0},{8,12},{12,8},{16,20},{20,16},{24,28},{28,24},{1,5},{5... | collective-permute-start | bytes 1572872 | tf_op jit(solution)/shard_map/ppermute | solution.py:61
  381.0 21.2 %collective-permute-start.54 = (bf16[256,768]{1,0:T(8,128)(2,1)S(1)}, bf16[256,768]{1,0:T(8,128)(2,1)S(1)}, u32[]{:S(2)}, u32[]{:S(2)}) collective-permute-start(bf16[256,768]{1,0:T(8,128)(2,1)S(1)} %get-tuple-element.334), channel_id=1, source_target_pairs={{0,4},{4,0},{8,12},{12,8},{16,20},{20,16},{24,28},{28,24},{1,5},{5... | collective-permute-start | bytes 1179656 | tf_op jit(solution)/shard_map/ppermute | solution.py:61
  406.9 18.1 %collective-permute-start.57 = (bf16[256,1024]{1,0:T(8,128)(2,1)}, bf16[256,1024]{1,0:T(8,128)(2,1)}, u32[]{:S(2)}, u32[]{:S(2)}) collective-permute-start(bf16[256,1024]{1,0:T(8,128)(2,1)} %get-tuple-element.342), channel_id=1, source_target_pairs={{0,4},{4,0},{8,12},{12,8},{16,20},{20,16},{24,28},{28,24},{1,5},{5... | collective-permute-start | bytes 1572872 | tf_op jit(solution)/shard_map/ppermute | solution.py:61
  430.3 106.9 %reduce-scatter.12.cloned.1.call-start = ((), (), s32[]{:S(2)}) async-start(), calls=%async_computation.8 | async-start | bytes 3932160 | tf_op jit(solution)/shard_map/reduce_scatter | solution.py:130
  433.7 18.7 %collective-permute-start.64 = (bf16[128,1024]{1,0:T(8,128)(2,1)S(1)}, bf16[128,1024]{1,0:T(8,128)(2,1)S(1)}, u32[]{:S(2)}, u32[]{:S(2)}) collective-permute-start(bf16[128,1024]{1,0:T(8,128)(2,1)S(1)} %copy-done.113), channel_id=1, source_target_pairs={{0,4},{4,0},{8,12},{12,8},{16,20},{20,16},{24,28},{28,24},{1,5},{5... | collective-permute-start | bytes 786440 | tf_op jit(solution)/shard_map/ppermute | solution.py:61
  434.3 18.1 %collective-permute-start.63 = (bf16[128,1024]{1,0:T(8,128)(2,1)S(1)}, bf16[128,1024]{1,0:T(8,128)(2,1)S(1)}, u32[]{:S(2)}, u32[]{:S(2)}) collective-permute-start(bf16[128,1024]{1,0:T(8,128)(2,1)S(1)} %copy-done.112), channel_id=1, source_target_pairs={{0,4},{4,0},{8,12},{12,8},{16,20},{20,16},{24,28},{28,24},{1,5},{5... | collective-permute-start | bytes 786440 | tf_op jit(solution)/shard_map/ppermute | solution.py:61
  435.8 17.8 %collective-permute-start.62 = (bf16[128,1024]{1,0:T(8,128)(2,1)S(1)}, bf16[128,1024]{1,0:T(8,128)(2,1)S(1)}, u32[]{:S(2)}, u32[]{:S(2)}) collective-permute-start(bf16[128,1024]{1,0:T(8,128)(2,1)S(1)} %copy-done.111), channel_id=1, source_target_pairs={{0,4},{4,0},{8,12},{12,8},{16,20},{20,16},{24,28},{28,24},{1,5},{5... | collective-permute-start | bytes 786440 | tf_op jit(solution)/shard_map/ppermute | solution.py:61
  474.2 129.7 %reduce-scatter.14.cloned.1.call-start = ((), (), s32[]{:S(2)}) async-start(), calls=%async_computation.9 | async-start | bytes 4177920 | tf_op jit(solution)/shard_map/reduce_scatter | solution.py:130
  474.8 18.1 %collective-permute-start.69 = (bf16[768,256]{1,0:T(8,128)(2,1)}, bf16[768,256]{1,0:T(8,128)(2,1)S(1)}, u32[]{:S(2)}, u32[]{:S(2)}) collective-permute-start(bf16[768,256]{1,0:T(8,128)(2,1)} %copy-done.50), channel_id=1, source_target_pairs={{0,4},{4,0},{8,12},{12,8},{16,20},{20,16},{24,28},{28,24},{1,5},{5... | collective-permute-start | bytes 1179656 | tf_op jit(solution)/shard_map/ppermute | solution.py:61
  476.3 18.7 %collective-permute-start.68 = (bf16[2,192,512]{2,1,0:T(8,128)(2,1)}, bf16[2,192,512]{2,1,0:T(8,128)(2,1)S(1)}, u32[]{:S(2)}, u32[]{:S(2)}) collective-permute-start(bf16[2,192,512]{2,1,0:T(8,128)(2,1)} %add_convert_fusion.9), channel_id=1, source_target_pairs={{0,24},{4,28},{16,8},{20,12},{1,25},{5,29},{17,9},{21,13},{2,26},{... | collective-permute-start | bytes 1179656 | tf_op jit(solution)/shard_map/ppermute | solution.py:124
  504.0 25.9 %collective-permute-start.78 = (bf16[768,256]{1,0:T(8,128)(2,1)S(1)}, bf16[768,256]{1,0:T(8,128)(2,1)S(1)}, u32[]{:S(2)}, u32[]{:S(2)}) collective-permute-start(bf16[768,256]{1,0:T(8,128)(2,1)S(1)} %copy-done.108), channel_id=1, source_target_pairs={{0,1},{1,0},{2,3},{3,2},{4,5},{5,4},{6,7},{7,6},{8,9},{9,8},{10,11... | collective-permute-start | bytes 1179656 | tf_op jit(solution)/shard_map/ppermute | solution.py:61
  504.8 23.3 %collective-permute-start.77 = (bf16[768,256]{1,0:T(8,128)(2,1)S(1)}, bf16[768,256]{1,0:T(8,128)(2,1)S(1)}, u32[]{:S(2)}, u32[]{:S(2)}) collective-permute-start(bf16[768,256]{1,0:T(8,128)(2,1)S(1)} %collective-permute-done.70), channel_id=1, source_target_pairs={{0,1},{1,0},{2,3},{3,2},{4,5},{5,4},{6,7},{7,6},{8,9},{9,8},{10,11... | collective-permute-start | bytes 1179656 | tf_op jit(solution)/shard_map/ppermute | solution.py:61
  506.3 19.7 %collective-permute-start.72 = (bf16[128,1536]{1,0:T(8,128)(2,1)S(1)}, bf16[128,1536]{1,0:T(8,128)(2,1)S(1)}, u32[]{:S(2)}, u32[]{:S(2)}) collective-permute-start(bf16[128,1536]{1,0:T(8,128)(2,1)S(1)} %add_convert_fusion.8), channel_id=1, source_target_pairs={{0,2},{1,3},{2,0},{3,1},{4,6},{5,7},{6,4},{7,5},{8,10},{9,11},{10,... | collective-permute-start | bytes 1179656 | tf_op jit(solution)/shard_map/ppermute | solution.py:61
  507.4 18.7 %collective-permute-start.73 = (bf16[256,768]{1,0:T(8,128)(2,1)S(1)}, bf16[256,768]{1,0:T(8,128)(2,1)S(1)}, u32[]{:S(2)}, u32[]{:S(2)}) collective-permute-start(bf16[256,768]{1,0:T(8,128)(2,1)S(1)} %get-tuple-element.397), channel_id=1, source_target_pairs={{0,4},{4,0},{8,12},{12,8},{16,20},{20,16},{24,28},{28,24},{1,5},{5... | collective-permute-start | bytes 1179656 | tf_op jit(solution)/shard_map/ppermute | solution.py:61
  539.9 18.0 %collective-permute-start.76 = (bf16[128,1536]{1,0:T(8,128)(2,1)S(1)}, bf16[128,1536]{1,0:T(8,128)(2,1)}, u32[]{:S(2)}, u32[]{:S(2)}) collective-permute-start(bf16[128,1536]{1,0:T(8,128)(2,1)S(1)} %copy-done.80), channel_id=1, source_target_pairs={{0,2},{1,3},{2,0},{3,1},{4,6},{5,7},{6,4},{7,5},{8,10},{9,11},{10,... | collective-permute-start | bytes 1179656 | tf_op jit(solution)/shard_map/ppermute | solution.py:61
  (192 other events, 1822.0 us)
Sparse Core Ops, SparseCore 0:
  320.8 32.1 reduce-scatter.5
  358.7 57.2 reduce-scatter.7
  430.4 35.0 reduce-scatter.9
  474.3 62.8 reduce-scatter.11
  539.4 64.3 reduce-scatter.13
